TPU v7x, 256 devices: a whole 4x4x8 slice. The times are simulated.
256 devices in a mesh: seq: 8 (over z_hi, x), exp: 32 (over z_lo, y, core).
Axes of the slice: x: 4, y: 4, z: 8 (z_hi: 2, z_lo: 4; z = z_hi * 4 + z_lo), core: 2. Of those that a mesh axis runs over, the one named last changes fastest.
Arguments:
- tokens: bfloat16 [8192, 1664], P('seq'), may hold values from -6 to 6
- out_grad: bfloat16 [8192, 1664], P('seq'), may hold values from -6 to 6
- slot_params: bfloat16 [1024, 1664], P('exp'), may hold values from -6 to 6
- first_mixing: float32 [64, 4, 4, 4], P('exp'), may hold values from -3 to 3
- first_blocks: bfloat16 [64, 4, 416, 2048], P('exp', None, None, 'seq'), may hold values from -0.15625 to 0.15625
- second_mixing: float32 [64, 4, 4, 4], P('exp'), may hold values from -3 to 3
- second_blocks: bfloat16 [64, 4, 2048, 416], P('exp', None, 'seq'), may hold values from -0.0625 to 0.0625
Outputs:
- grad_tokens: float32 [8192, 1664], P(('seq', 'exp'))
- grad_slots: float32 [1024, 1664], P('exp')
- grad_first_mixing: float32 [64, 4, 4, 4], P('exp')
- grad_first_blocks: bfloat16 [64, 4, 416, 2048], P('exp', None, None, 'seq')
- grad_second_mixing: float32 [64, 4, 4, 4], P('exp')
- grad_second_blocks: bfloat16 [64, 4, 2048, 416], P('exp', None, 'seq')
All inputs are finite; a program needn't handle non-finite values.
Results may differ from a plain program's by a relative error of at most 0.04.
Values may be sent and summed in bfloat16 or wider, within the bound.
No kernel may reach another device: no remote copies, remote signals or barrier semaphores. Data moves between devices by JAX's collectives and lax.ppermute only.
A program may use at most 128 MiB of HBM per device.

v0:
```python
import jax
import jax.numpy as jnp
from jax import lax
from jax.sharding import PartitionSpec as P

logit_gain = 64.0
norm_eps = 1e-06
gelu_coef = 0.7978845608028654
cubic_coef = 0.044715


def gelu_pair(preact):
    inner_arg = gelu_coef * (preact + cubic_coef * preact * preact * preact)
    tangent = jnp.tanh(inner_arg)
    output = 0.5 * preact * (1.0 + tangent)
    slopes = 0.5 * (1.0 + tangent) + 0.5 * preact * (1.0 - tangent * tangent) * gelu_coef * (
        1.0 + 3.0 * cubic_coef * preact * preact
    )
    return (output, slopes)


def mix_blocks(blocks, mixing):
    return jnp.einsum("sak,iab->sbik", blocks.astype(jnp.float32), mixing)


def expert_forward(slot_in, first_mixing, first_blocks, second_mixing, second_blocks):
    slots_here, model_width = slot_in.shape
    factors = first_mixing.shape[0]
    inner_width = model_width // factors
    hidden_block = first_blocks.shape[2]
    first_flat = (
        mix_blocks(slot_in.reshape(slots_here, factors, inner_width), first_mixing)
        .astype(jnp.bfloat16)
        .reshape(slots_here * factors, factors * inner_width)
    )
    preact = jnp.dot(
        first_flat,
        first_blocks.reshape(factors * inner_width, hidden_block),
        preferred_element_type=jnp.float32,
    ).reshape(slots_here, factors, hidden_block)
    activated, slopes = gelu_pair(preact)
    hidden = activated.astype(jnp.bfloat16)
    second_flat = (
        mix_blocks(hidden, second_mixing)
        .astype(jnp.bfloat16)
        .reshape(slots_here * factors, factors * hidden_block)
    )
    slot_out = jnp.dot(
        second_flat,
        second_blocks.reshape(factors * hidden_block, inner_width),
        preferred_element_type=jnp.float32,
    ).reshape(slots_here, model_width)
    return (slot_out, first_flat, hidden, slopes, second_flat)


def expert_backward(
    slot_in,
    grad_out,
    first_flat,
    hidden,
    slopes,
    second_flat,
    first_mixing,
    first_blocks,
    second_mixing,
    second_blocks,
):
    slots_here, model_width = slot_in.shape
    factors = first_mixing.shape[0]
    inner_width = model_width // factors
    hidden_block = first_blocks.shape[2]
    first_matrix = first_blocks.reshape(factors * inner_width, hidden_block)
    second_matrix = second_blocks.reshape(factors * hidden_block, inner_width)
    grad_rows = grad_out.reshape(slots_here * factors, inner_width)
    grad_second_in = jnp.dot(
        grad_rows, second_matrix.T, preferred_element_type=jnp.float32
    ).reshape(slots_here, factors, factors, hidden_block)
    grad_second_blocks = (
        jnp.dot(second_flat.T, grad_rows, preferred_element_type=jnp.float32)
        .astype(jnp.bfloat16)
        .reshape(factors, hidden_block, inner_width)
    )
    grad_second_mixing = jnp.einsum("sak,sbik->iab", hidden.astype(jnp.float32), grad_second_in)
    grad_hidden = jnp.einsum("iab,sbik->sak", second_mixing, grad_second_in)
    grad_preact = (
        (grad_hidden * slopes).astype(jnp.bfloat16).reshape(slots_here * factors, hidden_block)
    )
    grad_first_in = jnp.dot(
        grad_preact, first_matrix.T, preferred_element_type=jnp.float32
    ).reshape(slots_here, factors, factors, inner_width)
    grad_first_blocks = (
        jnp.dot(first_flat.T, grad_preact, preferred_element_type=jnp.float32)
        .astype(jnp.bfloat16)
        .reshape(factors, inner_width, hidden_block)
    )
    slot_split = slot_in.reshape(slots_here, factors, inner_width).astype(jnp.float32)
    grad_first_mixing = jnp.einsum("sad,sbid->iab", slot_split, grad_first_in)
    grad_slot = jnp.einsum("iab,sbid->sad", first_mixing, grad_first_in).reshape(
        slots_here, model_width
    )
    return (grad_slot, grad_first_mixing, grad_first_blocks, grad_second_mixing, grad_second_blocks)


def token_total(partial_sums):
    return lax.psum(partial_sums, "exp")


def slot_total(first_part, second_part):
    return lax.psum((first_part, second_part), "seq")


def unit_grad(unit_rows, unit_grad_rows, norms):
    return (
        unit_grad_rows - unit_rows * jnp.sum(unit_rows * unit_grad_rows, axis=1, keepdims=True)
    ) / norms


def local(tokens, out_grad, slot_params, first_mixing, first_blocks, second_mixing, second_blocks):
    token_values = tokens.astype(jnp.float32)
    token_norm = jnp.sqrt(jnp.sum(token_values * token_values, axis=1, keepdims=True) + norm_eps)
    token_unit = token_values / token_norm
    token_unit_b = token_unit.astype(jnp.bfloat16)
    slot_values = slot_params.astype(jnp.float32)
    slot_norm = jnp.sqrt(jnp.sum(slot_values * slot_values, axis=1, keepdims=True) + norm_eps)
    slot_unit = slot_values / slot_norm
    slot_unit_b = slot_unit.astype(jnp.bfloat16)
    logits = logit_gain * jnp.einsum(
        "sd,td->st", slot_unit_b, token_unit_b, preferred_element_type=jnp.float32
    )
    weights = jnp.exp(logits)
    input_part = jnp.dot(weights.astype(jnp.bfloat16), tokens, preferred_element_type=jnp.float32)
    combine_total = token_total(jnp.sum(weights, axis=0))
    input_sum, dispatch_total = slot_total(input_part, jnp.sum(weights, axis=1))
    slot_inputs = input_sum / dispatch_total[:, None]
    slot_inputs_b = slot_inputs.astype(jnp.bfloat16)
    dispatch = weights / dispatch_total[:, None]
    combine = weights / combine_total[None, :]
    grad_out_part = jnp.dot(
        combine.astype(jnp.bfloat16), out_grad, preferred_element_type=jnp.float32
    )
    experts_here = first_mixing.shape[0]
    model_width = tokens.shape[1]
    slots_each = slot_inputs_b.shape[0] // experts_here
    grouped = slot_inputs_b.reshape(experts_here, slots_each, model_width)
    slot_out_part, first_flat, hidden, slopes, second_flat = jax.vmap(expert_forward)(
        grouped, first_mixing, first_blocks, second_mixing, second_blocks
    )
    slot_out_sum, slot_grad_sum = slot_total(
        slot_out_part.reshape(experts_here * slots_each, model_width), grad_out_part
    )
    slot_out_b = slot_out_sum.astype(jnp.bfloat16)
    slot_grad_b = slot_grad_sum.astype(jnp.bfloat16)
    combine_grad = jnp.einsum("sd,td->st", slot_out_b, out_grad, preferred_element_type=jnp.float32)
    combine_dot = token_total(jnp.sum(combine * combine_grad, axis=0))
    expert_results = jax.vmap(expert_backward)(
        grouped,
        slot_grad_b.reshape(experts_here, slots_each, model_width),
        first_flat,
        hidden,
        slopes,
        second_flat,
        first_mixing,
        first_blocks,
        second_mixing,
        second_blocks,
    )
    input_grad_part, first_mix_part, first_blocks_grad, second_mix_part, second_blocks_grad = (
        expert_results
    )
    input_grad, mixing_grads = slot_total(
        input_grad_part.reshape(experts_here * slots_each, model_width),
        jnp.stack([first_mix_part, second_mix_part]),
    )
    input_grad_b = input_grad.astype(jnp.bfloat16)
    dispatch_dot = jnp.sum(slot_inputs * input_grad, axis=1)
    dispatch_grad = jnp.einsum(
        "sd,td->st", input_grad_b, tokens, preferred_element_type=jnp.float32
    )
    logit_grad = combine * (combine_grad - combine_dot[None, :]) + dispatch * (
        dispatch_grad - dispatch_dot[:, None]
    )
    logit_grad_b = (logit_gain * logit_grad).astype(jnp.bfloat16)
    slot_unit_grad = lax.psum(
        jnp.dot(logit_grad_b, token_unit_b, preferred_element_type=jnp.float32), "seq"
    )
    grad_slots = unit_grad(slot_unit, slot_unit_grad, slot_norm)
    row_count = tokens.shape[0] // lax.axis_size("exp")
    grad_all, out_all, unit_all = (
        lax.all_gather(input_grad_b, "exp", axis=0, tiled=True),
        lax.all_gather(slot_out_b, "exp", axis=0, tiled=True),
        lax.all_gather(slot_unit_b, "exp", axis=0, tiled=True),
    )
    dispatch_all, dot_all = (
        lax.all_gather(dispatch_total, "exp", axis=0, tiled=True),
        lax.all_gather(dispatch_dot, "exp", axis=0, tiled=True),
    )
    first_row = lax.axis_index("exp") * row_count
    own_tokens = lax.dynamic_slice_in_dim(tokens, first_row, row_count, 0)
    own_grad = lax.dynamic_slice_in_dim(out_grad, first_row, row_count, 0)
    own_unit = lax.dynamic_slice_in_dim(token_unit, first_row, row_count, 0)
    own_unit_b = lax.dynamic_slice_in_dim(token_unit_b, first_row, row_count, 0)
    own_norm = lax.dynamic_slice_in_dim(token_norm, first_row, row_count, 0)
    own_total = lax.dynamic_slice_in_dim(combine_total, first_row, row_count, 0)
    own_dot = lax.dynamic_slice_in_dim(combine_dot, first_row, row_count, 0)
    own_weights = jnp.exp(
        logit_gain * jnp.dot(own_unit_b, unit_all.T, preferred_element_type=jnp.float32)
    )
    own_dispatch = own_weights / dispatch_all[None, :]
    own_combine = own_weights / own_total[:, None]
    own_combine_grad = jnp.dot(own_grad, out_all.T, preferred_element_type=jnp.float32)
    own_dispatch_grad = jnp.dot(own_tokens, grad_all.T, preferred_element_type=jnp.float32)
    own_logit = own_combine * (own_combine_grad - own_dot[:, None]) + own_dispatch * (
        own_dispatch_grad - dot_all[None, :]
    )
    own_logit_b = (logit_gain * own_logit).astype(jnp.bfloat16)
    direct = jnp.dot(
        own_dispatch.astype(jnp.bfloat16), grad_all, preferred_element_type=jnp.float32
    )
    through = jnp.dot(own_logit_b, unit_all, preferred_element_type=jnp.float32)
    grad_tokens = direct + unit_grad(own_unit, through, own_norm)
    return (
        grad_tokens,
        grad_slots,
        mixing_grads[0],
        first_blocks_grad,
        mixing_grads[1],
        second_blocks_grad,
    )


def solution(mesh):
    placed = (
        P("seq", None),
        P("seq", None),
        P("exp", None),
        P("exp", None, None, None),
        P("exp", None, None, "seq"),
        P("exp", None, None, None),
        P("exp", None, "seq", None),
    )
    return jax.shard_map(
        local,
        mesh=mesh,
        in_specs=placed,
        out_specs=(
            P(("seq", "exp"), None),
            P("exp", None),
            P("exp", None, None, None),
            P("exp", None, None, "seq"),
            P("exp", None, None, None),
            P("exp", None, "seq", None),
        ),
        check_vma=False,
    )
```

profile of v0, /device:TPU:1, one launch (start us, length us, event | category | flops | bytes accessed | tf_op | source)
XLA Modules:
  0.0 651.7 jit_solution(12688127571988477652)
XLA Ops:
  8.1 2.9 fusion
  11.2 5.0 convert_divide_fusion
  17.6 3.9 fusion.57
  23.0 71.5 %psum.64 = f32[1024]{0:T(1024)S(1)} all-reduce(f32[1024]{0:T(1024)S(1)} %get-tuple-element.19), channel_id=1, replica_groups=mesh['seq'=8,'exp'=32] {'exp'}, use_global_device_ids=true, to_apply=%region_5.0 | all-reduce | flops 1024 | bytes 8192 | tf_op jit(solution)/shard_map/psum | solution.py:105
  96.5 50.3 %all-reduce.16 = (bf16[32,1664]{1,0:T(8,128)(2,1)}, f32[32]{0:T(128)}) all-reduce(f32[32,1664]{1,0:T(8,128)} %fusion.41, f32[32]{0:T(128)} %get-tuple-element.18), channel_id=1, replica_groups=mesh['seq'=8,'exp'=32] {'seq'}, use_global_device_ids=true, to_apply=%region_6.0 | all-reduce | flops 53280 | bytes 319744 | tf_op jit(solution)/shard_map/psum | solution.py:109
  152.5 1.8 reshape.84
  166.3 2.3 reshape.85
  168.6 2.7 fusion.67
  172.8 2.0 fusion.2
  174.8 1.9 convolution_bitcast_fusion.3
  176.7 2.0 fusion.15
  180.2 2.9 fusion.68
  183.0 2.5 reshape.89
  185.6 2.2 convolution_bitcast_fusion.2
  191.8 1.8 reshape.91
  193.6 2.9 fusion.69
  198.3 2.2 convolution_bitcast_fusion
  200.4 1.9 reshape.90
  203.7 46.9 %all-reduce.17 = (bf16[32,1664]{1,0:T(8,128)(2,1)}, f32[2,2,4,4,4]{4,3,2,1,0:T(4,128)}) all-reduce(f32[32,1664]{1,0:T(8,128)} %reshape.92, f32[2,2,4,4,4]{4,3,2,1,0:T(4,128)} %pad_maximum_fusion), channel_id=1, replica_groups=mesh['seq'=8,'exp'=32] {'seq'}, use_global_device_ids=true, to_apply=%region_9.0 | all-reduce | flops 53504 | bytes 321536 | tf_op jit(solution)/shard_map/psum | solution.py:109
  250.7 3.2 multiply_reduce_fusion.3
  253.9 51.0 %all-reduce.13.cloned.1.call-done = f32[32,1664]{1,0:T(8,128)} async-done(((f32[32,1664]{1,0:T(8,128)}), f32[32,1664]{1,0:T(8,128)}) %all-reduce.13.cloned.1.call-update) | async-done | bytes 213008 | tf_op jit(solution)/shard_map/psum | solution.py:109
  304.9 1.9 multiply_reduce_fusion.2
  307.3 132.5 %all-reduce.2 = (f32[1024]{0:T(1024)}, f32[1024]{0:T(1024)}, f32[1024]{0:T(1024)S(1)}) all-reduce(f32[1024]{0:T(1024)} %get-tuple-element.34, f32[1024]{0:T(1024)S(1)} %dynamic-update-slice.1, f32[1024]{0:T(1024)S(1)} %copy-done.14), channel_id=1, replica_groups=mesh['seq'=8,'exp'=32] {'exp'}, use_global_device_ids=true, to_apply=%region_11.0 | all-reduce | flops 3072 | bytes 24576 | tf_op jit(solution)/shard_map/psum | solution.py:105
  439.8 5.5 fusion.16
  451.6 1.8 convolution_convert_fusion
  454.7 89.4 %all-reduce.15.cloned.1.call-done = f32[32,1664]{1,0:T(8,128)} async-done(((f32[32,1664]{1,0:T(8,128)}), f32[32,1664]{1,0:T(8,128)}) %all-reduce.15.cloned.1.call-update) | async-done | bytes 213008 | tf_op jit(solution)/shard_map/psum | solution.py:183
  547.0 3.2 fusion.12
  550.2 22.4 %all-gather.8.cloned.1.call-done = bf16[1024,1664]{1,0:T(8,128)(2,1)} async-done(((bf16[32,1664]{1,0:T(8,128)(2,1)}), bf16[1024,1664]{1,0:T(8,128)(2,1)}) %all-gather.8.cloned.1.call-update) | async-done | bytes 3407888 | tf_op jit(solution)/shard_map/all_gather | solution.py:190
  572.6 3.7 fusion.10
  576.3 59.0 %all-gather.6.cloned.1.call-done = bf16[1024,1664]{1,0:T(8,128)(2,1)} async-done(((bf16[32,1664]{1,0:T(8,128)(2,1)}), bf16[1024,1664]{1,0:T(8,128)(2,1)}) %all-gather.6.cloned.1.call-update) | async-done | bytes 3407888 | tf_op jit(solution)/shard_map/all_gather | solution.py:189
  635.3 5.5 multiply_reduce_fusion.1
  640.8 3.5 convolution_add_fusion
  (91 shorter events, 43.3 us)
Async XLA Ops:
  8.0 87.1 %copy-start = (bf16[1024,1664]{1,0:T(8,128)(2,1)S(1)}, bf16[1024,1664]{1,0:T(8,128)(2,1)}, u32[]{:S(2)}) copy-start(bf16[1024,1664]{1,0:T(8,128)(2,1)} %param.8) | copy-start | bytes 10223620
  8.0 152.4 %all-reduce.11.cloned.1.call-start = ((), (), s32[]{:S(2)}) async-start(), calls=%async_computation.1 | async-start | bytes 425984 | tf_op jit(solution)/shard_map/psum | solution.py:109
  8.1 3.1 copy-start.1
  11.2 5.0 copy-start.13
  11.2 5.0 copy-start.5
  16.3 0.6 copy-start.16
  17.6 3.9 copy-start.2
  23.0 282.0 %all-reduce.13.cloned.1.call-start = ((), (), s32[]{:S(2)}) async-start(), calls=%async_computation.2 | async-start | bytes 425984 | tf_op jit(solution)/shard_map/psum | solution.py:109
  94.5 0.6 copy-start.10
  96.5 59.4 %copy-start.9 = (f32[2,4,4,4]{3,2,1,0:T(4,128)S(1)}, f32[2,4,4,4]{3,2,1,0:T(4,128)}, u32[]{:S(2)}) copy-start(f32[2,4,4,4]{3,2,1,0:T(4,128)} %param.10) | copy-start | bytes 1540
  148.5 2.9 copy-start.7
  150.2 1.2 copy-start.3
  165.2 7.6 %copy-start.15 = (f32[2,4,4,4]{3,2,1,0:T(4,128)S(1)}, f32[2,4,4,4]{3,2,1,0:T(4,128)}, u32[]{:S(2)}) copy-start(f32[2,4,4,4]{3,2,1,0:T(4,128)} %param.12) | copy-start | bytes 1540
  202.3 341.8 %all-reduce.15.cloned.1.call-start = ((), (), s32[]{:S(2)}) async-start(), calls=%async_computation.5 | async-start | bytes 425984 | tf_op jit(solution)/shard_map/psum | solution.py:183
  203.7 101.2 %copy-start.18 = (f32[32]{0:T(128)S(1)}, f32[32]{0:T(128)}, u32[]{:S(2)}) copy-start(f32[32]{0:T(128)} %get-tuple-element.26) | copy-start | bytes 388
  203.7 103.6 %copy-start.14 = (f32[1024]{0:T(1024)S(1)}, f32[1024]{0:T(1024)}, u32[]{:S(2)}) copy-start(f32[1024]{0:T(1024)} %dynamic-update-slice) | copy-start | bytes 12292
  203.7 236.1 %copy-start.11 = (f32[1024]{0:T(1024)S(1)}, f32[1024]{0:T(1024)}, u32[]{:S(2)}) copy-start(f32[1024]{0:T(1024)} %copy-done.10) | copy-start | bytes 12292
  306.8 0.5 copy-start.20
  445.3 101.7 %all-gather.4.cloned.1.call-start = ((), (), s32[]{:S(2)}) async-start(), calls=%async_computation | async-start | bytes 3514368 | tf_op jit(solution)/shard_map/all_gather | solution.py:191
  445.9 126.6 %all-gather.8.cloned.1.call-start = ((), (), s32[]{:S(2)}) async-start(), calls=%async_computation.4 | async-start | bytes 3514368 | tf_op jit(solution)/shard_map/all_gather | solution.py:190
  446.5 188.8 %all-gather.6.cloned.1.call-start = ((), (), s32[]{:S(2)}) async-start(), calls=%async_computation.3 | async-start | bytes 3514368 | tf_op jit(solution)/shard_map/all_gather | solution.py:189
  447.1 3.9 copy-start.12
  447.1 4.5 copy-start.4
  447.1 4.5 copy-start.8
  448.0 96.1 %copy-start.6 = (bf16[32,1664]{1,0:T(8,128)(2,1)S(1)}, bf16[32,1664]{1,0:T(8,128)(2,1)}, u32[]{:S(2)}) copy-start(bf16[32,1664]{1,0:T(8,128)(2,1)} %param.9) | copy-start | bytes 319492
  448.0 96.1 %copy-start.17 = (f32[32]{0:T(128)S(1)}, f32[32]{0:T(128)}, u32[]{:S(2)}) copy-start(f32[32]{0:T(128)} %copy-done.16) | copy-start | bytes 388
  547.0 88.3 %copy-start.19 = (f32[1024]{0:T(1024)S(1)}, f32[1024]{0:T(1024)}, u32[]{:S(2)}) copy-start(f32[1024]{0:T(1024)} %get-tuple-element.21) | copy-start | bytes 12292
Sparse Core Ops, SparseCore 0:
  23.1 102.7 all-reduce.10
  202.4 102.4 all-reduce.12
  445.5 98.6 all-reduce.14
Sparse Core Ops, SparseCore 1:
  447.7 62.2 all-gather.3
  511.8 60.7 all-gather.7
  574.3 61.0 all-gather.5
where the time goes:
time: 653 us; the launch traced here: 652 us
  blocking collectives  301 us (46%)
  waiting for transfers between devices  223 us (34%)
  matrix products  55.9 us (9%)
  local copies, waits for them, and re-layouts  38.1 us (6%)
  other arithmetic  16.5 us (3%)
  between operations  16.3 us (2%)
    psum x2, blocking collectives, token_total(): return lax.psum(partial_sums, 'exp')  204 us
    psum x2, blocking collectives, slot_total(): return lax.psum((first_part, second_part), 'seq')  97.3 us
    psum x1, waiting for transfers between devices, local(): lax.psum(jnp.dot(logit_grad_b, token_unit_b, preferred_element_type=jnp.f...  89.4 us
    all_gather x1, waiting for transfers between devices, local(): lax.all_gather(input_grad_b, 'exp', axis=0, tiled=True)  59 us
    psum x2, waiting for transfers between devices, slot_total(): return lax.psum((first_part, second_part), 'seq')  51 us
    all_gather x1, waiting for transfers between devices, local(): lax.all_gather(slot_out_b, 'exp', axis=0, tiled=True)  22.4 us
  transfers between devices with their start and end apart: 6, of which 4 were waited for; matrix products, arithmetic and copies ran while one was open for 5% of the time, Pallas kernels for 0%

commit v1 on v0

v1 whole, which is shorter than its diff:
```python
import functools

import jax
import jax.numpy as jnp
from jax import lax
from jax.experimental import pallas as pl
from jax.experimental.pallas import tpu as pltpu
from jax.sharding import Mesh, PartitionSpec as P

logit_gain = 64.0
norm_eps = 1e-06
gelu_coef = 0.7978845608028654
cubic_coef = 0.044715

f32 = jnp.float32
bf16 = jnp.bfloat16
DIM = 1664
EXTRA = 128
DB = 416
NF = 4
ROWS = 16
HB = 256
TOK = 1024
CHUNK = 256
VMEM = pltpu.VMEM
SMEM = pltpu.SMEM
seq_axes = ("h", "x")
exp_axes = ("z", "y", "c")


def dot(a, b):
    return jnp.dot(a, b, preferred_element_type=f32)


def dot_t(a, b):
    return lax.dot_general(a, b, (((1,), (1,)), ((), ())), preferred_element_type=f32)


def dot_0(a, b):
    return lax.dot_general(a, b, (((0,), (0,)), ((), ())), preferred_element_type=f32)


def call(body, out, n_smem, n_in, flops, byts, name, scratch=()):
    return pl.pallas_call(
        body,
        out_shape=out,
        in_specs=[pl.BlockSpec(memory_space=SMEM)] * n_smem
        + [pl.BlockSpec(memory_space=VMEM)] * n_in,
        out_specs=jax.tree.map(lambda _: pl.BlockSpec(memory_space=VMEM), out),
        scratch_shapes=list(scratch),
        compiler_params=pltpu.CompilerParams(vmem_limit_bytes=32 << 20),
        cost_estimate=pl.CostEstimate(flops=flops, bytes_accessed=byts, transcendentals=0),
        name=name,
    )


def sds(shape, dtype):
    return jax.ShapeDtypeStruct(shape, dtype)


def unit_rows(values):
    norm = jnp.sqrt(jnp.sum(values * values, axis=1, keepdims=True) + norm_eps)
    return values / norm


def hi_lo(value, first):
    hi = value.astype(bf16).astype(f32)
    return jnp.where(first, hi, value - hi)


def split_blocks(rows):
    return jnp.concatenate([rows[:, a * DB : (a + 1) * DB] for a in range(NF)], axis=0)


def group(rows, a):
    return rows[a * ROWS : (a + 1) * ROWS]


def routing_body(tok_ref, slot_ref, w_ref, inv_ref, colsum_ref, pay_ref, acc_ref, tot_ref, col_ref):
    step = pl.program_id(0)
    tok = tok_ref[...]
    unit_b = unit_rows(slot_ref[...].astype(f32)).astype(bf16)
    inv = []
    for r in range(CHUNK // 128):
        part = tok_ref[pl.ds(r * 128, 128), :].astype(f32)
        sq = jnp.sum(part * part, axis=1, keepdims=True)
        inv.append(jnp.transpose(jnp.broadcast_to(sq, (128, 128)))[0:1])
    inv = lax.rsqrt(jnp.concatenate(inv, axis=1) + norm_eps)
    inv_ref[...] = inv
    w = jnp.exp(logit_gain * dot_t(unit_b, tok) * inv)
    w_ref[...] = w
    cols = jnp.sum(w, axis=0, keepdims=True)
    for r in range(CHUNK // 128):
        col_ref[pl.ds(step * (CHUNK // 128) + r, 1), :] = cols[:, r * 128 : (r + 1) * 128]
    part = dot(w.astype(bf16), tok)
    total = jnp.broadcast_to(jnp.sum(w, axis=1, keepdims=True), (w.shape[0], EXTRA))

    @pl.when(step == 0)
    def _():
        acc_ref[...] = part
        tot_ref[...] = total

    @pl.when(step > 0)
    def _():
        acc_ref[...] += part
        tot_ref[...] += total

    @pl.when(step == pl.num_programs(0) - 1)
    def _():
        lane = lax.broadcasted_iota(jnp.int32, tot_ref.shape, 1)
        pay_ref[:, :DIM] = acc_ref[...].astype(bf16)
        pay_ref[:, DIM:] = hi_lo(tot_ref[...], lane < 1).astype(bf16)
        colsum_ref[...] = jnp.broadcast_to(col_ref[...][None], colsum_ref.shape)


def routing(tokens, slot_params):
    slots = slot_params.shape[0]
    return pl.pallas_call(
        routing_body,
        grid=(TOK // CHUNK,),
        in_specs=[
            pl.BlockSpec((CHUNK, DIM), lambda i: (i, 0)),
            pl.BlockSpec((slots, DIM), lambda i: (0, 0)),
        ],
        out_specs=[
            pl.BlockSpec((slots, CHUNK), lambda i: (0, i)),
            pl.BlockSpec((1, CHUNK), lambda i: (0, i)),
            pl.BlockSpec((32, 8, 128), lambda i: (0, 0, 0)),
            pl.BlockSpec((slots, DIM + EXTRA), lambda i: (0, 0)),
        ],
        out_shape=[
            sds((slots, TOK), f32),
            sds((1, TOK), f32),
            sds((32, 8, 128), f32),
            sds((slots, DIM + EXTRA), bf16),
        ],
        scratch_shapes=[VMEM((slots, DIM), f32), VMEM((slots, EXTRA), f32), VMEM((8, 128), f32)],
        compiler_params=pltpu.CompilerParams(vmem_limit_bytes=32 << 20),
        cost_estimate=pl.CostEstimate(flops=4 * 32 * TOK * DIM, bytes_accessed=4 << 20, transcendentals=0),
        name="routing",
    )(tokens, slot_params)


def row_of(tile):
    return jnp.concatenate([tile[r : r + 1] for r in range(8)], axis=1)


def tile_of(row):
    return jnp.concatenate([row[:, r * 128 : (r + 1) * 128] for r in range(8)], axis=0)


def combine_body(parts_ref, w_ref, grad_ref, total_ref, out_ref):
    total = row_of(jnp.sum(parts_ref[...], axis=0))
    total_ref[...] = total
    combine = (w_ref[...] / total).astype(bf16)
    out_ref[...] = dot(combine, grad_ref[...]).astype(bf16)


def sum_parts(ref):
    total = ref[0].astype(f32)
    for k in range(1, ref.shape[0]):
        total = total + ref[k].astype(f32)
    return total


def forward_body(m1, m2, parts_ref, first_ref, second_ref, x_ref, xs_ref, dt_ref, y_ref, h_ref, sl_ref, s_ref, out_ref):
    total = sum_parts(parts_ref)
    dt = total[:, DIM : DIM + 1] + total[:, DIM + 1 : DIM + 2]
    dt_ref[...] = dt
    x = total[:, :DIM] / dt
    x_ref[...] = x
    xb = x.astype(bf16)
    for e in range(2):
        xs = split_blocks(xb[e * ROWS : (e + 1) * ROWS])
        xs_ref[e] = xs
        ys = [dot(xs, first_ref[e, i]) for i in range(NF)]
        for i in range(NF):
            y_ref[e, :, i * HB : (i + 1) * HB] = ys[i].astype(bf16)
        hid = []
        for b in range(NF):
            pre = None
            for i in range(NF):
                for a in range(NF):
                    term = m1[e, i * 16 + a * 4 + b] * group(ys[i], a)
                    pre = term if pre is None else pre + term
            inner = gelu_coef * (pre + cubic_coef * pre * pre * pre)
            tang = jnp.tanh(inner)
            hid_b = (0.5 * pre * (1.0 + tang)).astype(bf16)
            h_ref[e, b * ROWS : (b + 1) * ROWS, :] = hid_b
            hid.append(hid_b.astype(f32))
            sl_ref[e, b * ROWS : (b + 1) * ROWS, :] = 0.5 * (1.0 + tang) + 0.5 * pre * (
                1.0 - tang * tang
            ) * gelu_coef * (1.0 + 3.0 * cubic_coef * pre * pre)
        out = None
        for i in range(NF):
            rows = []
            for b in range(NF):
                acc = None
                for a in range(NF):
                    term = m2[e, i * 16 + a * 4 + b] * hid[a]
                    acc = term if acc is None else acc + term
                rows.append(acc.astype(bf16))
            si = jnp.concatenate(rows, axis=0)
            s_ref[e, :, i * HB : (i + 1) * HB] = si
            term = dot(si, second_ref[e, i])
            out = term if out is None else out + term
        for b in range(NF):
            out_ref[e * ROWS : (e + 1) * ROWS, b * DB : (b + 1) * DB] = group(out, b).astype(bf16)


def pair_sums(mats, same, column):
    rows = []
    for mat in mats:
        masked = jnp.where(same, mat, 0.0)
        for a in range(NF):
            rows.append(jnp.sum(group(masked, a), axis=0, keepdims=True))
    stack = jnp.concatenate(rows, axis=0)
    lane = lax.broadcasted_iota(jnp.int32, (NF * NF, EXTRA), 1)
    result = jnp.zeros((NF * NF, EXTRA), f32)
    for b in range(NF):
        value = jnp.sum(stack[:, b * ROWS : (b + 1) * ROWS], axis=1, keepdims=True)
        here = (lane == column + b) | (lane == column + b + 2 * NF)
        result = jnp.where(here, value, result)
    return result


def backward_body(m1, m2, parts_ref, first_ref, second_ref, y_ref, h_ref, sl_ref, gb_ref, hm_ref, out_ref):
    grad_b = sum_parts(parts_ref).astype(bf16)
    n = NF * ROWS
    r = lax.broadcasted_iota(jnp.int32, (n, n), 0)
    c = lax.broadcasted_iota(jnp.int32, (n, n), 1)
    same = (r & (ROWS - 1)) == (c & (ROWS - 1))
    lane = lax.broadcasted_iota(jnp.int32, (NF * NF, EXTRA), 1)
    for e in range(2):
        g = split_blocks(grad_b[e * ROWS : (e + 1) * ROWS])
        gb_ref[e] = g
        gs = [dot_t(g, second_ref[e, i]) for i in range(NF)]
        gps = []
        for a in range(NF):
            acc = None
            for i in range(NF):
                for b in range(NF):
                    term = m2[e, i * 16 + a * 4 + b] * group(gs[i], b)
                    acc = term if acc is None else acc + term
            gps.append((acc * sl_ref[e, a * ROWS : (a + 1) * ROWS, :]).astype(bf16))
        gp = jnp.concatenate(gps, axis=0)
        gpf = [v.astype(f32) for v in gps]
        out = None
        for i in range(NF):
            rows = []
            for a in range(NF):
                acc = None
                for b in range(NF):
                    term = m1[e, i * 16 + a * 4 + b] * gpf[b]
                    acc = term if acc is None else acc + term
                rows.append(acc.astype(bf16))
            hi = jnp.concatenate(rows, axis=0)
            hm_ref[e, :, i * HB : (i + 1) * HB] = hi
            term = dot_t(hi, first_ref[e, i])
            out = term if out is None else out + term
        for a in range(NF):
            out_ref[e * ROWS : (e + 1) * ROWS, a * DB : (a + 1) * DB] = group(out, a).astype(bf16)
        hid = h_ref[e]
        mix2 = pair_sums([dot_t(hid, gs[i].astype(bf16)) for i in range(NF)], same, NF)
        mix1 = pair_sums([dot_t(y_ref[e, :, i * HB : (i + 1) * HB], gp) for i in range(NF)], same, 0)
        out_ref[e * ROWS : (e + 1) * ROWS, DIM:] = hi_lo(mix1 + mix2, lane < 2 * NF).astype(bf16)


def weight_grad_body(xs_ref, hm_ref, s_ref, gb_ref, first_ref, second_ref):
    for e in range(2):
        for i in range(NF):
            cols = slice(i * HB, (i + 1) * HB)
            first_ref[e, i] = dot_0(xs_ref[e], hm_ref[e, :, cols]).astype(bf16)
            second_ref[e, i] = dot_0(s_ref[e, :, cols], gb_ref[e]).astype(bf16)


def combine_grad_body(parts_ref, grad_ref, w_ref, total_ref, cg_ref, cols_ref):
    out_b = sum_parts(parts_ref).astype(bf16)
    cg = dot_t(out_b, grad_ref[...])
    cg_ref[...] = cg
    combine = w_ref[...] / total_ref[...]
    cols = tile_of(jnp.sum(combine * cg, axis=0, keepdims=True))
    cols_ref[...] = jnp.broadcast_to(cols[None], cols_ref.shape)


def logit_body(parts_ref, x_ref, dt_ref, w_ref, total_ref, cg_ref, cdots_ref, inv_ref, tok_ref, pay_ref, ug_ref, mix_ref):
    total = sum_parts(parts_ref)
    mix_ref[...] = total[:, DIM:]
    grad = total[:, :DIM]
    grad_b = grad.astype(bf16)
    ddot = jnp.sum(x_ref[...] * grad, axis=1, keepdims=True)
    cdot = row_of(jnp.sum(cdots_ref[...], axis=0))
    tok = tok_ref[...]
    dg = dot_t(grad_b, tok)
    w = w_ref[...]
    combine = w / total_ref[...]
    dispatch = w / dt_ref[...]
    lg = combine * (cg_ref[...] - cdot) + dispatch * (dg - ddot)
    lgb = (logit_gain * lg * inv_ref[...]).astype(bf16)
    ug_ref[...] = dot(lgb, tok).astype(bf16)
    db = dispatch.astype(bf16)
    for k in range(4):
        pay_ref[k, :, :DIM] = grad_b
        pay_ref[k, :, DIM : DIM + 256] = lgb[:, k * 256 : (k + 1) * 256]
        pay_ref[k, :, DIM + 256 :] = db[:, k * 256 : (k + 1) * 256]


def token_body(core, recv_ref, slot_ref, tok_ref, keep_ref, send_ref):
    n = 4 * 32
    unit_b = unit_rows(slot_ref[...].reshape(n, DIM).astype(f32)).astype(bf16)
    recv = recv_ref[...].reshape(n, DIM + 512)
    grad = recv[:, :DIM]
    lgb = recv[:, DIM : DIM + 256]
    db = recv[:, DIM + 256 :]
    direct = dot_0(db, grad)
    through = dot_0(lgb, unit_b)
    first = core[0] == 0
    for y in range(4):
        pair = []
        for c in range(2):
            lo = (y * 2 + c) * 32
            t = tok_ref[lo : lo + 32, :].astype(f32)
            u = through[lo : lo + 32]
            n2 = jnp.sum(t * t, axis=1, keepdims=True) + norm_eps
            coef = jnp.sum(t * u, axis=1, keepdims=True) / n2
            pair.append(direct[lo : lo + 32] + u - t * coef)
        keep_ref[y] = jnp.where(first, pair[0], pair[1])
        send_ref[y] = jnp.where(first, pair[1], pair[0]).astype(bf16)


def slot_body(parts_ref, slot_ref, out_ref):
    ug = sum_parts(parts_ref)
    values = slot_ref[...].astype(f32)
    norm = jnp.sqrt(jnp.sum(values * values, axis=1, keepdims=True) + norm_eps)
    unit = values / norm
    out_ref[...] = (ug - unit * jnp.sum(unit * ug, axis=1, keepdims=True)) / norm


def swap(value, axis):
    return lax.ppermute(value, axis, [(0, 1), (1, 0)])


def spread(value, axes, count):
    return lax.all_to_all(jnp.broadcast_to(value[None], (count,) + value.shape), axes, 0, 0)


def seq_parts(value):
    both = (value.astype(f32) + swap(value, "h").astype(f32)).astype(bf16)
    return spread(both, "x", 4)


def local(tokens, out_grad, slot_params, first_mixing, first_blocks, second_mixing, second_blocks):
    m1 = first_mixing.reshape(2, NF * NF * NF)
    m2 = second_mixing.reshape(2, NF * NF * NF)
    slot_all = spread(slot_params, "z", 4)
    w, inv, colsum, input_part = routing(tokens, slot_params)
    col_parts = lax.all_to_all(colsum, exp_axes, 0, 0)
    input_parts = seq_parts(input_part)
    total, grad_part = call(
        combine_body, (sds((1, TOK), f32), sds((32, DIM), bf16)), 0, 3, 2 * 32 * TOK * DIM, 4 << 20, "combine"
    )(col_parts, w, out_grad)
    x, xs, dt, y, hid, slopes, second_in, out_part = call(
        forward_body,
        (
            sds((32, DIM), f32),
            sds((2, 64, DB), bf16),
            sds((32, 1), f32),
            sds((2, 64, NF * HB), bf16),
            sds((2, 64, HB), bf16),
            sds((2, 64, HB), f32),
            sds((2, 64, NF * HB), bf16),
            sds((32, DIM), bf16),
        ),
        2,
        3,
        4 * 128 * 1024 * DB,
        5 << 20,
        "forward",
    )(m1, m2, input_parts, first_blocks, second_blocks)
    grad_parts = seq_parts(grad_part)
    out_parts = seq_parts(out_part)
    gb, hm, input_grad_part = call(
        backward_body,
        (sds((2, 64, DB), bf16), sds((2, 64, NF * HB), bf16), sds((32, DIM + EXTRA), bf16)),
        2,
        6,
        4 * 128 * 1024 * DB,
        5 << 20,
        "backward",
    )(m1, m2, grad_parts, first_blocks, second_blocks, y, hid, slopes)
    input_grad_parts = seq_parts(input_grad_part)
    first_grad, second_grad = call(
        weight_grad_body,
        (sds(first_blocks.shape, bf16), sds(second_blocks.shape, bf16)),
        0,
        4,
        4 * 128 * 1024 * DB,
        5 << 20,
        "weight_grad",
    )(xs, hm, second_in, gb)
    cg, cols = call(
        combine_grad_body,
        (sds((32, TOK), f32), sds((32, 8, 128), f32)),
        0,
        4,
        2 * 32 * TOK * DIM,
        4 << 20,
        "combine_grad",
    )(out_parts, out_grad, w, total)
    cdots = lax.all_to_all(cols, exp_axes, 0, 0)
    pay, ug_part, mix = call(
        logit_body,
        (sds((4, 32, DIM + 512), bf16), sds((32, DIM), bf16), sds((32, EXTRA), f32)),
        0,
        9,
        4 * 32 * TOK * DIM,
        4 << 20,
        "logit_grad",
    )(input_grad_parts, x, dt, w, total, cg, cdots, inv, tokens)
    recv = lax.all_to_all(pay, "z", 0, 0)
    ug_parts = seq_parts(ug_part)
    quarter = lax.dynamic_slice_in_dim(tokens, lax.axis_index("z") * 256, 256, 0)
    core = lax.axis_index("c").astype(jnp.int32).reshape(1)
    keep, send = call(
        token_body,
        (sds((4, 32, DIM), f32), sds((4, 32, DIM), bf16)),
        1,
        3,
        4 * 128 * 256 * DIM,
        4 << 20,
        "token_grad",
    )(core, recv, slot_all, quarter)
    half = (keep + swap(send, "c").astype(f32)).astype(bf16)
    grad_tokens = jnp.sum(lax.all_to_all(half, "y", 0, 0).astype(f32), axis=0)
    grad_slots = call(
        slot_body, sds((32, DIM), f32), 0, 2, 32 * DIM * 8, 1 << 20, "slot_grad"
    )(ug_parts, slot_params)
    mixes = (mix[:, : 2 * NF] + mix[:, 2 * NF : 4 * NF]).reshape(2, NF, NF, 2, NF)
    return (
        grad_tokens,
        grad_slots,
        mixes[:, :, :, 0],
        first_grad,
        mixes[:, :, :, 1],
        second_grad,
    )


def solution(mesh):
    fine = Mesh(mesh.devices.reshape(2, 4, 4, 4, 2), seq_axes + exp_axes)
    return jax.shard_map(
        local,
        mesh=fine,
        in_specs=(
            P(seq_axes, None),
            P(seq_axes, None),
            P(exp_axes, None),
            P(exp_axes, None, None, None),
            P(exp_axes, None, None, seq_axes),
            P(exp_axes, None, None, None),
            P(exp_axes, None, seq_axes, None),
        ),
        out_specs=(
            P(seq_axes + exp_axes, None),
            P(exp_axes, None),
            P(exp_axes, None, None, None),
            P(exp_axes, None, None, seq_axes),
            P(exp_axes, None, None, None),
            P(exp_axes, None, seq_axes, None),
        ),
        check_vma=False,
    )
```

time: 653 us -> 185 us (0.28)
  blocking collectives: 301 us -> 12.6 us
  waiting for transfers between devices: 223 us -> 41.1 us
  starting transfers between devices: 0.25 us -> 61.8 us
  matrix products: 55.9 us -> 0 us
  Pallas kernels: 0 us -> 20.9 us
  between operations: 16.3 us -> 0.92 us
  other arithmetic: 16.5 us -> 8.33 us
    psum x4 -> x0, blocking collectives: 301 us -> none  [the longest x2 204 us: token_total(): return lax.psum(partial_sums, 'exp')]
    psum x3 -> x0, waiting for transfers between devices: 140 us -> none  [the longest x1 89.4 us: local(): lax.psum(jnp.dot(logit_grad_b, token_unit_b, preferred_element_type=jnp.f...]
    all_gather x3 -> x0, waiting for transfers between devices: 81.4 us -> none  [the longest x1 59 us: local(): lax.all_gather(input_grad_b, 'exp', axis=0, tiled=True)]
    dot_general x21 -> x0, matrix products: 55.9 us -> none  [the longest x1 5.5 us: local(): through = jnp.dot(own_logit_b, unit_all, preferred_element_type=jnp.float32)]
    all_to_all x0 -> x9, starting transfers between devices: none -> 41.5 us  [the longest x5 19.4 us: spread(): lax.all_to_all(jnp.broadcast_to(value[None], (count,) + value.shape), axe...]
    all_to_all x0 -> x9, waiting for transfers between devices: none -> 41.1 us  [the longest x5 15.7 us: spread(): lax.all_to_all(jnp.broadcast_to(value[None], (count,) + value.shape), axe...]
    pallas_call x0 -> x9, Pallas kernels: none -> 20.9 us  [the longest x1 4.11 us: routing(): pl.pallas_call(routing_body, grid=(TOK // CHUNK,), in_specs=[pl.BlockSpec...]
    ppermute x0 -> x6, starting transfers between devices: none -> 20.3 us  [swap(): return lax.ppermute(value, axis, [(0, 1), (1, 0)])]
  transfers between devices with their start and end apart: 6 -> 15, of which waited for: 4 -> 8; matrix products, arithmetic and copies ran while one was open for 5% -> 10% of each run, Pallas kernels for 0% -> 9%
where the time goes in v1:
time: 185 us; the launch traced here: 184 us
  starting transfers between devices  61.8 us (33%)
  waiting for transfers between devices  41.1 us (22%)
  local copies, waits for them, and re-layouts  38.2 us (21%)
  Pallas kernels  20.9 us (11%)
  blocking collectives  12.6 us (7%)
  other arithmetic  8.33 us (5%)
    unnamed x68, local copies, waits for them, and re-layouts  26.4 us
    ppermute x6, starting transfers between devices, swap(): return lax.ppermute(value, axis, [(0, 1), (1, 0)])  20.3 us
    all_to_all x5, starting transfers between devices, spread(): lax.all_to_all(jnp.broadcast_to(value[None], (count,) + value.shape), axe...  19.4 us
    all_to_all x5, waiting for transfers between devices, spread(): lax.all_to_all(jnp.broadcast_to(value[None], (count,) + value.shape), axe...  15.7 us
    all_to_all x1, blocking collectives, spread(): lax.all_to_all(jnp.broadcast_to(value[None], (count,) + value.shape), axe...  12.6 us
    broadcast_in_dim x6, local copies, waits for them, and re-layouts, spread(): jnp.broadcast_to(value[None], (count,) + value.shape)  7.57 us
    all_to_all x1, starting transfers between devices, local(): cdots = lax.all_to_all(cols, exp_axes, 0, 0)  7.56 us
    all_to_all x1, starting transfers between devices, local(): col_parts = lax.all_to_all(colsum, exp_axes, 0, 0)  7 us
  transfers between devices with their start and end apart: 15, of which 8 were waited for; matrix products, arithmetic and copies ran while one was open for 10% of the time, Pallas kernels for 9%

profile of v1, /device:TPU:1, one launch (start us, length us, event | category | flops | bytes accessed | tf_op | source)
XLA Modules:
  0.0 183.9 jit_solution(2284127843650876113)
XLA Ops:
  0.6 2.0 %copy-done = bf16[1024,1664]{1,0:T(8,128)(2,1)S(1)} copy-done((bf16[1024,1664]{1,0:T(8,128)(2,1)S(1)}, bf16[1024,1664]{1,0:T(8,128)(2,1)}, u32[]{:S(2)}) %copy-start) | copy-done | bytes 3407896
  3.5 4.1 %routing.1 = (f32[32,1024]{1,0:T(8,128)S(1)}, f32[1,1024]{1,0:T(1,128)S(1)}, f32[32,8,128]{2,1,0:T(8,128)S(1)}, bf16[32,1792]{1,0:T(8,128)(2,1)}) custom-call(bf16[1024,1664]{1,0:T(8,128)(2,1)S(1)} %copy-done, bf16[32,1664]{1,0:T(8,128)(2,1)S(1)} %copy-done.8), custom_call_target="tpu_custom_call" | custom-call | flops 218103808 | bytes 4194304 | tf_op jit(solution)/shard_map/routing/pallas_call | solution.py:118
  8.2 7.7 %collective-permute-start.1 = (bf16[32,1792]{1,0:T(8,128)(2,1)}, bf16[32,1792]{1,0:T(8,128)(2,1)}, u32[]{:S(2)}, u32[]{:S(2)}) collective-permute-start(bf16[32,1792]{1,0:T(8,128)(2,1)} %get-tuple-element.35), channel_id=1, source_target_pairs={{0,128},{128,0},{1,129},{129,1},{2,130},{130,2},{3,131},{131,3},{4... | collective-permute-start | bytes 344072 | tf_op jit(solution)/shard_map/ppermute | solution.py:340
  15.9 7.0 %all-to-all-start = ((f32[32,8,128]{2,1,0:T(8,128)}), f32[32,8,128]{2,1,0:T(8,128)}, u32[]{:S(2)}, u32[]{:S(2)}) async-start(f32[32,8,128]{2,1,0:T(8,128)} %copy-done.15), calls=%async_computation | async-start | bytes 262144 | tf_op jit(solution)/shard_map/all_to_all | solution.py:357
  24.6 7.0 %all-to-all-done.parts_ref = f32[32,8,128]{2,1,0:T(8,128)} async-done(((f32[32,8,128]{2,1,0:T(8,128)}), f32[32,8,128]{2,1,0:T(8,128)}, u32[]{:S(2)}, u32[]{:S(2)}) %all-to-all-start) | async-done | bytes 131104 | tf_op jit(solution)/shard_map/all_to_all | solution.py:357
  31.5 1.7 broadcast_in_dim.13
  33.2 4.1 %all-to-all-start.2 = ((bf16[4,32,1792]{2,1,0:T(8,128)(2,1)}), bf16[4,32,1792]{2,1,0:T(8,128)(2,1)}, u32[]{:S(2)}, u32[]{:S(2)}) async-start(bf16[4,32,1792]{2,1,0:T(8,128)(2,1)} %broadcast_in_dim.13), calls=%async_computation.2 | async-start | bytes 917504 | tf_op jit(solution)/shard_map/all_to_all | solution.py:344
  37.4 2.3 %combine.1 = (f32[1,1024]{1,0:T(1,128)S(1)}, bf16[32,1664]{1,0:T(8,128)(2,1)}) custom-call(f32[32,8,128]{2,1,0:T(8,128)} %all-to-all-done.parts_ref, f32[32,1024]{1,0:T(8,128)S(1)} %get-tuple-element.33.w_ref, bf16[1024,1664]{1,0:T(8,128)(2,1)S(1)} %copy-done.2), custom_call_target="tpu_custom_call" | custom-call | flops 109051904 | bytes 4194304 | tf_op jit(solution)/shard_map/combine/pallas_call | solution.py:359
  42.8 2.7 %copy.19.second_ref = bf16[2,4,256,416]{3,2,1,0:T(8,128)(2,1)S(1)} copy(bf16[2,4,256,416]{2,3,1,0:T(8,128)(2,1)} %param.13) | data formatting | bytes 3407872 | tf_op args[6]
  47.2 2.4 %forward.1 = (f32[32,1664]{1,0:T(8,128)S(1)}, bf16[2,64,416]{2,1,0:T(8,128)(2,1)S(1)}, f32[32,1]{1,0:T(8,128)S(1)}, bf16[2,64,1024]{2,1,0:T(8,128)(2,1)S(1)}, bf...) custom-call(f32[2,64]{1,0:T(2,128)S(1)} %reshape.31.m1, ...), custom_call_target="tpu_custom_call" | custom-call | flops 218103808 | bytes 5242880 | tf_op jit(solution)/shard_map/forward/pallas_call | solution.py:362
  50.9 3.7 %collective-permute-start.3 = (bf16[32,1664]{1,0:T(8,128)(2,1)S(1)}, bf16[32,1664]{1,0:T(8,128)(2,1)}, u32[]{:S(2)}, u32[]{:S(2)}) collective-permute-start(bf16[32,1664]{1,0:T(8,128)(2,1)S(1)} %get-tuple-element.43), channel_id=1, source_target_pairs={{0,128},{128,0},{1,129},{129,1},{2,130},{130,2},{3,131},{131,3},{4... | collective-permute-start | bytes 319496 | tf_op jit(solution)/shard_map/ppermute | solution.py:340
  56.3 4.2 %all-to-all-start.1 = ((bf16[4,32,1664]{2,1,0:T(8,128)(2,1)}), bf16[4,32,1664]{2,1,0:T(8,128)(2,1)S(1)}, u32[]{:S(2)}, u32[]{:S(2)}) async-start(bf16[4,32,1664]{2,1,0:T(8,128)(2,1)} %broadcast_in_dim.12), calls=%async_computation.1 | async-start | bytes 851968 | tf_op jit(solution)/shard_map/all_to_all | solution.py:344
  62.0 4.9 %all-to-all-done.1.parts_ref = bf16[4,32,1664]{2,1,0:T(8,128)(2,1)S(1)} async-done(((bf16[4,32,1664]{2,1,0:T(8,128)(2,1)}), bf16[4,32,1664]{2,1,0:T(8,128)(2,1)S(1)}, u32[]{:S(2)}, u32[]{:S(2)}) %all-to-all-start.1) | async-done | bytes 426016 | tf_op jit(solution)/shard_map/all_to_all | solution.py:344
  68.6 3.5 %all-to-all-start.4 = ((bf16[4,32,1664]{2,1,0:T(8,128)(2,1)}), bf16[4,32,1664]{2,1,0:T(8,128)(2,1)S(1)}, u32[]{:S(2)}, u32[]{:S(2)}) async-start(bf16[4,32,1664]{2,1,0:T(8,128)(2,1)} %broadcast_in_dim.15), calls=%async_computation.4 | async-start | bytes 851968 | tf_op jit(solution)/shard_map/all_to_all | solution.py:344
  73.5 3.0 %backward.1 = (bf16[2,64,416]{2,1,0:T(8,128)(2,1)S(1)}, bf16[2,64,1024]{2,1,0:T(8,128)(2,1)S(1)}, bf16[32,1792]{1,0:T(8,128)(2,1)}) custom-call(f32[2,64]{1,0:T(2,128)S(1)} %reshape.31.m1, f32[2,64]{1,0:T(2,128)S(1)} %reshape.32.m2, bf16[4,32,1664]{2,1,0:T(8,128)(2,1)S(1)} %all-to-all-done.1.parts_ref, bf16[2,4,416,256]{3,2,1,0:T(8,128)(2,1)S(1)} %copy-done.5, ...), custom_call_target="tpu_custom_call" | custom-call | flops 218103808 | bytes 5242880 | tf_op jit(solution)/shard_map/backward/pallas_call | solution.py:382
  79.5 2.0 %copy-done.3 = bf16[1024,1664]{1,0:T(8,128)(2,1)S(1)} copy-done((bf16[1024,1664]{1,0:T(8,128)(2,1)S(1)}, bf16[1024,1664]{1,0:T(8,128)(2,1)}, u32[]{:S(2)}) %copy-start.3) | copy-done | bytes 3407896
  83.9 7.6 %all-to-all-start.5 = ((f32[32,8,128]{2,1,0:T(8,128)}), f32[32,8,128]{2,1,0:T(8,128)}, u32[]{:S(2)}, u32[]{:S(2)}) async-start(f32[32,8,128]{2,1,0:T(8,128)} %copy-done.16), calls=%async_computation.5 | async-start | bytes 262144 | tf_op jit(solution)/shard_map/all_to_all | solution.py:410
  93.1 7.0 %all-to-all-done.5.cdots_ref = f32[32,8,128]{2,1,0:T(8,128)} async-done(((f32[32,8,128]{2,1,0:T(8,128)}), f32[32,8,128]{2,1,0:T(8,128)}, u32[]{:S(2)}, u32[]{:S(2)}) %all-to-all-start.5) | async-done | bytes 131104 | tf_op jit(solution)/shard_map/all_to_all | solution.py:410
  101.0 12.6 %all_to_all.50.parts_ref = bf16[4,32,1792]{2,1,0:T(8,128)(2,1)} all-to-all(bf16[4,32,1792]{2,1,0:T(8,128)(2,1)S(1)} %broadcast_in_dim.14), channel_id=1, replica_groups=mesh['h'=2,'x'=4,'z'=4,'y'=4,'c'=2] {'x'}, dimensions={0} | all-to-all | bytes 917504 | tf_op jit(solution)/shard_map/all_to_all | solution.py:344
  115.3 4.1 %all-to-all-start.7 = ((bf16[4,32,1664]{2,1,0:T(8,128)(2,1)}), bf16[4,32,1664]{2,1,0:T(8,128)(2,1)}, u32[]{:S(2)}, u32[]{:S(2)}) async-start(bf16[4,32,1664]{2,1,0:T(8,128)(2,1)} %broadcast_in_dim.16), calls=%async_computation.7 | async-start | bytes 851968 | tf_op jit(solution)/shard_map/all_to_all | solution.py:344
  124.3 2.6 %logit_grad.1 = (bf16[4,32,2176]{2,1,0:T(8,128)(2,1)S(1)}, bf16[32,1664]{1,0:T(8,128)(2,1)S(1)}, f32[32,128]{1,0:T(8,128)S(1)}) custom-call(bf16[4,32,1792]{2,1,0:T(8,128)(2,1)S(1)} %copy-done.7, f32[32,1664]{1,0:T(8,128)S(1)} %copy-done.12, f32[32,1]{1,0:T(8,128)S(1)} %copy-done.20, f32[32,1024]{1,0:T(8,128)S(1)} %get-tuple-element.33.w_ref, ...), custom_call_target="tpu_custom_call" | custom-call | flops 218103808 | bytes 4194304 | tf_op jit(solution)/shard_map/logit_grad/pallas_call | solution.py:411
  128.4 2.9 %all-to-all-done.7.slot_ref = bf16[4,32,1664]{2,1,0:T(8,128)(2,1)} async-done(((bf16[4,32,1664]{2,1,0:T(8,128)(2,1)}), bf16[4,32,1664]{2,1,0:T(8,128)(2,1)}, u32[]{:S(2)}, u32[]{:S(2)}) %all-to-all-start.7) | async-done | bytes 426016 | tf_op jit(solution)/shard_map/all_to_all | solution.py:344
  131.3 4.2 %all-to-all-start.6 = ((bf16[4,32,2176]{2,1,0:T(8,128)(2,1)}), bf16[4,32,2176]{2,1,0:T(8,128)(2,1)}, u32[]{:S(2)}, u32[]{:S(2)}) async-start(bf16[4,32,2176]{2,1,0:T(8,128)(2,1)} %copy-done.10), calls=%async_computation.6 | async-start | bytes 1114112 | tf_op jit(solution)/shard_map/all_to_all | solution.py:420
  135.5 4.1 %collective-permute-start.5 = (bf16[32,1664]{1,0:T(8,128)(2,1)}, bf16[32,1664]{1,0:T(8,128)(2,1)}, u32[]{:S(2)}, u32[]{:S(2)}) collective-permute-start(bf16[32,1664]{1,0:T(8,128)(2,1)} %copy-done.17), channel_id=1, source_target_pairs={{0,128},{128,0},{1,129},{129,1},{2,130},{130,2},{3,131},{131,3},{4... | collective-permute-start | bytes 319496 | tf_op jit(solution)/shard_map/ppermute | solution.py:340
  143.4 2.3 %weight_grad.1 = (bf16[2,4,416,256]{3,2,1,0:T(8,128)(2,1)}, bf16[2,4,256,416]{3,2,1,0:T(8,128)(2,1)S(1)}) custom-call(bf16[2,64,416]{2,1,0:T(8,128)(2,1)S(1)} %copy-done.30, bf16[2,64,1024]{2,1,0:T(8,128)(2,1)S(1)} %copy-done.28, bf16[2,64,1024]{2,1,0:T(8,128)(2,1)S(1)} %copy-done.26, bf16[2,64,416]{2,1,0:T(8,128)(2,1)S(1)} %copy-done.32), custom_call_target="tpu_custom_call" | custom-call | flops 218103808 | bytes 5242880 | tf_op jit(solution)/shard_map/weight_grad/pallas_call | solution.py:392
  145.7 2.3 %copy.23 = bf16[2,4,256,416]{2,3,1,0:T(8,128)(2,1)} copy(bf16[2,4,256,416]{3,2,1,0:T(8,128)(2,1)S(1)} %get-tuple-element.69) | data formatting | bytes 3407872
  148.0 6.8 %all-to-all-done.6.recv_ref = bf16[4,32,2176]{2,1,0:T(8,128)(2,1)} async-done(((bf16[4,32,2176]{2,1,0:T(8,128)(2,1)}), bf16[4,32,2176]{2,1,0:T(8,128)(2,1)}, u32[]{:S(2)}, u32[]{:S(2)}) %all-to-all-start.6) | async-done | bytes 557088 | tf_op jit(solution)/shard_map/all_to_all | solution.py:420
  154.8 2.2 %token_grad.1 = (f32[4,32,1664]{2,1,0:T(8,128)S(1)}, bf16[4,32,1664]{2,1,0:T(8,128)(2,1)S(1)}) custom-call(s32[1]{0:T(128)} %bitcast.core, bf16[4,32,2176]{2,1,0:T(8,128)(2,1)} %all-to-all-done.6.recv_ref, bf16[4,32,1664]{2,1,0:T(8,128)(2,1)} %all-to-all-done.7.slot_ref, bf16[256,1664]{1,0:T(8,128)(2,1)S(1)} %copy-done.6), custom_call_target="tpu_custom_call" | custom-call | flops 218103808 | bytes 4194304 | tf_op jit(solution)/shard_map/token_grad/pallas_call | solution.py:424
  160.3 3.5 %all-to-all-start.9 = ((bf16[4,32,1664]{2,1,0:T(8,128)(2,1)}), bf16[4,32,1664]{2,1,0:T(8,128)(2,1)S(1)}, u32[]{:S(2)}, u32[]{:S(2)}) async-start(bf16[4,32,1664]{2,1,0:T(8,128)(2,1)} %broadcast_in_dim.17), calls=%async_computation.9 | async-start | bytes 851968 | tf_op jit(solution)/shard_map/all_to_all | solution.py:344
  164.6 7.7 %all-to-all-done.9.parts_ref = bf16[4,32,1664]{2,1,0:T(8,128)(2,1)S(1)} async-done(((bf16[4,32,1664]{2,1,0:T(8,128)(2,1)}), bf16[4,32,1664]{2,1,0:T(8,128)(2,1)S(1)}, u32[]{:S(2)}, u32[]{:S(2)}) %all-to-all-start.9) | async-done | bytes 426016 | tf_op jit(solution)/shard_map/all_to_all | solution.py:344
  172.3 3.5 %all-to-all-start.8 = ((bf16[4,32,1664]{2,1,0:T(8,128)(2,1)}), bf16[4,32,1664]{2,1,0:T(8,128)(2,1)S(1)}, u32[]{:S(2)}, u32[]{:S(2)}) async-start(bf16[4,32,1664]{2,1,0:T(8,128)(2,1)} %add_convert_fusion), calls=%async_computation.8 | async-start | bytes 851968 | tf_op jit(solution)/shard_map/all_to_all | solution.py:434
  178.4 4.7 %all-to-all-done.8 = bf16[4,32,1664]{2,1,0:T(8,128)(2,1)S(1)} async-done(((bf16[4,32,1664]{2,1,0:T(8,128)(2,1)}), bf16[4,32,1664]{2,1,0:T(8,128)(2,1)S(1)}, u32[]{:S(2)}, u32[]{:S(2)}) %all-to-all-start.8) | async-done | bytes 426016 | tf_op jit(solution)/shard_map/all_to_all | solution.py:434
  (98 shorter events, 42.9 us)
Async XLA Ops:
  0.6 2.0 %copy-start = (bf16[1024,1664]{1,0:T(8,128)(2,1)S(1)}, bf16[1024,1664]{1,0:T(8,128)(2,1)}, u32[]{:S(2)}) copy-start(bf16[1024,1664]{1,0:T(8,128)(2,1)} %tok_ref.3) | copy-start | bytes 10223620
  3.5 33.9 %copy-start.2 = (bf16[1024,1664]{1,0:T(8,128)(2,1)S(1)}, bf16[1024,1664]{1,0:T(8,128)(2,1)}, u32[]{:S(2)}) copy-start(bf16[1024,1664]{1,0:T(8,128)(2,1)} %grad_ref.3) | copy-start | bytes 10223620
  8.2 7.7 %copy-start.15 = (f32[32,8,128]{2,1,0:T(8,128)}, f32[32,8,128]{2,1,0:T(8,128)S(1)}, u32[]{:S(2)}) copy-start(f32[32,8,128]{2,1,0:T(8,128)S(1)} %get-tuple-element.32) | copy-start | bytes 393220
  8.2 14.8 %collective-permute-start.1 = (bf16[32,1792]{1,0:T(8,128)(2,1)}, bf16[32,1792]{1,0:T(8,128)(2,1)}, u32[]{:S(2)}, u32[]{:S(2)}) collective-permute-start(bf16[32,1792]{1,0:T(8,128)(2,1)} %get-tuple-element.35), channel_id=1, source_target_pairs={{0,128},{128,0},{1,129},{129,1},{2,130},{130,2},{3,131},{131,3},{4... | collective-permute-start | bytes 344072 | tf_op jit(solution)/shard_map/ppermute | solution.py:340
  15.9 15.6 %all-to-all-start = ((f32[32,8,128]{2,1,0:T(8,128)}), f32[32,8,128]{2,1,0:T(8,128)}, u32[]{:S(2)}, u32[]{:S(2)}) async-start(f32[32,8,128]{2,1,0:T(8,128)} %copy-done.15), calls=%async_computation | async-start | bytes 262144 | tf_op jit(solution)/shard_map/all_to_all | solution.py:357
  33.2 12.5 %all-to-all-start.2 = ((bf16[4,32,1792]{2,1,0:T(8,128)(2,1)}), bf16[4,32,1792]{2,1,0:T(8,128)(2,1)}, u32[]{:S(2)}, u32[]{:S(2)}) async-start(bf16[4,32,1792]{2,1,0:T(8,128)(2,1)} %broadcast_in_dim.13), calls=%async_computation.2 | async-start | bytes 917504 | tf_op jit(solution)/shard_map/all_to_all | solution.py:344
  39.6 39.8 %copy-start.21 = (f32[1,1024]{1,0:T(1,128)}, f32[1,1024]{1,0:T(1,128)S(1)}, u32[]{:S(2)}) copy-start(f32[1,1024]{1,0:T(1,128)S(1)} %get-tuple-element.42.total_ref) | copy-start | bytes 12292
  39.6 14.9 %collective-permute-start = (bf16[32,1664]{1,0:T(8,128)(2,1)}, bf16[32,1664]{1,0:T(8,128)(2,1)S(1)}, u32[]{:S(2)}, u32[]{:S(2)}) collective-permute-start(bf16[32,1664]{1,0:T(8,128)(2,1)} %get-tuple-element.34), channel_id=1, source_target_pairs={{0,128},{128,0},{1,129},{129,1},{2,130},{130,2},{3,131},{131,3},{4... | collective-permute-start | bytes 319496 | tf_op jit(solution)/shard_map/ppermute | solution.py:340
  45.7 1.5 copy-start.4
  50.9 5.4 %copy-start.29 = (bf16[2,64,416]{2,1,0:T(8,128)(2,1)}, bf16[2,64,416]{2,1,0:T(8,128)(2,1)S(1)}, u32[]{:S(2)}) copy-start(bf16[2,64,416]{2,1,0:T(8,128)(2,1)S(1)} %get-tuple-element.52.xs_ref) | copy-start | bytes 319492
  50.9 17.7 %copy-start.25 = (bf16[2,64,1024]{2,1,0:T(8,128)(2,1)}, bf16[2,64,1024]{2,1,0:T(8,128)(2,1)S(1)}, u32[]{:S(2)}) copy-start(bf16[2,64,1024]{2,1,0:T(8,128)(2,1)S(1)} %get-tuple-element.54.s_ref) | copy-start | bytes 786436
  50.9 9.6 %collective-permute-start.3 = (bf16[32,1664]{1,0:T(8,128)(2,1)S(1)}, bf16[32,1664]{1,0:T(8,128)(2,1)}, u32[]{:S(2)}, u32[]{:S(2)}) collective-permute-start(bf16[32,1664]{1,0:T(8,128)(2,1)S(1)} %get-tuple-element.43), channel_id=1, source_target_pairs={{0,128},{128,0},{1,129},{129,1},{2,130},{130,2},{3,131},{131,3},{4... | collective-permute-start | bytes 319496 | tf_op jit(solution)/shard_map/ppermute | solution.py:340
  56.3 10.6 %all-to-all-start.1 = ((bf16[4,32,1664]{2,1,0:T(8,128)(2,1)}), bf16[4,32,1664]{2,1,0:T(8,128)(2,1)S(1)}, u32[]{:S(2)}, u32[]{:S(2)}) async-start(bf16[4,32,1664]{2,1,0:T(8,128)(2,1)} %broadcast_in_dim.12), calls=%async_computation.1 | async-start | bytes 851968 | tf_op jit(solution)/shard_map/all_to_all | solution.py:344
  68.6 10.9 %all-to-all-start.4 = ((bf16[4,32,1664]{2,1,0:T(8,128)(2,1)}), bf16[4,32,1664]{2,1,0:T(8,128)(2,1)S(1)}, u32[]{:S(2)}, u32[]{:S(2)}) async-start(bf16[4,32,1664]{2,1,0:T(8,128)(2,1)} %broadcast_in_dim.15), calls=%async_computation.4 | async-start | bytes 851968 | tf_op jit(solution)/shard_map/all_to_all | solution.py:344
  72.0 1.5 copy-start.5
  77.8 13.7 %collective-permute-start.2 = (bf16[32,1792]{1,0:T(8,128)(2,1)}, bf16[32,1792]{1,0:T(8,128)(2,1)}, u32[]{:S(2)}, u32[]{:S(2)}) collective-permute-start(bf16[32,1792]{1,0:T(8,128)(2,1)} %get-tuple-element.39), channel_id=1, source_target_pairs={{0,128},{128,0},{1,129},{129,1},{2,130},{130,2},{3,131},{131,3},{4... | collective-permute-start | bytes 344072 | tf_op jit(solution)/shard_map/ppermute | solution.py:340
  79.5 2.0 %copy-start.3 = (bf16[1024,1664]{1,0:T(8,128)(2,1)S(1)}, bf16[1024,1664]{1,0:T(8,128)(2,1)}, u32[]{:S(2)}) copy-start(bf16[1024,1664]{1,0:T(8,128)(2,1)} %grad_ref.3) | copy-start | bytes 10223620
  83.9 35.5 %copy-start.1 = (bf16[1024,1664]{1,0:T(8,128)(2,1)S(1)}, bf16[1024,1664]{1,0:T(8,128)(2,1)}, u32[]{:S(2)}) copy-start(bf16[1024,1664]{1,0:T(8,128)(2,1)} %tok_ref.3) | copy-start | bytes 10223620
  83.9 16.2 %all-to-all-start.5 = ((f32[32,8,128]{2,1,0:T(8,128)}), f32[32,8,128]{2,1,0:T(8,128)}, u32[]{:S(2)}, u32[]{:S(2)}) async-start(f32[32,8,128]{2,1,0:T(8,128)} %copy-done.16), calls=%async_computation.5 | async-start | bytes 262144 | tf_op jit(solution)/shard_map/all_to_all | solution.py:410
  115.3 16.1 %all-to-all-start.7 = ((bf16[4,32,1664]{2,1,0:T(8,128)(2,1)}), bf16[4,32,1664]{2,1,0:T(8,128)(2,1)}, u32[]{:S(2)}, u32[]{:S(2)}) async-start(bf16[4,32,1664]{2,1,0:T(8,128)(2,1)} %broadcast_in_dim.16), calls=%async_computation.7 | async-start | bytes 851968 | tf_op jit(solution)/shard_map/all_to_all | solution.py:344
  119.4 1.0 copy-start.7
  128.4 12.2 %copy-start.30 = (bf16[2,64,416]{2,1,0:T(8,128)(2,1)S(1)}, bf16[2,64,416]{2,1,0:T(8,128)(2,1)}, u32[]{:S(2)}) copy-start(bf16[2,64,416]{2,1,0:T(8,128)(2,1)} %copy-done.29) | copy-start | bytes 319492
  131.3 23.5 %all-to-all-start.6 = ((bf16[4,32,2176]{2,1,0:T(8,128)(2,1)}), bf16[4,32,2176]{2,1,0:T(8,128)(2,1)}, u32[]{:S(2)}, u32[]{:S(2)}) async-start(bf16[4,32,2176]{2,1,0:T(8,128)(2,1)} %copy-done.10), calls=%async_computation.6 | async-start | bytes 1114112 | tf_op jit(solution)/shard_map/all_to_all | solution.py:420
  135.5 23.1 %collective-permute-start.5 = (bf16[32,1664]{1,0:T(8,128)(2,1)}, bf16[32,1664]{1,0:T(8,128)(2,1)}, u32[]{:S(2)}, u32[]{:S(2)}) collective-permute-start(bf16[32,1664]{1,0:T(8,128)(2,1)} %copy-done.17), channel_id=1, source_target_pairs={{0,128},{128,0},{1,129},{129,1},{2,130},{130,2},{3,131},{131,3},{4... | collective-permute-start | bytes 319496 | tf_op jit(solution)/shard_map/ppermute | solution.py:340
  140.6 1.0 copy-start.26
  141.6 0.9 copy-start.28
  145.7 9.1 %copy-start.6 = (bf16[256,1664]{1,0:T(8,128)(2,1)S(1)}, bf16[256,1664]{1,0:T(8,128)(2,1)}, u32[]{:S(2)}) copy-start(bf16[256,1664]{1,0:T(8,128)(2,1)} %constant_dynamic-slice_fusion.tok_ref) | copy-start | bytes 2555908
  145.7 12.8 %copy-start.18 = (bf16[32,1664]{1,0:T(8,128)(2,1)S(1)}, bf16[32,1664]{1,0:T(8,128)(2,1)}, u32[]{:S(2)}) copy-start(bf16[32,1664]{1,0:T(8,128)(2,1)} %copy-done.17) | copy-start | bytes 319492
  157.0 6.8 %collective-permute-start.4 = (bf16[4,32,1664]{2,1,0:T(8,128)(2,1)S(1)}, bf16[4,32,1664]{2,1,0:T(8,128)(2,1)S(1)}, u32[]{:S(2)}, u32[]{:S(2)}) collective-permute-start(bf16[4,32,1664]{2,1,0:T(8,128)(2,1)S(1)} %get-tuple-element.49), channel_id=1, source_target_pairs={{0,1},{1,0},{2,3},{3,2},{4,5},{5,4},{6,7},{7,6},{8,9},{9,8},{10,11... | collective-permute-start | bytes 1277960 | tf_op jit(solution)/shard_map/ppermute | solution.py:340
  159.5 18.0 %copy-start.9 = (bf16[32,1664]{1,0:T(8,128)(2,1)S(1)}, bf16[32,1664]{1,0:T(8,128)(2,1)}, u32[]{:S(2)}) copy-start(bf16[32,1664]{1,0:T(8,128)(2,1)} %slot_ref.3) | copy-start | bytes 319492
  160.3 12.0 %all-to-all-start.9 = ((bf16[4,32,1664]{2,1,0:T(8,128)(2,1)}), bf16[4,32,1664]{2,1,0:T(8,128)(2,1)S(1)}, u32[]{:S(2)}, u32[]{:S(2)}) async-start(bf16[4,32,1664]{2,1,0:T(8,128)(2,1)} %broadcast_in_dim.17), calls=%async_computation.9 | async-start | bytes 851968 | tf_op jit(solution)/shard_map/all_to_all | solution.py:344
  172.3 10.8 %all-to-all-start.8 = ((bf16[4,32,1664]{2,1,0:T(8,128)(2,1)}), bf16[4,32,1664]{2,1,0:T(8,128)(2,1)S(1)}, u32[]{:S(2)}, u32[]{:S(2)}) async-start(bf16[4,32,1664]{2,1,0:T(8,128)(2,1)} %add_convert_fusion), calls=%async_computation.8 | async-start | bytes 851968 | tf_op jit(solution)/shard_map/all_to_all | solution.py:434
  (16 other events, 11.7 us)

commit v2 on v1

v2 whole, which is shorter than its diff:
```python
import jax
import jax.numpy as jnp
from jax import lax
from jax.experimental import pallas as pl
from jax.experimental.pallas import tpu as pltpu
from jax.sharding import Mesh, PartitionSpec as P

logit_gain = 64.0
norm_eps = 1e-06
gelu_coef = 0.7978845608028654
cubic_coef = 0.044715

f32 = jnp.float32
bf16 = jnp.bfloat16
DIM = 1664
EXTRA = 128
DB = 416
NF = 4
ROWS = 16
HB = 256
TOK = 1024
CHUNK = 256
STEPS = TOK // CHUNK
WIDE = 60 << 20
SMALL = 52 << 20
SIDE = 2 * NF * HB
VMEM = pltpu.VMEM
SMEM = pltpu.SMEM
seq_axes = ("h", "x")
exp_axes = ("z", "y", "c")


def dot(a, b):
    return jnp.dot(a, b, preferred_element_type=f32)


def dot_t(a, b):
    return lax.dot_general(a, b, (((1,), (1,)), ((), ())), preferred_element_type=f32)


def dot_0(a, b):
    return lax.dot_general(a, b, (((0,), (0,)), ((), ())), preferred_element_type=f32)


def call(body, out, n_smem, args, flops, byts, name, streamed=False):
    ins = [pl.BlockSpec(memory_space=VMEM)] * (len(args) - n_smem)
    scratch = []
    if streamed:
        ins[-1] = pl.BlockSpec(memory_space=pl.ANY)
        scratch = [VMEM(args[-1].shape, args[-1].dtype), pltpu.SemaphoreType.DMA((STEPS,))]
    return pl.pallas_call(
        body,
        out_shape=out,
        in_specs=[pl.BlockSpec(memory_space=SMEM)] * n_smem + ins,
        out_specs=jax.tree.map(lambda o: pl.BlockSpec(memory_space=VMEM), out),
        scratch_shapes=scratch,
        compiler_params=pltpu.CompilerParams(vmem_limit_bytes=WIDE if streamed else SMALL),
        cost_estimate=pl.CostEstimate(flops=flops, bytes_accessed=byts, transcendentals=0),
        name=name,
    )(*args)


def stream(source, target, sems):
    copies = []
    for k in range(STEPS):
        rows = pl.ds(k * CHUNK, CHUNK)
        copies.append(pltpu.make_async_copy(source.at[rows], target.at[rows], sems.at[k]))
        copies[-1].start()
    return copies


def chunk(k):
    return slice(k * CHUNK, (k + 1) * CHUNK)


def sds(shape, dtype):
    return jax.ShapeDtypeStruct(shape, dtype)


def unit_rows(values):
    norm = jnp.sqrt(jnp.sum(values * values, axis=1, keepdims=True) + norm_eps)
    return values / norm


def hi_lo(value, first):
    hi = value.astype(bf16).astype(f32)
    return jnp.where(first, hi, value - hi)


def split_blocks(rows):
    return jnp.concatenate([rows[:, a * DB : (a + 1) * DB] for a in range(NF)], axis=0)


def group(rows, a):
    return rows[a * ROWS : (a + 1) * ROWS]


def routing_body(slot_ref, tok_hbm, w_ref, colsum_ref, pay_ref, tok_ref, sems):
    copies = stream(tok_hbm, tok_ref, sems)
    unit_b = unit_rows(slot_ref[...].astype(f32)).astype(bf16)
    acc = jnp.zeros(slot_ref.shape, f32)
    total = jnp.zeros((slot_ref.shape[0], 1), f32)
    tiles = []
    for k in range(STEPS):
        copies[k].wait()
        inv = []
        for r in range(CHUNK // 128):
            part = tok_ref[k * CHUNK + r * 128 : k * CHUNK + (r + 1) * 128, :].astype(f32)
            sq = jnp.sum(part * part, axis=1, keepdims=True)
            inv.append(jnp.transpose(jnp.broadcast_to(sq, (128, 128)))[0:1])
        inv = lax.rsqrt(jnp.concatenate(inv, axis=1) + norm_eps)
        cols = chunk(k)
        w_ref[32:, cols] = jnp.broadcast_to(inv, (8, CHUNK))
        tok = tok_ref[cols, :]
        w = jnp.exp(logit_gain * dot_t(unit_b, tok) * inv)
        w_ref[:32, cols] = w
        sums = jnp.sum(w, axis=0, keepdims=True)
        tiles += [sums[:, r * 128 : (r + 1) * 128] for r in range(CHUNK // 128)]
        acc = acc + dot(w.astype(bf16), tok)
        total = total + jnp.sum(w, axis=1, keepdims=True)
    wide = jnp.broadcast_to(total, (total.shape[0], EXTRA))
    lane = lax.broadcasted_iota(jnp.int32, wide.shape, 1)
    pay_ref[:, :DIM] = acc.astype(bf16)
    pay_ref[:, DIM:] = hi_lo(wide, lane < 1).astype(bf16)
    cols = jnp.concatenate(tiles, axis=0)
    colsum_ref[...] = jnp.broadcast_to(cols[None], colsum_ref.shape)


def row_of(tile):
    return jnp.concatenate([tile[r : r + 1] for r in range(8)], axis=1)


def tile_of(row):
    return jnp.concatenate([row[:, r * 128 : (r + 1) * 128] for r in range(8)], axis=0)


def combine_body(parts_ref, w_ref, grad_ref, total_ref, out_ref):
    total = row_of(jnp.sum(parts_ref[...], axis=0))
    total_ref[...] = total
    combine = (w_ref[:32] / total).astype(bf16)
    out_ref[...] = dot(combine, grad_ref[...]).astype(bf16)


def sum_parts(ref):
    total = ref[0].astype(f32)
    for k in range(1, ref.shape[0]):
        total = total + ref[k].astype(f32)
    return total


def sum_ring(a, b, c, d):
    return (a[...].astype(f32) + c[...].astype(f32)) + (b[...].astype(f32) + d[...].astype(f32))


def forward_body(m1, m2, p0, p1, p2, p3, first_ref, second_ref, x_ref, side_ref, sl_ref, out_ref):
    total = sum_ring(p0, p1, p2, p3)
    dt = total[:, DIM : DIM + 1] + total[:, DIM + 1 : DIM + 2]
    x_ref[:, DIM:] = jnp.broadcast_to(dt, (dt.shape[0], EXTRA))
    x = total[:, :DIM] / dt
    x_ref[:, :DIM] = x
    xb = x.astype(bf16)
    for e in range(2):
        xs = split_blocks(xb[e * ROWS : (e + 1) * ROWS])
        ys = [dot(xs, first_ref[e, i]) for i in range(NF)]
        for i in range(NF):
            side_ref[e, :, i * HB : (i + 1) * HB] = ys[i].astype(bf16)
        hid = []
        for b in range(NF):
            pre = None
            for i in range(NF):
                for a in range(NF):
                    term = m1[e, i, a, b] * group(ys[i], a)
                    pre = term if pre is None else pre + term
            inner = gelu_coef * (pre + cubic_coef * pre * pre * pre)
            tang = jnp.tanh(inner)
            hid_b = (0.5 * pre * (1.0 + tang)).astype(bf16)
            side_ref[e, b * ROWS : (b + 1) * ROWS, SIDE:] = hid_b
            hid.append(hid_b.astype(f32))
            sl_ref[e, b * ROWS : (b + 1) * ROWS, :] = 0.5 * (1.0 + tang) + 0.5 * pre * (
                1.0 - tang * tang
            ) * gelu_coef * (1.0 + 3.0 * cubic_coef * pre * pre)
        out = None
        for i in range(NF):
            rows = []
            for b in range(NF):
                acc = None
                for a in range(NF):
                    term = m2[e, i, a, b] * hid[a]
                    acc = term if acc is None else acc + term
                rows.append(acc.astype(bf16))
            si = jnp.concatenate(rows, axis=0)
            side_ref[e, :, (NF + i) * HB : (NF + i + 1) * HB] = si
            term = dot_t(si, second_ref[e, i])
            out = term if out is None else out + term
        for b in range(NF):
            out_ref[e * ROWS : (e + 1) * ROWS, b * DB : (b + 1) * DB] = group(out, b).astype(bf16)


def pair_sums(mats, same, column):
    rows = []
    for mat in mats:
        masked = jnp.where(same, mat, 0.0)
        for a in range(NF):
            rows.append(jnp.sum(group(masked, a), axis=0, keepdims=True))
    stack = jnp.concatenate(rows, axis=0)
    lane = lax.broadcasted_iota(jnp.int32, (NF * NF, EXTRA), 1)
    result = jnp.zeros((NF * NF, EXTRA), f32)
    for b in range(NF):
        value = jnp.sum(stack[:, b * ROWS : (b + 1) * ROWS], axis=1, keepdims=True)
        here = (lane == column + b) | (lane == column + b + 2 * NF)
        result = jnp.where(here, value, result)
    return result


def backward_body(m1, m2, parts_ref, first_ref, second_ref, side_ref, sl_ref, hg_ref, out_ref):
    grad_b = sum_parts(parts_ref).astype(bf16)
    n = NF * ROWS
    r = lax.broadcasted_iota(jnp.int32, (n, n), 0)
    c = lax.broadcasted_iota(jnp.int32, (n, n), 1)
    same = (r & (ROWS - 1)) == (c & (ROWS - 1))
    lane = lax.broadcasted_iota(jnp.int32, (NF * NF, EXTRA), 1)
    for e in range(2):
        g = split_blocks(grad_b[e * ROWS : (e + 1) * ROWS])
        hg_ref[e, :, NF * HB : NF * HB + DB] = g
        gs = [dot(g, second_ref[e, i]) for i in range(NF)]
        gps = []
        for a in range(NF):
            acc = None
            for i in range(NF):
                for b in range(NF):
                    term = m2[e, i, a, b] * group(gs[i], b)
                    acc = term if acc is None else acc + term
            gps.append((acc * sl_ref[e, a * ROWS : (a + 1) * ROWS, :]).astype(bf16))
        gp = jnp.concatenate(gps, axis=0)
        gpf = [v.astype(f32) for v in gps]
        out = None
        for i in range(NF):
            rows = []
            for a in range(NF):
                acc = None
                for b in range(NF):
                    term = m1[e, i, a, b] * gpf[b]
                    acc = term if acc is None else acc + term
                rows.append(acc.astype(bf16))
            hi = jnp.concatenate(rows, axis=0)
            hg_ref[e, :, i * HB : (i + 1) * HB] = hi
            term = dot_t(hi, first_ref[e, i])
            out = term if out is None else out + term
        for a in range(NF):
            out_ref[e * ROWS : (e + 1) * ROWS, a * DB : (a + 1) * DB] = group(out, a).astype(bf16)
        hid = side_ref[e, :, SIDE:]
        mix2 = pair_sums([dot_t(hid, gs[i].astype(bf16)) for i in range(NF)], same, NF)
        mix1 = pair_sums([dot_t(side_ref[e, :, i * HB : (i + 1) * HB], gp) for i in range(NF)], same, 0)
        out_ref[e * ROWS : (e + 1) * ROWS, DIM:] = hi_lo(mix1 + mix2, lane < 2 * NF).astype(bf16)


def weight_grad_body(x_ref, side_ref, hg_ref, first_ref, second_ref):
    for e in range(2):
        xs = split_blocks(x_ref[e * ROWS : (e + 1) * ROWS, :DIM].astype(bf16))
        g = hg_ref[e, :, NF * HB : NF * HB + DB]
        for i in range(NF):
            first_ref[e, i] = dot_0(xs, hg_ref[e, :, i * HB : (i + 1) * HB]).astype(bf16)
            second_ref[e, i] = dot_0(g, side_ref[e, :, (NF + i) * HB : (NF + i + 1) * HB]).astype(bf16)


def combine_grad_body(parts_ref, w_ref, total_ref, grad_ref, cg_ref, cols_ref):
    out_b = sum_parts(parts_ref).astype(bf16)
    cg = dot_t(out_b, grad_ref[...])
    total = total_ref[...]
    cg_ref[:32] = cg
    cg_ref[32:] = jnp.broadcast_to(total, (8, TOK))
    cols = tile_of(jnp.sum(w_ref[:32] / total * cg, axis=0, keepdims=True))
    cols_ref[...] = jnp.broadcast_to(cols[None], cols_ref.shape)


def logit_body(p0, p1, p2, p3, cdots_ref, x_ref, w_ref, cg_ref, tok_ref, pay_ref, ug_ref, mix_ref):
    total = sum_ring(p0, p1, p2, p3)
    mix_ref[...] = total[:, DIM:]
    grad = total[:, :DIM]
    grad_b = grad.astype(bf16)
    ddot = jnp.sum(x_ref[:, :DIM] * grad, axis=1, keepdims=True)
    cdot = row_of(jnp.sum(cdots_ref[...], axis=0))
    tok = tok_ref[...]
    dg = dot_t(grad_b, tok)
    w = w_ref[:32]
    combine = w / cg_ref[32:33]
    dispatch = w / x_ref[:, DIM : DIM + 1]
    lg = combine * (cg_ref[:32] - cdot) + dispatch * (dg - ddot)
    lgb = (logit_gain * lg * w_ref[32:33]).astype(bf16)
    ug_ref[...] = dot(lgb, tok).astype(bf16)
    db = dispatch.astype(bf16)
    for k in range(STEPS):
        pay_ref[k, :, :DIM] = grad_b
        pay_ref[k, :, DIM : DIM + CHUNK] = lgb[:, chunk(k)]
        pay_ref[k, :, DIM + CHUNK :] = db[:, chunk(k)]


def token_body(place, recv_ref, s0, s1, s2, s3, tok_ref, keep_ref, send_ref):
    direct = None
    through = None
    for k, slot_ref in enumerate((s0, s1, s2, s3)):
        at = (place[0] + 4 - k) & 3
        unit_b = unit_rows(slot_ref[...].astype(f32)).astype(bf16)
        d = dot_0(recv_ref[at, :, DIM + CHUNK :], recv_ref[at, :, :DIM])
        u = dot_0(recv_ref[at, :, DIM : DIM + CHUNK], unit_b)
        direct = d if direct is None else direct + d
        through = u if through is None else through + u
    first = place[1] == 0
    for y in range(4):
        pair = []
        for c in range(2):
            lo = (y * 2 + c) * 32
            t = tok_ref[lo : lo + 32, :].astype(f32)
            u = through[lo : lo + 32]
            n2 = jnp.sum(t * t, axis=1, keepdims=True) + norm_eps
            coef = jnp.sum(t * u, axis=1, keepdims=True) / n2
            pair.append(direct[lo : lo + 32] + u - t * coef)
        keep_ref[y] = jnp.where(first, pair[0], pair[1])
        send_ref[y] = jnp.where(first, pair[1], pair[0]).astype(bf16)


def slot_body(p0, p1, p2, p3, slot_ref, out_ref):
    ug = sum_ring(p0, p1, p2, p3)
    values = slot_ref[...].astype(f32)
    norm = jnp.sqrt(jnp.sum(values * values, axis=1, keepdims=True) + norm_eps)
    unit = values / norm
    out_ref[...] = (ug - unit * jnp.sum(unit * ug, axis=1, keepdims=True)) / norm


def swap(value, axis):
    return lax.ppermute(value, axis, [(0, 1), (1, 0)])


def exchange(value, axes):
    return lax.all_to_all(value, axes, 0, 0)


def ring(value, axis):
    pairs = [[(i, (i + k) % 4) for i in range(4)] for k in range(1, 4)]
    return [value] + [lax.ppermute(value, axis, p) for p in pairs]


def far_sum(value):
    return (value.astype(f32) + swap(value, "h").astype(f32)).astype(bf16)


def gather_x(value):
    return exchange(jnp.broadcast_to(value[None], (4,) + value.shape), "x")


tie = lax.optimization_barrier


def local(tokens, out_grad, slot_params, m1, first_blocks, m2, second_blocks):
    second_turned = jnp.swapaxes(second_blocks, 2, 3)
    slot_all = ring(slot_params, "z")
    w, colsum, input_part = call(
        routing_body,
        (sds((40, TOK), f32), sds((32, 8, 128), f32), sds((32, DIM + EXTRA), bf16)),
        0,
        (slot_params, tokens),
        4 * 32 * TOK * DIM,
        4 << 20,
        "routing",
        True,
    )
    input_far = far_sum(input_part)
    col_parts = exchange(colsum, exp_axes)
    col_parts, input_far, *slot_all = tie((col_parts, input_far, *slot_all))
    total, grad_part = call(
        combine_body,
        (sds((1, TOK), f32), sds((32, DIM), bf16)),
        0,
        (col_parts, w, out_grad),
        2 * 32 * TOK * DIM,
        4 << 20,
        "combine",
    )
    input_parts = ring(input_far, "x")
    grad_far = far_sum(grad_part)
    *input_parts, grad_far = tie((*input_parts, grad_far))
    grad_parts = gather_x(grad_far)
    x, side, slopes, out_part = call(
        forward_body,
        (
            sds((32, DIM + EXTRA), f32),
            sds((2, 64, SIDE + HB), bf16),
            sds((2, 64, HB), f32),
            sds((32, DIM), bf16),
        ),
        2,
        (m1, m2, *input_parts, first_blocks, second_turned),
        4 * 128 * 1024 * DB,
        5 << 20,
        "forward",
    )
    out_far = far_sum(out_part)
    hg, input_grad_part = call(
        backward_body,
        (sds((2, 64, NF * HB + 512), bf16), sds((32, DIM + EXTRA), bf16)),
        2,
        (m1, m2, grad_parts, first_blocks, second_turned, side, slopes),
        4 * 128 * 1024 * DB,
        5 << 20,
        "backward",
    )
    out_parts = gather_x(out_far)
    input_grad_far = far_sum(input_grad_part)
    out_parts, input_grad_far = tie((out_parts, input_grad_far))
    input_grad_parts = ring(input_grad_far, "x")
    cg, cols = call(
        combine_grad_body,
        (sds((40, TOK), f32), sds((32, 8, 128), f32)),
        0,
        (out_parts, w, total, out_grad),
        2 * 32 * TOK * DIM,
        4 << 20,
        "combine_grad",
    )
    cdots = exchange(cols, exp_axes)
    pay, ug_part, mix = call(
        logit_body,
        (sds((4, 32, DIM + 512), bf16), sds((32, DIM), bf16), sds((32, EXTRA), f32)),
        0,
        (*input_grad_parts, cdots, x, w, cg, tokens),
        4 * 32 * TOK * DIM,
        4 << 20,
        "logit_grad",
    )
    first_grad, second_grad = call(
        weight_grad_body,
        (sds(first_blocks.shape, bf16), sds(second_turned.shape, bf16)),
        0,
        (x, side, hg),
        4 * 128 * 1024 * DB,
        5 << 20,
        "weight_grad",
    )
    recv = exchange(pay, "z")
    ug_far = far_sum(ug_part)
    recv, ug_far = tie((recv, ug_far))
    ug_parts = ring(ug_far, "x")
    quarter = lax.dynamic_slice_in_dim(tokens, lax.axis_index("z") * 256, 256, 0)
    place = jnp.stack([lax.axis_index("z"), lax.axis_index("c")]).astype(jnp.int32)
    keep, send = call(
        token_body,
        (sds((4, 32, DIM), f32), sds((4, 32, DIM), bf16)),
        1,
        (place, recv, *slot_all, quarter),
        4 * 128 * 256 * DIM,
        4 << 20,
        "token_grad",
    )
    half = (keep + swap(send, "c").astype(f32)).astype(bf16)
    grad_tokens = jnp.sum(exchange(half, "y").astype(f32), axis=0)
    grad_slots = call(
        slot_body, sds((32, DIM), f32), 0, (*ug_parts, slot_params), 32 * DIM * 8, 1 << 20, "slot_grad"
    )
    mixes = (mix[:, : 2 * NF] + mix[:, 2 * NF : 4 * NF]).reshape(2, NF, NF, 2, NF)
    return (
        grad_tokens,
        grad_slots,
        mixes[:, :, :, 0],
        first_grad,
        mixes[:, :, :, 1],
        jnp.swapaxes(second_grad, 2, 3),
    )


def solution(mesh):
    fine = Mesh(mesh.devices.reshape(2, 4, 4, 4, 2), seq_axes + exp_axes)
    return jax.shard_map(
        local,
        mesh=fine,
        in_specs=(
            P(seq_axes, None),
            P(seq_axes, None),
            P(exp_axes, None),
            P(exp_axes, None, None, None),
            P(exp_axes, None, None, seq_axes),
            P(exp_axes, None, None, None),
            P(exp_axes, None, seq_axes, None),
        ),
        out_specs=(
            P(seq_axes + exp_axes, None),
            P(exp_axes, None),
            P(exp_axes, None, None, None),
            P(exp_axes, None, None, seq_axes),
            P(exp_axes, None, None, None),
            P(exp_axes, None, seq_axes, None),
        ),
        check_vma=False,
    )
```

time: 185 us -> 156 us (0.84)
  local copies, waits for them, and re-layouts: 38.2 us -> 6.26 us
  blocking collectives: 12.6 us -> 0 us
  Pallas kernels: 20.9 us -> 31.7 us
  waiting for transfers between devices: 41.1 us -> 49.3 us
  other arithmetic: 8.33 us -> 2.76 us
  starting transfers between devices: 61.8 us -> 64.2 us
    unnamed x68 -> x12, local copies, waits for them, and re-layouts: 26.4 us -> 0.94 us
    all_to_all x9 -> x6, waiting for transfers between devices: 41.1 us -> 15.8 us  [exchange(): return lax.all_to_all(value, axes, 0, 0)]
    ppermute x0 -> x12, waiting for transfers between devices: none -> 18.4 us  [ring(): return [value] + [lax.ppermute(value, axis, p) for p in pairs]]
    ppermute x6, waiting for transfers between devices: 0.02 us -> 15.1 us  [swap(): return lax.ppermute(value, axis, [(0, 1), (1, 0)])]
    all_to_all x1 -> x0, blocking collectives: 12.6 us -> none  [spread(): lax.all_to_all(jnp.broadcast_to(value[None], (count,) + value.shape), axe...]
    ppermute x0 -> x12, starting transfers between devices: none -> 10.9 us  [ring(): return [value] + [lax.ppermute(value, axis, p) for p in pairs]]
    pallas_call x9, Pallas kernels: 20.9 us -> 31.7 us  [call(): pl.pallas_call(body, out_shape=out, in_specs=[pl.BlockSpec(memory_space=S...]
    all_to_all x9 -> x6, starting transfers between devices: 41.5 us -> 32.2 us  [exchange(): return lax.all_to_all(value, axes, 0, 0)]
  transfers between devices with their start and end apart: 15 -> 24, of which waited for: 8 -> 13; matrix products, arithmetic and copies ran while one was open for 10% -> 4% of each run, Pallas kernels for 9% -> 7%
where the time goes in v2:
time: 156 us; the launch traced here: 155 us
  starting transfers between devices  64.2 us (41%)
  waiting for transfers between devices  49.3 us (32%)
  Pallas kernels  31.7 us (20%)
  local copies, waits for them, and re-layouts  6.26 us (4%)
  other arithmetic  2.76 us (2%)
    all_to_all x6, starting transfers between devices, exchange(): return lax.all_to_all(value, axes, 0, 0)  32.2 us
    pallas_call x9, Pallas kernels, call(): pl.pallas_call(body, out_shape=out, in_specs=[pl.BlockSpec(memory_space=S...  31.7 us
    ppermute x6, starting transfers between devices, swap(): return lax.ppermute(value, axis, [(0, 1), (1, 0)])  21.1 us
    ppermute x12, waiting for transfers between devices, ring(): return [value] + [lax.ppermute(value, axis, p) for p in pairs]  18.4 us
    all_to_all x6, waiting for transfers between devices, exchange(): return lax.all_to_all(value, axes, 0, 0)  15.8 us
    ppermute x6, waiting for transfers between devices, swap(): return lax.ppermute(value, axis, [(0, 1), (1, 0)])  15.1 us
    ppermute x12, starting transfers between devices, ring(): return [value] + [lax.ppermute(value, axis, p) for p in pairs]  10.9 us
  transfers between devices with their start and end apart: 24, of which 13 were waited for; matrix products, arithmetic and copies ran while one was open for 4% of the time, Pallas kernels for 7%

profile of v2, /device:TPU:1, one launch (start us, length us, event | category | flops | bytes accessed | tf_op | source)
XLA Modules:
  0.0 155.0 jit_solution(375635823804471136)
XLA Ops:
  0.6 6.2 %routing.1 = (f32[40,1024]{1,0:T(8,128)}, f32[32,8,128]{2,1,0:T(8,128)}, bf16[32,1792]{1,0:T(8,128)(2,1)}) custom-call(bf16[32,1664]{1,0:T(8,128)(2,1)} %slot_ref.3, bf16[1024,1664]{1,0:T(8,128)(2,1)} %tok_ref.1), custom_call_target="tpu_custom_call" | custom-call | flops 218103808 | bytes 4194304 | tf_op jit(solution)/shard_map/routing/pallas_call | solution.py:51
  6.8 7.8 %collective-permute-start = (bf16[32,1792]{1,0:T(8,128)(2,1)}, bf16[32,1792]{1,0:T(8,128)(2,1)S(1)}, u32[]{:S(2)}, u32[]{:S(2)}) collective-permute-start(bf16[32,1792]{1,0:T(8,128)(2,1)} %get-tuple-element.42), channel_id=1, source_target_pairs={{0,128},{128,0},{1,129},{129,1},{2,130},{130,2},{3,131},{131,3},{4... | collective-permute-start | bytes 344072 | tf_op jit(solution)/shard_map/ppermute | solution.py:331
  14.7 1.6 %collective-permute-start.3 = (bf16[32,1664]{1,0:T(8,128)(2,1)S(1)}, bf16[32,1664]{1,0:T(8,128)(2,1)S(1)}, u32[]{:S(2)}, u32[]{:S(2)}) collective-permute-start(bf16[32,1664]{1,0:T(8,128)(2,1)S(1)} %copy-done.2), channel_id=1, source_target_pairs={{0,24},{8,0},{16,8},{24,16},{1,25},{9,1},{17,9},{25,17},{2,26},{10... | collective-permute-start | bytes 319496 | tf_op jit(solution)/shard_map/ppermute | solution.py:340
  17.3 8.7 %all-to-all-start = ((f32[32,8,128]{2,1,0:T(8,128)}), f32[32,8,128]{2,1,0:T(8,128)S(1)}, u32[]{:S(2)}, u32[]{:S(2)}) async-start(f32[32,8,128]{2,1,0:T(8,128)} %get-tuple-element.41), calls=%async_computation | async-start | bytes 262144 | tf_op jit(solution)/shard_map/all_to_all | solution.py:335
  26.9 3.6 %collective-permute-done.2.s2 = bf16[32,1664]{1,0:T(8,128)(2,1)S(1)} collective-permute-done((bf16[32,1664]{1,0:T(8,128)(2,1)S(1)}, bf16[32,1664]{1,0:T(8,128)(2,1)S(1)}, u32[]{:S(2)}, u32[]{:S(2)}) %collective-permute-start.2) | collective-permute-done | bytes 106528 | tf_op jit(solution)/shard_map/ppermute | solution.py:340
  30.5 5.1 %all-to-all-done.parts_ref = f32[32,8,128]{2,1,0:T(8,128)S(1)} async-done(((f32[32,8,128]{2,1,0:T(8,128)}), f32[32,8,128]{2,1,0:T(8,128)S(1)}, u32[]{:S(2)}, u32[]{:S(2)}) %all-to-all-start) | async-done | bytes 131104 | tf_op jit(solution)/shard_map/all_to_all | solution.py:335
  36.5 2.7 %combine.1 = (f32[1,1024]{1,0:T(1,128)S(1)}, bf16[32,1664]{1,0:T(8,128)(2,1)S(1)}) custom-call(f32[32,8,128]{2,1,0:T(8,128)S(1)} %all-to-all-done.parts_ref, f32[40,1024]{1,0:T(8,128)S(1)} %copy-done, bf16[1024,1664]{1,0:T(8,128)(2,1)} %grad_ref.3), custom_call_target="tpu_custom_call" | custom-call | flops 109051904 | bytes 4194304 | tf_op jit(solution)/shard_map/combine/pallas_call | solution.py:51
  40.7 2.5 %collective-permute-start.6 = (bf16[32,1792]{1,0:T(8,128)(2,1)S(1)}, bf16[32,1792]{1,0:T(8,128)(2,1)S(1)}, u32[]{:S(2)}, u32[]{:S(2)}) collective-permute-start(bf16[32,1792]{1,0:T(8,128)(2,1)S(1)} %add_convert_fusion.2.p0), channel_id=1, source_target_pairs={{0,96},{32,0},{64,32},{96,64},{1,97},{33,1},{65,33},{97,65},{2,98}... | collective-permute-start | bytes 344072 | tf_op jit(solution)/shard_map/ppermute | solution.py:340
  44.3 5.0 %collective-permute-done.7 = bf16[32,1664]{1,0:T(8,128)(2,1)S(1)} collective-permute-done((bf16[32,1664]{1,0:T(8,128)(2,1)S(1)}, bf16[32,1664]{1,0:T(8,128)(2,1)S(1)}, u32[]{:S(2)}, u32[]{:S(2)}) %collective-permute-start.7) | collective-permute-done | bytes 106528 | tf_op jit(solution)/shard_map/ppermute | solution.py:331
  49.4 2.3 %collective-permute-done.4.p1 = bf16[32,1792]{1,0:T(8,128)(2,1)S(1)} collective-permute-done((bf16[32,1792]{1,0:T(8,128)(2,1)S(1)}, bf16[32,1792]{1,0:T(8,128)(2,1)S(1)}, u32[]{:S(2)}, u32[]{:S(2)}) %collective-permute-start.4) | collective-permute-done | bytes 114720 | tf_op jit(solution)/shard_map/ppermute | solution.py:340
  52.5 3.5 %all-to-all-start.2 = ((bf16[4,32,1664]{2,1,0:T(8,128)(2,1)}), bf16[4,32,1664]{2,1,0:T(8,128)(2,1)S(1)}, u32[]{:S(2)}, u32[]{:S(2)}) async-start(bf16[4,32,1664]{2,1,0:T(8,128)(2,1)} %broadcast_in_dim.5), calls=%async_computation.2 | async-start | bytes 851968 | tf_op jit(solution)/shard_map/all_to_all | solution.py:335
  56.0 3.5 %forward.1 = (f32[32,1792]{1,0:T(8,128)S(1)}, bf16[2,64,2304]{2,1,0:T(8,128)(2,1)S(1)}, f32[2,64,256]{2,1,0:T(8,128)S(1)}, bf16[32,1664]{1,0:T(8,128)(2,1)S(1)}) custom-call(f32[2,4,4,4]{3,2,1,0:T(4,128)S(1)} %copy-done.3, f32[2,4,4,4]{3,2,1,0:T(4,128)S(1)} %copy-done.4, bf16[32,1792]{1,0:T(8,128)(2,1)S(1)} %add_convert_fusion.2.p0, ...), custom_call_target="tpu_custom_call" | custom-call | flops 218103808 | bytes 5242880 | tf_op jit(solution)/shard_map/forward/pallas_call | solution.py:51
  59.5 4.2 %collective-permute-start.8 = (bf16[32,1664]{1,0:T(8,128)(2,1)S(1)}, bf16[32,1664]{1,0:T(8,128)(2,1)S(1)}, u32[]{:S(2)}, u32[]{:S(2)}) collective-permute-start(bf16[32,1664]{1,0:T(8,128)(2,1)S(1)} %get-tuple-element.51), channel_id=1, source_target_pairs={{0,128},{128,0},{1,129},{129,1},{2,130},{130,2},{3,131},{131,3},{4... | collective-permute-start | bytes 319496 | tf_op jit(solution)/shard_map/ppermute | solution.py:331
  63.7 3.4 %backward.1 = (bf16[2,64,1536]{2,1,0:T(8,128)(2,1)S(1)}, bf16[32,1792]{1,0:T(8,128)(2,1)S(1)}) custom-call(f32[2,4,4,4]{3,2,1,0:T(4,128)S(1)} %copy-done.3, f32[2,4,4,4]{3,2,1,0:T(4,128)S(1)} %copy-done.4, bf16[4,32,1664]{2,1,0:T(8,128)(2,1)S(1)} %all-to-all-done.2.parts_ref, bf16[2,4,416,256]{3,2,1,0:T(8,128)(2,1)} %first_ref.3, ...), custom_call_target="tpu_custom_call" | custom-call | flops 218103808 | bytes 5242880 | tf_op jit(solution)/shard_map/backward/pallas_call | solution.py:51
  67.1 3.8 %collective-permute-start.9 = (bf16[32,1792]{1,0:T(8,128)(2,1)S(1)}, bf16[32,1792]{1,0:T(8,128)(2,1)S(1)}, u32[]{:S(2)}, u32[]{:S(2)}) collective-permute-start(bf16[32,1792]{1,0:T(8,128)(2,1)S(1)} %get-tuple-element.55), channel_id=1, source_target_pairs={{0,128},{128,0},{1,129},{129,1},{2,130},{130,2},{3,131},{131,3},{4... | collective-permute-start | bytes 344072 | tf_op jit(solution)/shard_map/ppermute | solution.py:331
  71.7 3.6 %all-to-all-start.1 = ((bf16[4,32,1664]{2,1,0:T(8,128)(2,1)}), bf16[4,32,1664]{2,1,0:T(8,128)(2,1)S(1)}, u32[]{:S(2)}, u32[]{:S(2)}) async-start(bf16[4,32,1664]{2,1,0:T(8,128)(2,1)} %broadcast_in_dim.4), calls=%async_computation.1 | async-start | bytes 851968 | tf_op jit(solution)/shard_map/all_to_all | solution.py:335
  75.4 6.1 %all-to-all-done.1.parts_ref = bf16[4,32,1664]{2,1,0:T(8,128)(2,1)S(1)} async-done(((bf16[4,32,1664]{2,1,0:T(8,128)(2,1)}), bf16[4,32,1664]{2,1,0:T(8,128)(2,1)S(1)}, u32[]{:S(2)}, u32[]{:S(2)}) %all-to-all-start.1) | async-done | bytes 426016 | tf_op jit(solution)/shard_map/all_to_all | solution.py:335
  81.6 3.7 %combine_grad.1 = (f32[40,1024]{1,0:T(8,128)S(1)}, f32[32,8,128]{2,1,0:T(8,128)}) custom-call(bf16[4,32,1664]{2,1,0:T(8,128)(2,1)S(1)} %all-to-all-done.1.parts_ref, f32[40,1024]{1,0:T(8,128)S(1)} %copy-done.1, f32[1,1024]{1,0:T(1,128)S(1)} %get-tuple-element.58.total_ref, bf16[1024,1664]{1,0:T(8,128)(2,1)} %grad_ref.3), custom_call_target="tpu_custom_call" | custom-call | flops 109051904 | bytes 4194304 | tf_op jit(solution)/shard_map/combine_grad/pallas_call | solution.py:51
  85.3 8.1 %all-to-all-start.3 = ((f32[32,8,128]{2,1,0:T(8,128)}), f32[32,8,128]{2,1,0:T(8,128)S(1)}, u32[]{:S(2)}, u32[]{:S(2)}) async-start(f32[32,8,128]{2,1,0:T(8,128)} %get-tuple-element.59), calls=%async_computation.3 | async-start | bytes 262144 | tf_op jit(solution)/shard_map/all_to_all | solution.py:335
  95.6 2.4 %collective-permute-done.12.p3 = bf16[32,1792]{1,0:T(8,128)(2,1)S(1)} collective-permute-done((bf16[32,1792]{1,0:T(8,128)(2,1)S(1)}, bf16[32,1792]{1,0:T(8,128)(2,1)S(1)}, u32[]{:S(2)}, u32[]{:S(2)}) %collective-permute-start.12) | collective-permute-done | bytes 114720 | tf_op jit(solution)/shard_map/ppermute | solution.py:340
  98.0 2.1 %collective-permute-done.11.p2 = bf16[32,1792]{1,0:T(8,128)(2,1)S(1)} collective-permute-done((bf16[32,1792]{1,0:T(8,128)(2,1)S(1)}, bf16[32,1792]{1,0:T(8,128)(2,1)S(1)}, u32[]{:S(2)}, u32[]{:S(2)}) %collective-permute-start.11) | collective-permute-done | bytes 114720 | tf_op jit(solution)/shard_map/ppermute | solution.py:340
  100.1 3.1 %collective-permute-done.10.p1 = bf16[32,1792]{1,0:T(8,128)(2,1)S(1)} collective-permute-done((bf16[32,1792]{1,0:T(8,128)(2,1)S(1)}, bf16[32,1792]{1,0:T(8,128)(2,1)S(1)}, u32[]{:S(2)}, u32[]{:S(2)}) %collective-permute-start.10) | collective-permute-done | bytes 114720 | tf_op jit(solution)/shard_map/ppermute | solution.py:340
  103.2 3.9 %logit_grad.1 = (bf16[4,32,2176]{2,1,0:T(8,128)(2,1)}, bf16[32,1664]{1,0:T(8,128)(2,1)S(1)}, f32[32,128]{1,0:T(8,128)S(1)}) custom-call(bf16[32,1792]{1,0:T(8,128)(2,1)S(1)} %add_convert_fusion.1.p0, bf16[32,1792]{1,0:T(8,128)(2,1)S(1)} %collective-permute-done.10.p1, bf16[32,1792]{1,0:T(8,128)(2,1)S(1)} %collective-permute-done.11.p2, ...), custom_call_target="tpu_custom_call" | custom-call | flops 218103808 | bytes 4194304 | tf_op jit(solution)/shard_map/logit_grad/pallas_call | solution.py:51
  107.1 4.3 %all-to-all-start.4 = ((bf16[4,32,2176]{2,1,0:T(8,128)(2,1)}), bf16[4,32,2176]{2,1,0:T(8,128)(2,1)S(1)}, u32[]{:S(2)}, u32[]{:S(2)}) async-start(bf16[4,32,2176]{2,1,0:T(8,128)(2,1)} %get-tuple-element.62), calls=%async_computation.4 | async-start | bytes 1114112 | tf_op jit(solution)/shard_map/all_to_all | solution.py:335
  111.4 2.1 %constant_dynamic-slice_fusion.tok_ref = bf16[256,1664]{1,0:T(8,128)(2,1)} fusion(bf16[1024,1664]{1,0:T(8,128)(2,1)} %tok_ref.1, s32[]{:T(128)S(6)} %select_n.3), kind=kLoop, calls=%fused_computation.9 | loop fusion | bytes 1703940 | tf_op jit(solution)/shard_map/dynamic_slice | solution.py:443
  113.6 2.4 %collective-permute-start.13 = (bf16[32,1664]{1,0:T(8,128)(2,1)S(1)}, bf16[32,1664]{1,0:T(8,128)(2,1)S(1)}, u32[]{:S(2)}, u32[]{:S(2)}) collective-permute-start(bf16[32,1664]{1,0:T(8,128)(2,1)S(1)} %get-tuple-element.63), channel_id=1, source_target_pairs={{0,128},{128,0},{1,129},{129,1},{2,130},{130,2},{3,131},{131,3},{4... | collective-permute-start | bytes 319496 | tf_op jit(solution)/shard_map/ppermute | solution.py:331
  116.0 10.1 %collective-permute-done.13 = bf16[32,1664]{1,0:T(8,128)(2,1)S(1)} collective-permute-done((bf16[32,1664]{1,0:T(8,128)(2,1)S(1)}, bf16[32,1664]{1,0:T(8,128)(2,1)S(1)}, u32[]{:S(2)}, u32[]{:S(2)}) %collective-permute-start.13) | collective-permute-done | bytes 106528 | tf_op jit(solution)/shard_map/ppermute | solution.py:331
  126.1 4.6 %all-to-all-done.4.recv_ref = bf16[4,32,2176]{2,1,0:T(8,128)(2,1)S(1)} async-done(((bf16[4,32,2176]{2,1,0:T(8,128)(2,1)}), bf16[4,32,2176]{2,1,0:T(8,128)(2,1)S(1)}, u32[]{:S(2)}, u32[]{:S(2)}) %all-to-all-start.4) | async-done | bytes 557088 | tf_op jit(solution)/shard_map/all_to_all | solution.py:335
  130.7 4.5 %token_grad.1 = (f32[4,32,1664]{2,1,0:T(8,128)}, bf16[4,32,1664]{2,1,0:T(8,128)(2,1)S(1)}) custom-call(s32[2]{0:T(128)S(1)} %pad_add_fusion.place, bf16[4,32,2176]{2,1,0:T(8,128)(2,1)S(1)} %all-to-all-done.4.recv_ref, bf16[32,1664]{1,0:T(8,128)(2,1)S(1)} %copy-done.2, bf16[32,1664]{1,0:T(8,128)(2,1)S(1)} %collective-permute-done.1.s1, ...), custom_call_target="tpu_custom_call" | custom-call | flops 218103808 | bytes 4194304 | tf_op jit(solution)/shard_map/token_grad/pallas_call | solution.py:51
  136.6 2.9 %weight_grad.1 = (bf16[2,4,416,256]{3,2,1,0:T(8,128)(2,1)}, bf16[2,4,416,256]{3,2,1,0:T(8,128)(2,1)}) custom-call(f32[32,1792]{1,0:T(8,128)S(1)} %get-tuple-element.60.x_ref, bf16[2,64,2304]{2,1,0:T(8,128)(2,1)S(1)} %get-tuple-element.53.side_ref, bf16[2,64,1536]{2,1,0:T(8,128)(2,1)S(1)} %get-tuple-element.73.hg_ref), custom_call_target="tpu_custom_call" | custom-call | flops 218103808 | bytes 5242880 | tf_op jit(solution)/shard_map/weight_grad/pallas_call | solution.py:51
  140.3 4.0 %all-to-all-start.5 = ((bf16[4,32,1664]{2,1,0:T(8,128)(2,1)}), bf16[4,32,1664]{2,1,0:T(8,128)(2,1)S(1)}, u32[]{:S(2)}, u32[]{:S(2)}) async-start(bf16[4,32,1664]{2,1,0:T(8,128)(2,1)} %add_convert_fusion), calls=%async_computation.5 | async-start | bytes 851968 | tf_op jit(solution)/shard_map/all_to_all | solution.py:335
  150.5 2.9 %collective-permute-done.15.p1 = bf16[32,1664]{1,0:T(8,128)(2,1)S(1)} collective-permute-done((bf16[32,1664]{1,0:T(8,128)(2,1)S(1)}, bf16[32,1664]{1,0:T(8,128)(2,1)S(1)}, u32[]{:S(2)}, u32[]{:S(2)}) %collective-permute-start.15) | collective-permute-done | bytes 106528 | tf_op jit(solution)/shard_map/ppermute | solution.py:340
  (54 shorter events, 19.6 us)
Async XLA Ops:
  0.6 14.0 %copy-start.2 = (bf16[32,1664]{1,0:T(8,128)(2,1)S(1)}, bf16[32,1664]{1,0:T(8,128)(2,1)}, u32[]{:S(2)}) copy-start(bf16[32,1664]{1,0:T(8,128)(2,1)} %slot_ref.3) | copy-start | bytes 319492
  6.8 19.2 %collective-permute-start = (bf16[32,1792]{1,0:T(8,128)(2,1)}, bf16[32,1792]{1,0:T(8,128)(2,1)S(1)}, u32[]{:S(2)}, u32[]{:S(2)}) collective-permute-start(bf16[32,1792]{1,0:T(8,128)(2,1)} %get-tuple-element.42), channel_id=1, source_target_pairs={{0,128},{128,0},{1,129},{129,1},{2,130},{130,2},{3,131},{131,3},{4... | collective-permute-start | bytes 344072 | tf_op jit(solution)/shard_map/ppermute | solution.py:331
  14.7 12.3 %collective-permute-start.3 = (bf16[32,1664]{1,0:T(8,128)(2,1)S(1)}, bf16[32,1664]{1,0:T(8,128)(2,1)S(1)}, u32[]{:S(2)}, u32[]{:S(2)}) collective-permute-start(bf16[32,1664]{1,0:T(8,128)(2,1)S(1)} %copy-done.2), channel_id=1, source_target_pairs={{0,24},{8,0},{16,8},{24,16},{1,25},{9,1},{17,9},{25,17},{2,26},{10... | collective-permute-start | bytes 319496 | tf_op jit(solution)/shard_map/ppermute | solution.py:340
  16.3 14.2 %collective-permute-start.2 = (bf16[32,1664]{1,0:T(8,128)(2,1)S(1)}, bf16[32,1664]{1,0:T(8,128)(2,1)S(1)}, u32[]{:S(2)}, u32[]{:S(2)}) collective-permute-start(bf16[32,1664]{1,0:T(8,128)(2,1)S(1)} %copy-done.2), channel_id=1, source_target_pairs={{0,16},{8,24},{16,0},{24,8},{1,17},{9,25},{17,1},{25,9},{2,18},{10... | collective-permute-start | bytes 319496 | tf_op jit(solution)/shard_map/ppermute | solution.py:340
  16.6 14.0 %collective-permute-start.1 = (bf16[32,1664]{1,0:T(8,128)(2,1)S(1)}, bf16[32,1664]{1,0:T(8,128)(2,1)S(1)}, u32[]{:S(2)}, u32[]{:S(2)}) collective-permute-start(bf16[32,1664]{1,0:T(8,128)(2,1)S(1)} %copy-done.2), channel_id=1, source_target_pairs={{0,8},{8,16},{16,24},{24,0},{1,9},{9,17},{17,25},{25,1},{2,10},{10... | collective-permute-start | bytes 319496 | tf_op jit(solution)/shard_map/ppermute | solution.py:340
  17.3 18.3 %all-to-all-start = ((f32[32,8,128]{2,1,0:T(8,128)}), f32[32,8,128]{2,1,0:T(8,128)S(1)}, u32[]{:S(2)}, u32[]{:S(2)}) async-start(f32[32,8,128]{2,1,0:T(8,128)} %get-tuple-element.41), calls=%async_computation | async-start | bytes 262144 | tf_op jit(solution)/shard_map/all_to_all | solution.py:335
  35.6 0.9 copy-start
  39.2 16.8 %copy-start.3 = (f32[2,4,4,4]{3,2,1,0:T(4,128)S(1)}, f32[2,4,4,4]{3,2,1,0:T(4,128)}, u32[]{:S(2)}) copy-start(f32[2,4,4,4]{3,2,1,0:T(4,128)} %m1.3) | copy-start | bytes 1540
  39.2 16.8 %copy-start.4 = (f32[2,4,4,4]{3,2,1,0:T(4,128)S(1)}, f32[2,4,4,4]{3,2,1,0:T(4,128)}, u32[]{:S(2)}) copy-start(f32[2,4,4,4]{3,2,1,0:T(4,128)} %m2.3) | copy-start | bytes 1540
  39.2 10.1 %collective-permute-start.7 = (bf16[32,1664]{1,0:T(8,128)(2,1)S(1)}, bf16[32,1664]{1,0:T(8,128)(2,1)S(1)}, u32[]{:S(2)}, u32[]{:S(2)}) collective-permute-start(bf16[32,1664]{1,0:T(8,128)(2,1)S(1)} %get-tuple-element.46), channel_id=1, source_target_pairs={{0,128},{128,0},{1,129},{129,1},{2,130},{130,2},{3,131},{131,3},{4... | collective-permute-start | bytes 319496 | tf_op jit(solution)/shard_map/ppermute | solution.py:331
  40.7 8.7 %collective-permute-start.6 = (bf16[32,1792]{1,0:T(8,128)(2,1)S(1)}, bf16[32,1792]{1,0:T(8,128)(2,1)S(1)}, u32[]{:S(2)}, u32[]{:S(2)}) collective-permute-start(bf16[32,1792]{1,0:T(8,128)(2,1)S(1)} %add_convert_fusion.2.p0), channel_id=1, source_target_pairs={{0,96},{32,0},{64,32},{96,64},{1,97},{33,1},{65,33},{97,65},{2,98}... | collective-permute-start | bytes 344072 | tf_op jit(solution)/shard_map/ppermute | solution.py:340
  43.2 6.2 %collective-permute-start.5 = (bf16[32,1792]{1,0:T(8,128)(2,1)S(1)}, bf16[32,1792]{1,0:T(8,128)(2,1)S(1)}, u32[]{:S(2)}, u32[]{:S(2)}) collective-permute-start(bf16[32,1792]{1,0:T(8,128)(2,1)S(1)} %add_convert_fusion.2.p0), channel_id=1, source_target_pairs={{0,64},{32,96},{64,0},{96,32},{1,65},{33,97},{65,1},{97,33},{2,66}... | collective-permute-start | bytes 344072 | tf_op jit(solution)/shard_map/ppermute | solution.py:340
  43.7 8.0 %collective-permute-start.4 = (bf16[32,1792]{1,0:T(8,128)(2,1)S(1)}, bf16[32,1792]{1,0:T(8,128)(2,1)S(1)}, u32[]{:S(2)}, u32[]{:S(2)}) collective-permute-start(bf16[32,1792]{1,0:T(8,128)(2,1)S(1)} %add_convert_fusion.2.p0), channel_id=1, source_target_pairs={{0,32},{32,64},{64,96},{96,0},{1,33},{33,65},{65,97},{97,1},{2,34}... | collective-permute-start | bytes 344072 | tf_op jit(solution)/shard_map/ppermute | solution.py:340
  52.5 11.2 %all-to-all-start.2 = ((bf16[4,32,1664]{2,1,0:T(8,128)(2,1)}), bf16[4,32,1664]{2,1,0:T(8,128)(2,1)S(1)}, u32[]{:S(2)}, u32[]{:S(2)}) async-start(bf16[4,32,1664]{2,1,0:T(8,128)(2,1)} %broadcast_in_dim.5), calls=%async_computation.2 | async-start | bytes 851968 | tf_op jit(solution)/shard_map/all_to_all | solution.py:335
  59.5 11.4 %collective-permute-start.8 = (bf16[32,1664]{1,0:T(8,128)(2,1)S(1)}, bf16[32,1664]{1,0:T(8,128)(2,1)S(1)}, u32[]{:S(2)}, u32[]{:S(2)}) collective-permute-start(bf16[32,1664]{1,0:T(8,128)(2,1)S(1)} %get-tuple-element.51), channel_id=1, source_target_pairs={{0,128},{128,0},{1,129},{129,1},{2,130},{130,2},{3,131},{131,3},{4... | collective-permute-start | bytes 319496 | tf_op jit(solution)/shard_map/ppermute | solution.py:331
  67.1 14.5 %copy-start.1 = (f32[40,1024]{1,0:T(8,128)S(1)}, f32[40,1024]{1,0:T(8,128)}, u32[]{:S(2)}) copy-start(f32[40,1024]{1,0:T(8,128)} %get-tuple-element.45.w_ref) | copy-start | bytes 491524
  67.1 8.3 %collective-permute-start.9 = (bf16[32,1792]{1,0:T(8,128)(2,1)S(1)}, bf16[32,1792]{1,0:T(8,128)(2,1)S(1)}, u32[]{:S(2)}, u32[]{:S(2)}) collective-permute-start(bf16[32,1792]{1,0:T(8,128)(2,1)S(1)} %get-tuple-element.55), channel_id=1, source_target_pairs={{0,128},{128,0},{1,129},{129,1},{2,130},{130,2},{3,131},{131,3},{4... | collective-permute-start | bytes 344072 | tf_op jit(solution)/shard_map/ppermute | solution.py:331
  71.7 9.8 %all-to-all-start.1 = ((bf16[4,32,1664]{2,1,0:T(8,128)(2,1)}), bf16[4,32,1664]{2,1,0:T(8,128)(2,1)S(1)}, u32[]{:S(2)}, u32[]{:S(2)}) async-start(bf16[4,32,1664]{2,1,0:T(8,128)(2,1)} %broadcast_in_dim.4), calls=%async_computation.1 | async-start | bytes 851968 | tf_op jit(solution)/shard_map/all_to_all | solution.py:335
  85.3 17.9 %all-to-all-start.3 = ((f32[32,8,128]{2,1,0:T(8,128)}), f32[32,8,128]{2,1,0:T(8,128)S(1)}, u32[]{:S(2)}, u32[]{:S(2)}) async-start(f32[32,8,128]{2,1,0:T(8,128)} %get-tuple-element.59), calls=%async_computation.3 | async-start | bytes 262144 | tf_op jit(solution)/shard_map/all_to_all | solution.py:335
  93.4 4.6 %collective-permute-start.12 = (bf16[32,1792]{1,0:T(8,128)(2,1)S(1)}, bf16[32,1792]{1,0:T(8,128)(2,1)S(1)}, u32[]{:S(2)}, u32[]{:S(2)}) collective-permute-start(bf16[32,1792]{1,0:T(8,128)(2,1)S(1)} %add_convert_fusion.1.p0), channel_id=1, source_target_pairs={{0,96},{32,0},{64,32},{96,64},{1,97},{33,1},{65,33},{97,65},{2,98}... | collective-permute-start | bytes 344072 | tf_op jit(solution)/shard_map/ppermute | solution.py:340
  94.4 5.7 %collective-permute-start.11 = (bf16[32,1792]{1,0:T(8,128)(2,1)S(1)}, bf16[32,1792]{1,0:T(8,128)(2,1)S(1)}, u32[]{:S(2)}, u32[]{:S(2)}) collective-permute-start(bf16[32,1792]{1,0:T(8,128)(2,1)S(1)} %add_convert_fusion.1.p0), channel_id=1, source_target_pairs={{0,64},{32,96},{64,0},{96,32},{1,65},{33,97},{65,1},{97,33},{2,66}... | collective-permute-start | bytes 344072 | tf_op jit(solution)/shard_map/ppermute | solution.py:340
  95.6 7.6 %collective-permute-start.10 = (bf16[32,1792]{1,0:T(8,128)(2,1)S(1)}, bf16[32,1792]{1,0:T(8,128)(2,1)S(1)}, u32[]{:S(2)}, u32[]{:S(2)}) collective-permute-start(bf16[32,1792]{1,0:T(8,128)(2,1)S(1)} %add_convert_fusion.1.p0), channel_id=1, source_target_pairs={{0,32},{32,64},{64,96},{96,0},{1,33},{33,65},{65,97},{97,1},{2,34}... | collective-permute-start | bytes 344072 | tf_op jit(solution)/shard_map/ppermute | solution.py:340
  107.1 23.6 %all-to-all-start.4 = ((bf16[4,32,2176]{2,1,0:T(8,128)(2,1)}), bf16[4,32,2176]{2,1,0:T(8,128)(2,1)S(1)}, u32[]{:S(2)}, u32[]{:S(2)}) async-start(bf16[4,32,2176]{2,1,0:T(8,128)(2,1)} %get-tuple-element.62), calls=%async_computation.4 | async-start | bytes 1114112 | tf_op jit(solution)/shard_map/all_to_all | solution.py:335
  113.6 12.5 %collective-permute-start.13 = (bf16[32,1664]{1,0:T(8,128)(2,1)S(1)}, bf16[32,1664]{1,0:T(8,128)(2,1)S(1)}, u32[]{:S(2)}, u32[]{:S(2)}) collective-permute-start(bf16[32,1664]{1,0:T(8,128)(2,1)S(1)} %get-tuple-element.63), channel_id=1, source_target_pairs={{0,128},{128,0},{1,129},{129,1},{2,130},{130,2},{3,131},{131,3},{4... | collective-permute-start | bytes 319496 | tf_op jit(solution)/shard_map/ppermute | solution.py:331
  135.2 4.3 %copy-start.5 = (f32[4,32,1664]{2,1,0:T(8,128)S(1)}, f32[4,32,1664]{2,1,0:T(8,128)}, u32[]{:S(2)}) copy-start(f32[4,32,1664]{2,1,0:T(8,128)} %get-tuple-element.69) | copy-start | bytes 2555908
  135.2 4.3 %collective-permute-start.14 = (bf16[4,32,1664]{2,1,0:T(8,128)(2,1)S(1)}, bf16[4,32,1664]{2,1,0:T(8,128)(2,1)S(1)}, u32[]{:S(2)}, u32[]{:S(2)}) collective-permute-start(bf16[4,32,1664]{2,1,0:T(8,128)(2,1)S(1)} %get-tuple-element.70), channel_id=1, source_target_pairs={{0,1},{1,0},{2,3},{3,2},{4,5},{5,4},{6,7},{7,6},{8,9},{9,8},{10,11... | collective-permute-start | bytes 1277960 | tf_op jit(solution)/shard_map/ppermute | solution.py:331
  140.3 14.0 %all-to-all-start.5 = ((bf16[4,32,1664]{2,1,0:T(8,128)(2,1)}), bf16[4,32,1664]{2,1,0:T(8,128)(2,1)S(1)}, u32[]{:S(2)}, u32[]{:S(2)}) async-start(bf16[4,32,1664]{2,1,0:T(8,128)(2,1)} %add_convert_fusion), calls=%async_computation.5 | async-start | bytes 851968 | tf_op jit(solution)/shard_map/all_to_all | solution.py:335
  144.6 4.4 %collective-permute-start.17 = (bf16[32,1664]{1,0:T(8,128)(2,1)S(1)}, bf16[32,1664]{1,0:T(8,128)(2,1)S(1)}, u32[]{:S(2)}, u32[]{:S(2)}) collective-permute-start(bf16[32,1664]{1,0:T(8,128)(2,1)S(1)} %add_convert_fusion.3.p0), channel_id=1, source_target_pairs={{0,96},{32,0},{64,32},{96,64},{1,97},{33,1},{65,33},{97,65},{2,98}... | collective-permute-start | bytes 319496 | tf_op jit(solution)/shard_map/ppermute | solution.py:340
  144.7 5.9 %collective-permute-start.16 = (bf16[32,1664]{1,0:T(8,128)(2,1)S(1)}, bf16[32,1664]{1,0:T(8,128)(2,1)S(1)}, u32[]{:S(2)}, u32[]{:S(2)}) collective-permute-start(bf16[32,1664]{1,0:T(8,128)(2,1)S(1)} %add_convert_fusion.3.p0), channel_id=1, source_target_pairs={{0,64},{32,96},{64,0},{96,32},{1,65},{33,97},{65,1},{97,33},{2,66}... | collective-permute-start | bytes 319496 | tf_op jit(solution)/shard_map/ppermute | solution.py:340
  146.3 7.1 %collective-permute-start.15 = (bf16[32,1664]{1,0:T(8,128)(2,1)S(1)}, bf16[32,1664]{1,0:T(8,128)(2,1)S(1)}, u32[]{:S(2)}, u32[]{:S(2)}) collective-permute-start(bf16[32,1664]{1,0:T(8,128)(2,1)S(1)} %add_convert_fusion.3.p0), channel_id=1, source_target_pairs={{0,32},{32,64},{64,96},{96,0},{1,33},{33,65},{65,97},{97,1},{2,34}... | collective-permute-start | bytes 319496 | tf_op jit(solution)/shard_map/ppermute | solution.py:340

commit v3 on v2

--- a/solution.py
+++ b/solution.py
@@ -22,7 +22,7 @@
 CHUNK = 256
 STEPS = TOK // CHUNK
 WIDE = 60 << 20
-SMALL = 52 << 20
+SMALL = 51 << 20
 SIDE = 2 * NF * HB
 VMEM = pltpu.VMEM
 SMEM = pltpu.SMEM
@@ -319,8 +319,8 @@
         send_ref[y] = jnp.where(first, pair[1], pair[0]).astype(bf16)
 
 
-def slot_body(p0, p1, p2, p3, slot_ref, out_ref):
-    ug = sum_ring(p0, p1, p2, p3)
+def slot_body(p0, p1, slot_ref, out_ref):
+    ug = p0[...].astype(f32) + p1[...].astype(f32)
     values = slot_ref[...].astype(f32)
     norm = jnp.sqrt(jnp.sum(values * values, axis=1, keepdims=True) + norm_eps)
     unit = values / norm
@@ -437,9 +437,10 @@
         "weight_grad",
     )
     recv = exchange(pay, "z")
-    ug_far = far_sum(ug_part)
-    recv, ug_far = tie((recv, ug_far))
-    ug_parts = ring(ug_far, "x")
+    u0, u1, u2, u3 = (u.astype(f32) for u in ring(ug_part, "x"))
+    ug_near = ((u0 + u2) + (u1 + u3)).astype(bf16)
+    recv, ug_near = tie((recv, ug_near))
+    ug_parts = (ug_near, swap(ug_near, "h"))
     quarter = lax.dynamic_slice_in_dim(tokens, lax.axis_index("z") * 256, 256, 0)
     place = jnp.stack([lax.axis_index("z"), lax.axis_index("c")]).astype(jnp.int32)
     keep, send = call(

time: 156 us -> 152 us (0.974)
  waiting for transfers between devices: 49.3 us -> 45.9 us
    ppermute x6, waiting for transfers between devices: 15.1 us -> 11.7 us  [swap(): return lax.ppermute(value, axis, [(0, 1), (1, 0)])]
where the time goes in v3:
time: 152 us; the launch traced here: 151 us
  starting transfers between devices  64.9 us (43%)
  waiting for transfers between devices  45.9 us (30%)
  Pallas kernels  30.8 us (20%)
  local copies, waits for them, and re-layouts  6.26 us (4%)
  other arithmetic  2.79 us (2%)
    all_to_all x6, starting transfers between devices, exchange(): return lax.all_to_all(value, axes, 0, 0)  32.2 us
    pallas_call x9, Pallas kernels, call(): pl.pallas_call(body, out_shape=out, in_specs=[pl.BlockSpec(memory_space=S...  30.8 us
    ppermute x6, starting transfers between devices, swap(): return lax.ppermute(value, axis, [(0, 1), (1, 0)])  21.3 us
    ppermute x12, waiting for transfers between devices, ring(): return [value] + [lax.ppermute(value, axis, p) for p in pairs]  18 us
    all_to_all x6, waiting for transfers between devices, exchange(): return lax.all_to_all(value, axes, 0, 0)  16.2 us
    ppermute x6, waiting for transfers between devices, swap(): return lax.ppermute(value, axis, [(0, 1), (1, 0)])  11.7 us
    ppermute x12, starting transfers between devices, ring(): return [value] + [lax.ppermute(value, axis, p) for p in pairs]  11.4 us
  transfers between devices with their start and end apart: 24, of which 13 were waited for; matrix products, arithmetic and copies ran while one was open for 4% of the time, Pallas kernels for 7%

profile of v3, /device:TPU:1, one launch (start us, length us, event | category | flops | bytes accessed | tf_op | source)
XLA Modules:
  0.0 151.4 jit_solution(11518843376186101481)
XLA Ops:
  0.6 6.2 %routing.1 = (f32[40,1024]{1,0:T(8,128)}, f32[32,8,128]{2,1,0:T(8,128)}, bf16[32,1792]{1,0:T(8,128)(2,1)}) custom-call(bf16[32,1664]{1,0:T(8,128)(2,1)} %slot_ref.3, bf16[1024,1664]{1,0:T(8,128)(2,1)} %tok_ref.1), custom_call_target="tpu_custom_call" | custom-call | flops 218103808 | bytes 4194304 | tf_op jit(solution)/shard_map/routing/pallas_call | solution.py:51
  6.8 7.8 %collective-permute-start = (bf16[32,1792]{1,0:T(8,128)(2,1)}, bf16[32,1792]{1,0:T(8,128)(2,1)S(1)}, u32[]{:S(2)}, u32[]{:S(2)}) collective-permute-start(bf16[32,1792]{1,0:T(8,128)(2,1)} %get-tuple-element.42), channel_id=1, source_target_pairs={{0,128},{128,0},{1,129},{129,1},{2,130},{130,2},{3,131},{131,3},{4... | collective-permute-start | bytes 344072 | tf_op jit(solution)/shard_map/ppermute | solution.py:331
  14.7 1.6 %collective-permute-start.3 = (bf16[32,1664]{1,0:T(8,128)(2,1)S(1)}, bf16[32,1664]{1,0:T(8,128)(2,1)S(1)}, u32[]{:S(2)}, u32[]{:S(2)}) collective-permute-start(bf16[32,1664]{1,0:T(8,128)(2,1)S(1)} %copy-done.2), channel_id=1, source_target_pairs={{0,24},{8,0},{16,8},{24,16},{1,25},{9,1},{17,9},{25,17},{2,26},{10... | collective-permute-start | bytes 319496 | tf_op jit(solution)/shard_map/ppermute | solution.py:340
  17.3 8.7 %all-to-all-start = ((f32[32,8,128]{2,1,0:T(8,128)}), f32[32,8,128]{2,1,0:T(8,128)S(1)}, u32[]{:S(2)}, u32[]{:S(2)}) async-start(f32[32,8,128]{2,1,0:T(8,128)} %get-tuple-element.41), calls=%async_computation | async-start | bytes 262144 | tf_op jit(solution)/shard_map/all_to_all | solution.py:335
  26.9 3.6 %collective-permute-done.2.s2 = bf16[32,1664]{1,0:T(8,128)(2,1)S(1)} collective-permute-done((bf16[32,1664]{1,0:T(8,128)(2,1)S(1)}, bf16[32,1664]{1,0:T(8,128)(2,1)S(1)}, u32[]{:S(2)}, u32[]{:S(2)}) %collective-permute-start.2) | collective-permute-done | bytes 106528 | tf_op jit(solution)/shard_map/ppermute | solution.py:340
  30.5 5.1 %all-to-all-done.parts_ref = f32[32,8,128]{2,1,0:T(8,128)S(1)} async-done(((f32[32,8,128]{2,1,0:T(8,128)}), f32[32,8,128]{2,1,0:T(8,128)S(1)}, u32[]{:S(2)}, u32[]{:S(2)}) %all-to-all-start) | async-done | bytes 131104 | tf_op jit(solution)/shard_map/all_to_all | solution.py:335
  36.5 2.7 %combine.1 = (f32[1,1024]{1,0:T(1,128)S(1)}, bf16[32,1664]{1,0:T(8,128)(2,1)S(1)}) custom-call(f32[32,8,128]{2,1,0:T(8,128)S(1)} %all-to-all-done.parts_ref, f32[40,1024]{1,0:T(8,128)S(1)} %copy-done, bf16[1024,1664]{1,0:T(8,128)(2,1)} %grad_ref.3), custom_call_target="tpu_custom_call" | custom-call | flops 109051904 | bytes 4194304 | tf_op jit(solution)/shard_map/combine/pallas_call | solution.py:51
  40.7 2.5 %collective-permute-start.6 = (bf16[32,1792]{1,0:T(8,128)(2,1)S(1)}, bf16[32,1792]{1,0:T(8,128)(2,1)S(1)}, u32[]{:S(2)}, u32[]{:S(2)}) collective-permute-start(bf16[32,1792]{1,0:T(8,128)(2,1)S(1)} %add_convert_fusion.2.p0), channel_id=1, source_target_pairs={{0,96},{32,0},{64,32},{96,64},{1,97},{33,1},{65,33},{97,65},{2,98}... | collective-permute-start | bytes 344072 | tf_op jit(solution)/shard_map/ppermute | solution.py:340
  44.3 5.0 %collective-permute-done.7 = bf16[32,1664]{1,0:T(8,128)(2,1)S(1)} collective-permute-done((bf16[32,1664]{1,0:T(8,128)(2,1)S(1)}, bf16[32,1664]{1,0:T(8,128)(2,1)S(1)}, u32[]{:S(2)}, u32[]{:S(2)}) %collective-permute-start.7) | collective-permute-done | bytes 106528 | tf_op jit(solution)/shard_map/ppermute | solution.py:331
  49.4 2.3 %collective-permute-done.4.p1 = bf16[32,1792]{1,0:T(8,128)(2,1)S(1)} collective-permute-done((bf16[32,1792]{1,0:T(8,128)(2,1)S(1)}, bf16[32,1792]{1,0:T(8,128)(2,1)S(1)}, u32[]{:S(2)}, u32[]{:S(2)}) %collective-permute-start.4) | collective-permute-done | bytes 114720 | tf_op jit(solution)/shard_map/ppermute | solution.py:340
  52.5 3.5 %all-to-all-start.2 = ((bf16[4,32,1664]{2,1,0:T(8,128)(2,1)}), bf16[4,32,1664]{2,1,0:T(8,128)(2,1)S(1)}, u32[]{:S(2)}, u32[]{:S(2)}) async-start(bf16[4,32,1664]{2,1,0:T(8,128)(2,1)} %broadcast_in_dim.5), calls=%async_computation.2 | async-start | bytes 851968 | tf_op jit(solution)/shard_map/all_to_all | solution.py:335
  56.0 3.5 %forward.1 = (f32[32,1792]{1,0:T(8,128)S(1)}, bf16[2,64,2304]{2,1,0:T(8,128)(2,1)S(1)}, f32[2,64,256]{2,1,0:T(8,128)S(1)}, bf16[32,1664]{1,0:T(8,128)(2,1)S(1)}) custom-call(f32[2,4,4,4]{3,2,1,0:T(4,128)S(1)} %copy-done.3, f32[2,4,4,4]{3,2,1,0:T(4,128)S(1)} %copy-done.4, bf16[32,1792]{1,0:T(8,128)(2,1)S(1)} %add_convert_fusion.2.p0, ...), custom_call_target="tpu_custom_call" | custom-call | flops 218103808 | bytes 5242880 | tf_op jit(solution)/shard_map/forward/pallas_call | solution.py:51
  59.5 4.2 %collective-permute-start.8 = (bf16[32,1664]{1,0:T(8,128)(2,1)S(1)}, bf16[32,1664]{1,0:T(8,128)(2,1)S(1)}, u32[]{:S(2)}, u32[]{:S(2)}) collective-permute-start(bf16[32,1664]{1,0:T(8,128)(2,1)S(1)} %get-tuple-element.51), channel_id=1, source_target_pairs={{0,128},{128,0},{1,129},{129,1},{2,130},{130,2},{3,131},{131,3},{4... | collective-permute-start | bytes 319496 | tf_op jit(solution)/shard_map/ppermute | solution.py:331
  63.7 3.4 %backward.1 = (bf16[2,64,1536]{2,1,0:T(8,128)(2,1)S(1)}, bf16[32,1792]{1,0:T(8,128)(2,1)S(1)}) custom-call(f32[2,4,4,4]{3,2,1,0:T(4,128)S(1)} %copy-done.3, f32[2,4,4,4]{3,2,1,0:T(4,128)S(1)} %copy-done.4, bf16[4,32,1664]{2,1,0:T(8,128)(2,1)S(1)} %all-to-all-done.2.parts_ref, bf16[2,4,416,256]{3,2,1,0:T(8,128)(2,1)} %first_ref.3, ...), custom_call_target="tpu_custom_call" | custom-call | flops 218103808 | bytes 5242880 | tf_op jit(solution)/shard_map/backward/pallas_call | solution.py:51
  67.1 3.8 %collective-permute-start.9 = (bf16[32,1792]{1,0:T(8,128)(2,1)S(1)}, bf16[32,1792]{1,0:T(8,128)(2,1)S(1)}, u32[]{:S(2)}, u32[]{:S(2)}) collective-permute-start(bf16[32,1792]{1,0:T(8,128)(2,1)S(1)} %get-tuple-element.55), channel_id=1, source_target_pairs={{0,128},{128,0},{1,129},{129,1},{2,130},{130,2},{3,131},{131,3},{4... | collective-permute-start | bytes 344072 | tf_op jit(solution)/shard_map/ppermute | solution.py:331
  71.7 3.6 %all-to-all-start.1 = ((bf16[4,32,1664]{2,1,0:T(8,128)(2,1)}), bf16[4,32,1664]{2,1,0:T(8,128)(2,1)S(1)}, u32[]{:S(2)}, u32[]{:S(2)}) async-start(bf16[4,32,1664]{2,1,0:T(8,128)(2,1)} %broadcast_in_dim.4), calls=%async_computation.1 | async-start | bytes 851968 | tf_op jit(solution)/shard_map/all_to_all | solution.py:335
  75.4 6.1 %all-to-all-done.1.parts_ref = bf16[4,32,1664]{2,1,0:T(8,128)(2,1)S(1)} async-done(((bf16[4,32,1664]{2,1,0:T(8,128)(2,1)}), bf16[4,32,1664]{2,1,0:T(8,128)(2,1)S(1)}, u32[]{:S(2)}, u32[]{:S(2)}) %all-to-all-start.1) | async-done | bytes 426016 | tf_op jit(solution)/shard_map/all_to_all | solution.py:335
  81.6 3.7 %combine_grad.1 = (f32[40,1024]{1,0:T(8,128)S(1)}, f32[32,8,128]{2,1,0:T(8,128)}) custom-call(bf16[4,32,1664]{2,1,0:T(8,128)(2,1)S(1)} %all-to-all-done.1.parts_ref, f32[40,1024]{1,0:T(8,128)S(1)} %copy-done.1, f32[1,1024]{1,0:T(1,128)S(1)} %get-tuple-element.58.total_ref, bf16[1024,1664]{1,0:T(8,128)(2,1)} %grad_ref.3), custom_call_target="tpu_custom_call" | custom-call | flops 109051904 | bytes 4194304 | tf_op jit(solution)/shard_map/combine_grad/pallas_call | solution.py:51
  85.3 8.1 %all-to-all-start.3 = ((f32[32,8,128]{2,1,0:T(8,128)}), f32[32,8,128]{2,1,0:T(8,128)S(1)}, u32[]{:S(2)}, u32[]{:S(2)}) async-start(f32[32,8,128]{2,1,0:T(8,128)} %get-tuple-element.59), calls=%async_computation.3 | async-start | bytes 262144 | tf_op jit(solution)/shard_map/all_to_all | solution.py:335
  95.6 2.4 %collective-permute-done.12.p3 = bf16[32,1792]{1,0:T(8,128)(2,1)S(1)} collective-permute-done((bf16[32,1792]{1,0:T(8,128)(2,1)S(1)}, bf16[32,1792]{1,0:T(8,128)(2,1)S(1)}, u32[]{:S(2)}, u32[]{:S(2)}) %collective-permute-start.12) | collective-permute-done | bytes 114720 | tf_op jit(solution)/shard_map/ppermute | solution.py:340
  98.0 2.1 %collective-permute-done.11.p2 = bf16[32,1792]{1,0:T(8,128)(2,1)S(1)} collective-permute-done((bf16[32,1792]{1,0:T(8,128)(2,1)S(1)}, bf16[32,1792]{1,0:T(8,128)(2,1)S(1)}, u32[]{:S(2)}, u32[]{:S(2)}) %collective-permute-start.11) | collective-permute-done | bytes 114720 | tf_op jit(solution)/shard_map/ppermute | solution.py:340
  100.1 3.1 %collective-permute-done.10.p1 = bf16[32,1792]{1,0:T(8,128)(2,1)S(1)} collective-permute-done((bf16[32,1792]{1,0:T(8,128)(2,1)S(1)}, bf16[32,1792]{1,0:T(8,128)(2,1)S(1)}, u32[]{:S(2)}, u32[]{:S(2)}) %collective-permute-start.10) | collective-permute-done | bytes 114720 | tf_op jit(solution)/shard_map/ppermute | solution.py:340
  103.2 3.9 %logit_grad.1 = (bf16[4,32,2176]{2,1,0:T(8,128)(2,1)}, bf16[32,1664]{1,0:T(8,128)(2,1)S(1)}, f32[32,128]{1,0:T(8,128)S(1)}) custom-call(bf16[32,1792]{1,0:T(8,128)(2,1)S(1)} %add_convert_fusion.1.p0, bf16[32,1792]{1,0:T(8,128)(2,1)S(1)} %collective-permute-done.10.p1, bf16[32,1792]{1,0:T(8,128)(2,1)S(1)} %collective-permute-done.11.p2, ...), custom_call_target="tpu_custom_call" | custom-call | flops 218103808 | bytes 4194304 | tf_op jit(solution)/shard_map/logit_grad/pallas_call | solution.py:51
  107.1 4.3 %all-to-all-start.4 = ((bf16[4,32,2176]{2,1,0:T(8,128)(2,1)}), bf16[4,32,2176]{2,1,0:T(8,128)(2,1)S(1)}, u32[]{:S(2)}, u32[]{:S(2)}) async-start(bf16[4,32,2176]{2,1,0:T(8,128)(2,1)} %get-tuple-element.62), calls=%async_computation.4 | async-start | bytes 1114112 | tf_op jit(solution)/shard_map/all_to_all | solution.py:335
  111.4 2.1 %constant_dynamic-slice_fusion.tok_ref = bf16[256,1664]{1,0:T(8,128)(2,1)} fusion(bf16[1024,1664]{1,0:T(8,128)(2,1)} %tok_ref.1, s32[]{:T(128)S(6)} %select_n.3), kind=kLoop, calls=%fused_computation.9 | loop fusion | bytes 1703940 | tf_op jit(solution)/shard_map/dynamic_slice | solution.py:444
  118.6 2.5 %collective-permute-done.13 = bf16[32,1664]{1,0:T(8,128)(2,1)S(1)} collective-permute-done((bf16[32,1664]{1,0:T(8,128)(2,1)S(1)}, bf16[32,1664]{1,0:T(8,128)(2,1)S(1)}, u32[]{:S(2)}, u32[]{:S(2)}) %collective-permute-start.13) | collective-permute-done | bytes 106528 | tf_op jit(solution)/shard_map/ppermute | solution.py:340
  121.1 5.0 %all-to-all-done.4.recv_ref = bf16[4,32,2176]{2,1,0:T(8,128)(2,1)S(1)} async-done(((bf16[4,32,2176]{2,1,0:T(8,128)(2,1)}), bf16[4,32,2176]{2,1,0:T(8,128)(2,1)S(1)}, u32[]{:S(2)}, u32[]{:S(2)}) %all-to-all-start.4) | async-done | bytes 557088 | tf_op jit(solution)/shard_map/all_to_all | solution.py:335
  126.1 3.6 %token_grad.1 = (f32[4,32,1664]{2,1,0:T(8,128)S(1)}, bf16[4,32,1664]{2,1,0:T(8,128)(2,1)S(1)}) custom-call(s32[2]{0:T(128)S(1)} %pad_add_fusion.place, bf16[4,32,2176]{2,1,0:T(8,128)(2,1)S(1)} %all-to-all-done.4.recv_ref, bf16[32,1664]{1,0:T(8,128)(2,1)S(1)} %copy-done.2, bf16[32,1664]{1,0:T(8,128)(2,1)S(1)} %collective-permute-done.1.s1, ...), custom_call_target="tpu_custom_call" | custom-call | flops 218103808 | bytes 4194304 | tf_op jit(solution)/shard_map/token_grad/pallas_call | solution.py:51
  131.2 2.9 %weight_grad.1 = (bf16[2,4,416,256]{3,2,1,0:T(8,128)(2,1)}, bf16[2,4,416,256]{3,2,1,0:T(8,128)(2,1)}) custom-call(f32[32,1792]{1,0:T(8,128)S(1)} %get-tuple-element.60.x_ref, bf16[2,64,2304]{2,1,0:T(8,128)(2,1)S(1)} %get-tuple-element.53.side_ref, bf16[2,64,1536]{2,1,0:T(8,128)(2,1)S(1)} %get-tuple-element.73.hg_ref), custom_call_target="tpu_custom_call" | custom-call | flops 218103808 | bytes 5242880 | tf_op jit(solution)/shard_map/weight_grad/pallas_call | solution.py:51
  134.9 4.0 %all-to-all-start.5 = ((bf16[4,32,1664]{2,1,0:T(8,128)(2,1)}), bf16[4,32,1664]{2,1,0:T(8,128)(2,1)S(1)}, u32[]{:S(2)}, u32[]{:S(2)}) async-start(bf16[4,32,1664]{2,1,0:T(8,128)(2,1)} %add_convert_fusion), calls=%async_computation.5 | async-start | bytes 851968 | tf_op jit(solution)/shard_map/all_to_all | solution.py:335
  139.2 2.5 %collective-permute-start.17 = (bf16[32,1664]{1,0:T(8,128)(2,1)S(1)}, bf16[32,1664]{1,0:T(8,128)(2,1)S(1)}, u32[]{:S(2)}, u32[]{:S(2)}) collective-permute-start(bf16[32,1664]{1,0:T(8,128)(2,1)S(1)} %add_convert_fusion.3.p0), channel_id=1, source_target_pairs={{0,128},{128,0},{1,129},{129,1},{2,130},{130,2},{3,131},{131,3},{4... | collective-permute-start | bytes 319496 | tf_op jit(solution)/shard_map/ppermute | solution.py:331
  143.1 6.6 %collective-permute-done.17.p1 = bf16[32,1664]{1,0:T(8,128)(2,1)S(1)} collective-permute-done((bf16[32,1664]{1,0:T(8,128)(2,1)S(1)}, bf16[32,1664]{1,0:T(8,128)(2,1)S(1)}, u32[]{:S(2)}, u32[]{:S(2)}) %collective-permute-start.17) | collective-permute-done | bytes 106528 | tf_op jit(solution)/shard_map/ppermute | solution.py:331
  (52 shorter events, 20.2 us)
Async XLA Ops:
  0.6 14.0 %copy-start.2 = (bf16[32,1664]{1,0:T(8,128)(2,1)S(1)}, bf16[32,1664]{1,0:T(8,128)(2,1)}, u32[]{:S(2)}) copy-start(bf16[32,1664]{1,0:T(8,128)(2,1)} %slot_ref.3) | copy-start | bytes 319492
  6.8 19.2 %collective-permute-start = (bf16[32,1792]{1,0:T(8,128)(2,1)}, bf16[32,1792]{1,0:T(8,128)(2,1)S(1)}, u32[]{:S(2)}, u32[]{:S(2)}) collective-permute-start(bf16[32,1792]{1,0:T(8,128)(2,1)} %get-tuple-element.42), channel_id=1, source_target_pairs={{0,128},{128,0},{1,129},{129,1},{2,130},{130,2},{3,131},{131,3},{4... | collective-permute-start | bytes 344072 | tf_op jit(solution)/shard_map/ppermute | solution.py:331
  14.7 12.3 %collective-permute-start.3 = (bf16[32,1664]{1,0:T(8,128)(2,1)S(1)}, bf16[32,1664]{1,0:T(8,128)(2,1)S(1)}, u32[]{:S(2)}, u32[]{:S(2)}) collective-permute-start(bf16[32,1664]{1,0:T(8,128)(2,1)S(1)} %copy-done.2), channel_id=1, source_target_pairs={{0,24},{8,0},{16,8},{24,16},{1,25},{9,1},{17,9},{25,17},{2,26},{10... | collective-permute-start | bytes 319496 | tf_op jit(solution)/shard_map/ppermute | solution.py:340
  16.3 14.2 %collective-permute-start.2 = (bf16[32,1664]{1,0:T(8,128)(2,1)S(1)}, bf16[32,1664]{1,0:T(8,128)(2,1)S(1)}, u32[]{:S(2)}, u32[]{:S(2)}) collective-permute-start(bf16[32,1664]{1,0:T(8,128)(2,1)S(1)} %copy-done.2), channel_id=1, source_target_pairs={{0,16},{8,24},{16,0},{24,8},{1,17},{9,25},{17,1},{25,9},{2,18},{10... | collective-permute-start | bytes 319496 | tf_op jit(solution)/shard_map/ppermute | solution.py:340
  16.6 14.0 %collective-permute-start.1 = (bf16[32,1664]{1,0:T(8,128)(2,1)S(1)}, bf16[32,1664]{1,0:T(8,128)(2,1)S(1)}, u32[]{:S(2)}, u32[]{:S(2)}) collective-permute-start(bf16[32,1664]{1,0:T(8,128)(2,1)S(1)} %copy-done.2), channel_id=1, source_target_pairs={{0,8},{8,16},{16,24},{24,0},{1,9},{9,17},{17,25},{25,1},{2,10},{10... | collective-permute-start | bytes 319496 | tf_op jit(solution)/shard_map/ppermute | solution.py:340
  17.3 18.3 %all-to-all-start = ((f32[32,8,128]{2,1,0:T(8,128)}), f32[32,8,128]{2,1,0:T(8,128)S(1)}, u32[]{:S(2)}, u32[]{:S(2)}) async-start(f32[32,8,128]{2,1,0:T(8,128)} %get-tuple-element.41), calls=%async_computation | async-start | bytes 262144 | tf_op jit(solution)/shard_map/all_to_all | solution.py:335
  35.6 0.9 copy-start
  39.2 16.8 %copy-start.3 = (f32[2,4,4,4]{3,2,1,0:T(4,128)S(1)}, f32[2,4,4,4]{3,2,1,0:T(4,128)}, u32[]{:S(2)}) copy-start(f32[2,4,4,4]{3,2,1,0:T(4,128)} %m1.3) | copy-start | bytes 1540
  39.2 16.8 %copy-start.4 = (f32[2,4,4,4]{3,2,1,0:T(4,128)S(1)}, f32[2,4,4,4]{3,2,1,0:T(4,128)}, u32[]{:S(2)}) copy-start(f32[2,4,4,4]{3,2,1,0:T(4,128)} %m2.3) | copy-start | bytes 1540
  39.2 10.1 %collective-permute-start.7 = (bf16[32,1664]{1,0:T(8,128)(2,1)S(1)}, bf16[32,1664]{1,0:T(8,128)(2,1)S(1)}, u32[]{:S(2)}, u32[]{:S(2)}) collective-permute-start(bf16[32,1664]{1,0:T(8,128)(2,1)S(1)} %get-tuple-element.46), channel_id=1, source_target_pairs={{0,128},{128,0},{1,129},{129,1},{2,130},{130,2},{3,131},{131,3},{4... | collective-permute-start | bytes 319496 | tf_op jit(solution)/shard_map/ppermute | solution.py:331
  40.7 8.7 %collective-permute-start.6 = (bf16[32,1792]{1,0:T(8,128)(2,1)S(1)}, bf16[32,1792]{1,0:T(8,128)(2,1)S(1)}, u32[]{:S(2)}, u32[]{:S(2)}) collective-permute-start(bf16[32,1792]{1,0:T(8,128)(2,1)S(1)} %add_convert_fusion.2.p0), channel_id=1, source_target_pairs={{0,96},{32,0},{64,32},{96,64},{1,97},{33,1},{65,33},{97,65},{2,98}... | collective-permute-start | bytes 344072 | tf_op jit(solution)/shard_map/ppermute | solution.py:340
  43.2 6.2 %collective-permute-start.5 = (bf16[32,1792]{1,0:T(8,128)(2,1)S(1)}, bf16[32,1792]{1,0:T(8,128)(2,1)S(1)}, u32[]{:S(2)}, u32[]{:S(2)}) collective-permute-start(bf16[32,1792]{1,0:T(8,128)(2,1)S(1)} %add_convert_fusion.2.p0), channel_id=1, source_target_pairs={{0,64},{32,96},{64,0},{96,32},{1,65},{33,97},{65,1},{97,33},{2,66}... | collective-permute-start | bytes 344072 | tf_op jit(solution)/shard_map/ppermute | solution.py:340
  43.7 8.0 %collective-permute-start.4 = (bf16[32,1792]{1,0:T(8,128)(2,1)S(1)}, bf16[32,1792]{1,0:T(8,128)(2,1)S(1)}, u32[]{:S(2)}, u32[]{:S(2)}) collective-permute-start(bf16[32,1792]{1,0:T(8,128)(2,1)S(1)} %add_convert_fusion.2.p0), channel_id=1, source_target_pairs={{0,32},{32,64},{64,96},{96,0},{1,33},{33,65},{65,97},{97,1},{2,34}... | collective-permute-start | bytes 344072 | tf_op jit(solution)/shard_map/ppermute | solution.py:340
  52.5 11.2 %all-to-all-start.2 = ((bf16[4,32,1664]{2,1,0:T(8,128)(2,1)}), bf16[4,32,1664]{2,1,0:T(8,128)(2,1)S(1)}, u32[]{:S(2)}, u32[]{:S(2)}) async-start(bf16[4,32,1664]{2,1,0:T(8,128)(2,1)} %broadcast_in_dim.5), calls=%async_computation.2 | async-start | bytes 851968 | tf_op jit(solution)/shard_map/all_to_all | solution.py:335
  59.5 11.4 %collective-permute-start.8 = (bf16[32,1664]{1,0:T(8,128)(2,1)S(1)}, bf16[32,1664]{1,0:T(8,128)(2,1)S(1)}, u32[]{:S(2)}, u32[]{:S(2)}) collective-permute-start(bf16[32,1664]{1,0:T(8,128)(2,1)S(1)} %get-tuple-element.51), channel_id=1, source_target_pairs={{0,128},{128,0},{1,129},{129,1},{2,130},{130,2},{3,131},{131,3},{4... | collective-permute-start | bytes 319496 | tf_op jit(solution)/shard_map/ppermute | solution.py:331
  67.1 14.5 %copy-start.1 = (f32[40,1024]{1,0:T(8,128)S(1)}, f32[40,1024]{1,0:T(8,128)}, u32[]{:S(2)}) copy-start(f32[40,1024]{1,0:T(8,128)} %get-tuple-element.45.w_ref) | copy-start | bytes 491524
  67.1 8.3 %collective-permute-start.9 = (bf16[32,1792]{1,0:T(8,128)(2,1)S(1)}, bf16[32,1792]{1,0:T(8,128)(2,1)S(1)}, u32[]{:S(2)}, u32[]{:S(2)}) collective-permute-start(bf16[32,1792]{1,0:T(8,128)(2,1)S(1)} %get-tuple-element.55), channel_id=1, source_target_pairs={{0,128},{128,0},{1,129},{129,1},{2,130},{130,2},{3,131},{131,3},{4... | collective-permute-start | bytes 344072 | tf_op jit(solution)/shard_map/ppermute | solution.py:331
  71.7 9.8 %all-to-all-start.1 = ((bf16[4,32,1664]{2,1,0:T(8,128)(2,1)}), bf16[4,32,1664]{2,1,0:T(8,128)(2,1)S(1)}, u32[]{:S(2)}, u32[]{:S(2)}) async-start(bf16[4,32,1664]{2,1,0:T(8,128)(2,1)} %broadcast_in_dim.4), calls=%async_computation.1 | async-start | bytes 851968 | tf_op jit(solution)/shard_map/all_to_all | solution.py:335
  85.3 17.9 %all-to-all-start.3 = ((f32[32,8,128]{2,1,0:T(8,128)}), f32[32,8,128]{2,1,0:T(8,128)S(1)}, u32[]{:S(2)}, u32[]{:S(2)}) async-start(f32[32,8,128]{2,1,0:T(8,128)} %get-tuple-element.59), calls=%async_computation.3 | async-start | bytes 262144 | tf_op jit(solution)/shard_map/all_to_all | solution.py:335
  93.4 4.6 %collective-permute-start.12 = (bf16[32,1792]{1,0:T(8,128)(2,1)S(1)}, bf16[32,1792]{1,0:T(8,128)(2,1)S(1)}, u32[]{:S(2)}, u32[]{:S(2)}) collective-permute-start(bf16[32,1792]{1,0:T(8,128)(2,1)S(1)} %add_convert_fusion.1.p0), channel_id=1, source_target_pairs={{0,96},{32,0},{64,32},{96,64},{1,97},{33,1},{65,33},{97,65},{2,98}... | collective-permute-start | bytes 344072 | tf_op jit(solution)/shard_map/ppermute | solution.py:340
  94.4 5.7 %collective-permute-start.11 = (bf16[32,1792]{1,0:T(8,128)(2,1)S(1)}, bf16[32,1792]{1,0:T(8,128)(2,1)S(1)}, u32[]{:S(2)}, u32[]{:S(2)}) collective-permute-start(bf16[32,1792]{1,0:T(8,128)(2,1)S(1)} %add_convert_fusion.1.p0), channel_id=1, source_target_pairs={{0,64},{32,96},{64,0},{96,32},{1,65},{33,97},{65,1},{97,33},{2,66}... | collective-permute-start | bytes 344072 | tf_op jit(solution)/shard_map/ppermute | solution.py:340
  95.6 7.6 %collective-permute-start.10 = (bf16[32,1792]{1,0:T(8,128)(2,1)S(1)}, bf16[32,1792]{1,0:T(8,128)(2,1)S(1)}, u32[]{:S(2)}, u32[]{:S(2)}) collective-permute-start(bf16[32,1792]{1,0:T(8,128)(2,1)S(1)} %add_convert_fusion.1.p0), channel_id=1, source_target_pairs={{0,32},{32,64},{64,96},{96,0},{1,33},{33,65},{65,97},{97,1},{2,34}... | collective-permute-start | bytes 344072 | tf_op jit(solution)/shard_map/ppermute | solution.py:340
  107.1 19.0 %all-to-all-start.4 = ((bf16[4,32,2176]{2,1,0:T(8,128)(2,1)}), bf16[4,32,2176]{2,1,0:T(8,128)(2,1)S(1)}, u32[]{:S(2)}, u32[]{:S(2)}) async-start(bf16[4,32,2176]{2,1,0:T(8,128)(2,1)} %get-tuple-element.62), calls=%async_computation.4 | async-start | bytes 1114112 | tf_op jit(solution)/shard_map/all_to_all | solution.py:335
  113.6 3.9 %collective-permute-start.15 = (bf16[32,1664]{1,0:T(8,128)(2,1)S(1)}, bf16[32,1664]{1,0:T(8,128)(2,1)S(1)}, u32[]{:S(2)}, u32[]{:S(2)}) collective-permute-start(bf16[32,1664]{1,0:T(8,128)(2,1)S(1)} %get-tuple-element.63), channel_id=1, source_target_pairs={{0,96},{32,0},{64,32},{96,64},{1,97},{33,1},{65,33},{97,65},{2,98}... | collective-permute-start | bytes 319496 | tf_op jit(solution)/shard_map/ppermute | solution.py:340
  113.6 5.1 %collective-permute-start.14 = (bf16[32,1664]{1,0:T(8,128)(2,1)S(1)}, bf16[32,1664]{1,0:T(8,128)(2,1)S(1)}, u32[]{:S(2)}, u32[]{:S(2)}) collective-permute-start(bf16[32,1664]{1,0:T(8,128)(2,1)S(1)} %get-tuple-element.63), channel_id=1, source_target_pairs={{0,32},{32,64},{64,96},{96,0},{1,33},{33,65},{65,97},{97,1},{2,34}... | collective-permute-start | bytes 319496 | tf_op jit(solution)/shard_map/ppermute | solution.py:340
  115.0 6.0 %collective-permute-start.13 = (bf16[32,1664]{1,0:T(8,128)(2,1)S(1)}, bf16[32,1664]{1,0:T(8,128)(2,1)S(1)}, u32[]{:S(2)}, u32[]{:S(2)}) collective-permute-start(bf16[32,1664]{1,0:T(8,128)(2,1)S(1)} %get-tuple-element.63), channel_id=1, source_target_pairs={{0,64},{32,96},{64,0},{96,32},{1,65},{33,97},{65,1},{97,33},{2,66}... | collective-permute-start | bytes 319496 | tf_op jit(solution)/shard_map/ppermute | solution.py:340
  129.7 4.4 %collective-permute-start.16 = (bf16[4,32,1664]{2,1,0:T(8,128)(2,1)S(1)}, bf16[4,32,1664]{2,1,0:T(8,128)(2,1)S(1)}, u32[]{:S(2)}, u32[]{:S(2)}) collective-permute-start(bf16[4,32,1664]{2,1,0:T(8,128)(2,1)S(1)} %get-tuple-element.70), channel_id=1, source_target_pairs={{0,1},{1,0},{2,3},{3,2},{4,5},{5,4},{6,7},{7,6},{8,9},{9,8},{10,11... | collective-permute-start | bytes 1277960 | tf_op jit(solution)/shard_map/ppermute | solution.py:331
  134.9 15.7 %all-to-all-start.5 = ((bf16[4,32,1664]{2,1,0:T(8,128)(2,1)}), bf16[4,32,1664]{2,1,0:T(8,128)(2,1)S(1)}, u32[]{:S(2)}, u32[]{:S(2)}) async-start(bf16[4,32,1664]{2,1,0:T(8,128)(2,1)} %add_convert_fusion), calls=%async_computation.5 | async-start | bytes 851968 | tf_op jit(solution)/shard_map/all_to_all | solution.py:335
  139.2 10.6 %collective-permute-start.17 = (bf16[32,1664]{1,0:T(8,128)(2,1)S(1)}, bf16[32,1664]{1,0:T(8,128)(2,1)S(1)}, u32[]{:S(2)}, u32[]{:S(2)}) collective-permute-start(bf16[32,1664]{1,0:T(8,128)(2,1)S(1)} %add_convert_fusion.3.p0), channel_id=1, source_target_pairs={{0,128},{128,0},{1,129},{129,1},{2,130},{130,2},{3,131},{131,3},{4... | collective-permute-start | bytes 319496 | tf_op jit(solution)/shard_map/ppermute | solution.py:331

commit v4 on v3

--- a/solution.py
+++ b/solution.py
@@ -353,7 +353,6 @@
 
 def local(tokens, out_grad, slot_params, m1, first_blocks, m2, second_blocks):
     second_turned = jnp.swapaxes(second_blocks, 2, 3)
-    slot_all = ring(slot_params, "z")
     w, colsum, input_part = call(
         routing_body,
         (sds((40, TOK), f32), sds((32, 8, 128), f32), sds((32, DIM + EXTRA), bf16)),
@@ -366,7 +365,7 @@
     )
     input_far = far_sum(input_part)
     col_parts = exchange(colsum, exp_axes)
-    col_parts, input_far, *slot_all = tie((col_parts, input_far, *slot_all))
+    col_parts, input_far = tie((col_parts, input_far))
     total, grad_part = call(
         combine_body,
         (sds((1, TOK), f32), sds((32, DIM), bf16)),
@@ -408,6 +407,10 @@
     input_grad_far = far_sum(input_grad_part)
     out_parts, input_grad_far = tie((out_parts, input_grad_far))
     input_grad_parts = ring(input_grad_far, "x")
+    out_parts, slot_own = tie((out_parts, slot_params))
+    slot_all = ring(slot_own, "z")
+    *input_grad_parts, s1, s2, s3 = tie((*input_grad_parts, *slot_all[1:]))
+    slot_all = (slot_params, s1, s2, s3)
     cg, cols = call(
         combine_grad_body,
         (sds((40, TOK), f32), sds((32, 8, 128), f32)),

time: 152 us -> 151 us (level)
    all_to_all x6, starting transfers between devices: 32.2 us -> 28.4 us  [exchange(): return lax.all_to_all(value, axes, 0, 0)]
    ppermute x12, starting transfers between devices: 11.4 us -> 14.8 us  [ring(): return [value] + [lax.ppermute(value, axis, p) for p in pairs]]
    ppermute x12, waiting for transfers between devices: 18 us -> 16 us  [ring(): return [value] + [lax.ppermute(value, axis, p) for p in pairs]]
    all_to_all x6, waiting for transfers between devices: 16.2 us -> 17.9 us  [exchange(): return lax.all_to_all(value, axes, 0, 0)]
  transfers between devices with their start and end apart: 24 -> 24, of which waited for: 13 -> 11; matrix products, arithmetic and copies ran while one was open for 4% -> 4% of each run, Pallas kernels for 7% -> 7%
where the time goes in v4:
time: 151 us; the launch traced here: 150 us
  starting transfers between devices  64.6 us (43%)
  waiting for transfers between devices  44.6 us (30%)
  Pallas kernels  30.7 us (20%)
  local copies, waits for them, and re-layouts  6.27 us (4%)
  other arithmetic  2.79 us (2%)
    pallas_call x9, Pallas kernels, call(): pl.pallas_call(body, out_shape=out, in_specs=[pl.BlockSpec(memory_space=S...  30.7 us
    all_to_all x6, starting transfers between devices, exchange(): return lax.all_to_all(value, axes, 0, 0)  28.4 us
    ppermute x6, starting transfers between devices, swap(): return lax.ppermute(value, axis, [(0, 1), (1, 0)])  21.4 us
    all_to_all x6, waiting for transfers between devices, exchange(): return lax.all_to_all(value, axes, 0, 0)  17.9 us
    ppermute x12, waiting for transfers between devices, ring(): return [value] + [lax.ppermute(value, axis, p) for p in pairs]  16 us
    ppermute x12, starting transfers between devices, ring(): return [value] + [lax.ppermute(value, axis, p) for p in pairs]  14.8 us
    ppermute x6, waiting for transfers between devices, swap(): return lax.ppermute(value, axis, [(0, 1), (1, 0)])  10.7 us
  transfers between devices with their start and end apart: 24, of which 11 were waited for; matrix products, arithmetic and copies ran while one was open for 4% of the time, Pallas kernels for 7%

profile of v4, /device:TPU:1, one launch (start us, length us, event | category | flops | bytes accessed | tf_op | source)
XLA Modules:
  0.0 149.9 jit_solution(7716013820272998472)
XLA Ops:
  0.6 6.1 %routing.1 = (f32[40,1024]{1,0:T(8,128)}, f32[32,8,128]{2,1,0:T(8,128)}, bf16[32,1792]{1,0:T(8,128)(2,1)}) custom-call(bf16[32,1664]{1,0:T(8,128)(2,1)} %slot_ref.3, bf16[1024,1664]{1,0:T(8,128)(2,1)} %tok_ref.1), custom_call_target="tpu_custom_call" | custom-call | flops 218103808 | bytes 4194304 | tf_op jit(solution)/shard_map/routing/pallas_call | solution.py:51
  6.8 7.8 %collective-permute-start = (bf16[32,1792]{1,0:T(8,128)(2,1)}, bf16[32,1792]{1,0:T(8,128)(2,1)S(1)}, u32[]{:S(2)}, u32[]{:S(2)}) collective-permute-start(bf16[32,1792]{1,0:T(8,128)(2,1)} %get-tuple-element.47), channel_id=1, source_target_pairs={{0,128},{128,0},{1,129},{129,1},{2,130},{130,2},{3,131},{131,3},{4... | collective-permute-start | bytes 344072 | tf_op jit(solution)/shard_map/ppermute | solution.py:331
  14.6 6.9 %all-to-all-start = ((f32[32,8,128]{2,1,0:T(8,128)}), f32[32,8,128]{2,1,0:T(8,128)S(1)}, u32[]{:S(2)}, u32[]{:S(2)}) async-start(f32[32,8,128]{2,1,0:T(8,128)} %get-tuple-element.46), calls=%async_computation | async-start | bytes 262144 | tf_op jit(solution)/shard_map/all_to_all | solution.py:335
  22.5 7.6 %all-to-all-done.parts_ref = f32[32,8,128]{2,1,0:T(8,128)S(1)} async-done(((f32[32,8,128]{2,1,0:T(8,128)}), f32[32,8,128]{2,1,0:T(8,128)S(1)}, u32[]{:S(2)}, u32[]{:S(2)}) %all-to-all-start) | async-done | bytes 131104 | tf_op jit(solution)/shard_map/all_to_all | solution.py:335
  31.0 2.7 %combine.1 = (f32[1,1024]{1,0:T(1,128)S(1)}, bf16[32,1664]{1,0:T(8,128)(2,1)S(1)}) custom-call(f32[32,8,128]{2,1,0:T(8,128)S(1)} %all-to-all-done.parts_ref, f32[40,1024]{1,0:T(8,128)S(1)} %copy-done, bf16[1024,1664]{1,0:T(8,128)(2,1)} %grad_ref.3), custom_call_target="tpu_custom_call" | custom-call | flops 109051904 | bytes 4194304 | tf_op jit(solution)/shard_map/combine/pallas_call | solution.py:51
  35.3 2.5 %collective-permute-start.3 = (bf16[32,1792]{1,0:T(8,128)(2,1)S(1)}, bf16[32,1792]{1,0:T(8,128)(2,1)S(1)}, u32[]{:S(2)}, u32[]{:S(2)}) collective-permute-start(bf16[32,1792]{1,0:T(8,128)(2,1)S(1)} %add_convert_fusion.2.p0), channel_id=1, source_target_pairs={{0,96},{32,0},{64,32},{96,64},{1,97},{33,1},{65,33},{97,65},{2,98}... | collective-permute-start | bytes 344072 | tf_op jit(solution)/shard_map/ppermute | solution.py:340
  38.9 4.6 %collective-permute-done.4 = bf16[32,1664]{1,0:T(8,128)(2,1)S(1)} collective-permute-done((bf16[32,1664]{1,0:T(8,128)(2,1)S(1)}, bf16[32,1664]{1,0:T(8,128)(2,1)S(1)}, u32[]{:S(2)}, u32[]{:S(2)}) %collective-permute-start.4) | collective-permute-done | bytes 106528 | tf_op jit(solution)/shard_map/ppermute | solution.py:331
  43.5 3.1 %collective-permute-done.1.p1 = bf16[32,1792]{1,0:T(8,128)(2,1)S(1)} collective-permute-done((bf16[32,1792]{1,0:T(8,128)(2,1)S(1)}, bf16[32,1792]{1,0:T(8,128)(2,1)S(1)}, u32[]{:S(2)}, u32[]{:S(2)}) %collective-permute-start.1) | collective-permute-done | bytes 114720 | tf_op jit(solution)/shard_map/ppermute | solution.py:340
  47.4 3.5 %all-to-all-start.2 = ((bf16[4,32,1664]{2,1,0:T(8,128)(2,1)}), bf16[4,32,1664]{2,1,0:T(8,128)(2,1)S(1)}, u32[]{:S(2)}, u32[]{:S(2)}) async-start(bf16[4,32,1664]{2,1,0:T(8,128)(2,1)} %broadcast_in_dim.5), calls=%async_computation.2 | async-start | bytes 851968 | tf_op jit(solution)/shard_map/all_to_all | solution.py:335
  50.9 3.5 %forward.1 = (f32[32,1792]{1,0:T(8,128)S(1)}, bf16[2,64,2304]{2,1,0:T(8,128)(2,1)S(1)}, f32[2,64,256]{2,1,0:T(8,128)S(1)}, bf16[32,1664]{1,0:T(8,128)(2,1)S(1)}) custom-call(f32[2,4,4,4]{3,2,1,0:T(4,128)S(1)} %copy-done.3, f32[2,4,4,4]{3,2,1,0:T(4,128)S(1)} %copy-done.4, bf16[32,1792]{1,0:T(8,128)(2,1)S(1)} %add_convert_fusion.2.p0, ...), custom_call_target="tpu_custom_call" | custom-call | flops 218103808 | bytes 5242880 | tf_op jit(solution)/shard_map/forward/pallas_call | solution.py:51
  54.4 3.7 %collective-permute-start.5 = (bf16[32,1664]{1,0:T(8,128)(2,1)S(1)}, bf16[32,1664]{1,0:T(8,128)(2,1)S(1)}, u32[]{:S(2)}, u32[]{:S(2)}) collective-permute-start(bf16[32,1664]{1,0:T(8,128)(2,1)S(1)} %get-tuple-element.56), channel_id=1, source_target_pairs={{0,128},{128,0},{1,129},{129,1},{2,130},{130,2},{3,131},{131,3},{4... | collective-permute-start | bytes 319496 | tf_op jit(solution)/shard_map/ppermute | solution.py:331
  58.4 3.4 %backward.1 = (bf16[2,64,1536]{2,1,0:T(8,128)(2,1)S(1)}, bf16[32,1792]{1,0:T(8,128)(2,1)S(1)}) custom-call(f32[2,4,4,4]{3,2,1,0:T(4,128)S(1)} %copy-done.3, f32[2,4,4,4]{3,2,1,0:T(4,128)S(1)} %copy-done.4, bf16[4,32,1664]{2,1,0:T(8,128)(2,1)S(1)} %all-to-all-done.2.parts_ref, bf16[2,4,416,256]{3,2,1,0:T(8,128)(2,1)} %first_ref.3, ...), custom_call_target="tpu_custom_call" | custom-call | flops 218103808 | bytes 5242880 | tf_op jit(solution)/shard_map/backward/pallas_call | solution.py:51
  61.8 3.5 %collective-permute-start.6 = (bf16[32,1792]{1,0:T(8,128)(2,1)S(1)}, bf16[32,1792]{1,0:T(8,128)(2,1)S(1)}, u32[]{:S(2)}, u32[]{:S(2)}) collective-permute-start(bf16[32,1792]{1,0:T(8,128)(2,1)S(1)} %get-tuple-element.60), channel_id=1, source_target_pairs={{0,128},{128,0},{1,129},{129,1},{2,130},{130,2},{3,131},{131,3},{4... | collective-permute-start | bytes 344072 | tf_op jit(solution)/shard_map/ppermute | solution.py:331
  66.1 3.5 %all-to-all-start.1 = ((bf16[4,32,1664]{2,1,0:T(8,128)(2,1)}), bf16[4,32,1664]{2,1,0:T(8,128)(2,1)S(1)}, u32[]{:S(2)}, u32[]{:S(2)}) async-start(bf16[4,32,1664]{2,1,0:T(8,128)(2,1)} %broadcast_in_dim.4), calls=%async_computation.1 | async-start | bytes 851968 | tf_op jit(solution)/shard_map/all_to_all | solution.py:335
  69.6 6.3 %all-to-all-done.1.parts_ref = bf16[4,32,1664]{2,1,0:T(8,128)(2,1)S(1)} async-done(((bf16[4,32,1664]{2,1,0:T(8,128)(2,1)}), bf16[4,32,1664]{2,1,0:T(8,128)(2,1)S(1)}, u32[]{:S(2)}, u32[]{:S(2)}) %all-to-all-start.1) | async-done | bytes 426016 | tf_op jit(solution)/shard_map/all_to_all | solution.py:335
  75.9 3.8 %combine_grad.1 = (f32[40,1024]{1,0:T(8,128)S(1)}, f32[32,8,128]{2,1,0:T(8,128)}) custom-call(bf16[4,32,1664]{2,1,0:T(8,128)(2,1)S(1)} %all-to-all-done.1.parts_ref, f32[40,1024]{1,0:T(8,128)S(1)} %copy-done.1, f32[1,1024]{1,0:T(1,128)S(1)} %get-tuple-element.69.total_ref, bf16[1024,1664]{1,0:T(8,128)(2,1)} %grad_ref.3), custom_call_target="tpu_custom_call" | custom-call | flops 109051904 | bytes 4194304 | tf_op jit(solution)/shard_map/combine_grad/pallas_call | solution.py:51
  79.7 7.1 %all-to-all-start.3 = ((f32[32,8,128]{2,1,0:T(8,128)}), f32[32,8,128]{2,1,0:T(8,128)S(1)}, u32[]{:S(2)}, u32[]{:S(2)}) async-start(f32[32,8,128]{2,1,0:T(8,128)} %get-tuple-element.70), calls=%async_computation.3 | async-start | bytes 262144 | tf_op jit(solution)/shard_map/all_to_all | solution.py:335
  86.8 3.4 %collective-permute-start.12 = (bf16[32,1664]{1,0:T(8,128)(2,1)S(1)}, bf16[32,1664]{1,0:T(8,128)(2,1)S(1)}, u32[]{:S(2)}, u32[]{:S(2)}) collective-permute-start(bf16[32,1664]{1,0:T(8,128)(2,1)S(1)} %copy-done.2), channel_id=1, source_target_pairs={{0,24},{8,0},{16,8},{24,16},{1,25},{9,1},{17,9},{25,17},{2,26},{10... | collective-permute-start | bytes 319496 | tf_op jit(solution)/shard_map/ppermute | solution.py:340
  93.2 2.2 %collective-permute-start.10 = (bf16[32,1664]{1,0:T(8,128)(2,1)S(1)}, bf16[32,1664]{1,0:T(8,128)(2,1)S(1)}, u32[]{:S(2)}, u32[]{:S(2)}) collective-permute-start(bf16[32,1664]{1,0:T(8,128)(2,1)S(1)} %copy-done.2), channel_id=1, source_target_pairs={{0,8},{8,16},{16,24},{24,0},{1,9},{9,17},{17,25},{25,1},{2,10},{10... | collective-permute-start | bytes 319496 | tf_op jit(solution)/shard_map/ppermute | solution.py:340
  95.4 6.8 %collective-permute-done.11.s2 = bf16[32,1664]{1,0:T(8,128)(2,1)S(1)} collective-permute-done((bf16[32,1664]{1,0:T(8,128)(2,1)S(1)}, bf16[32,1664]{1,0:T(8,128)(2,1)S(1)}, u32[]{:S(2)}, u32[]{:S(2)}) %collective-permute-start.11) | collective-permute-done | bytes 106528 | tf_op jit(solution)/shard_map/ppermute | solution.py:340
  102.2 3.9 %logit_grad.1 = (bf16[4,32,2176]{2,1,0:T(8,128)(2,1)}, bf16[32,1664]{1,0:T(8,128)(2,1)S(1)}, f32[32,128]{1,0:T(8,128)S(1)}) custom-call(bf16[32,1792]{1,0:T(8,128)(2,1)S(1)} %add_convert_fusion.1.p0, bf16[32,1792]{1,0:T(8,128)(2,1)S(1)} %collective-permute-done.7.p1, bf16[32,1792]{1,0:T(8,128)(2,1)S(1)} %collective-permute-done.8.p2, ...), custom_call_target="tpu_custom_call" | custom-call | flops 218103808 | bytes 4194304 | tf_op jit(solution)/shard_map/logit_grad/pallas_call | solution.py:51
  106.1 3.5 %all-to-all-start.4 = ((bf16[4,32,2176]{2,1,0:T(8,128)(2,1)}), bf16[4,32,2176]{2,1,0:T(8,128)(2,1)S(1)}, u32[]{:S(2)}, u32[]{:S(2)}) async-start(bf16[4,32,2176]{2,1,0:T(8,128)(2,1)} %get-tuple-element.73), calls=%async_computation.4 | async-start | bytes 1114112 | tf_op jit(solution)/shard_map/all_to_all | solution.py:335
  109.6 2.1 %constant_dynamic-slice_fusion.tok_ref = bf16[256,1664]{1,0:T(8,128)(2,1)} fusion(bf16[1024,1664]{1,0:T(8,128)(2,1)} %tok_ref.1, s32[]{:T(128)S(6)} %select_n.3), kind=kLoop, calls=%fused_computation.9 | loop fusion | bytes 1703940 | tf_op jit(solution)/shard_map/dynamic_slice | solution.py:447
  111.8 1.8 %collective-permute-start.15 = (bf16[32,1664]{1,0:T(8,128)(2,1)S(1)}, bf16[32,1664]{1,0:T(8,128)(2,1)S(1)}, u32[]{:S(2)}, u32[]{:S(2)}) collective-permute-start(bf16[32,1664]{1,0:T(8,128)(2,1)S(1)} %get-tuple-element.74), channel_id=1, source_target_pairs={{0,96},{32,0},{64,32},{96,64},{1,97},{33,1},{65,33},{97,65},{2,98}... | collective-permute-start | bytes 319496 | tf_op jit(solution)/shard_map/ppermute | solution.py:340
  113.5 1.8 %collective-permute-start.13 = (bf16[32,1664]{1,0:T(8,128)(2,1)S(1)}, bf16[32,1664]{1,0:T(8,128)(2,1)S(1)}, u32[]{:S(2)}, u32[]{:S(2)}) collective-permute-start(bf16[32,1664]{1,0:T(8,128)(2,1)S(1)} %get-tuple-element.74), channel_id=1, source_target_pairs={{0,64},{32,96},{64,0},{96,32},{1,65},{33,97},{65,1},{97,33},{2,66}... | collective-permute-start | bytes 319496 | tf_op jit(solution)/shard_map/ppermute | solution.py:340
  115.6 4.9 %collective-permute-done.14 = bf16[32,1664]{1,0:T(8,128)(2,1)S(1)} collective-permute-done((bf16[32,1664]{1,0:T(8,128)(2,1)S(1)}, bf16[32,1664]{1,0:T(8,128)(2,1)S(1)}, u32[]{:S(2)}, u32[]{:S(2)}) %collective-permute-start.14) | collective-permute-done | bytes 106528 | tf_op jit(solution)/shard_map/ppermute | solution.py:340
  120.6 3.7 %all-to-all-done.4.recv_ref = bf16[4,32,2176]{2,1,0:T(8,128)(2,1)S(1)} async-done(((bf16[4,32,2176]{2,1,0:T(8,128)(2,1)}), bf16[4,32,2176]{2,1,0:T(8,128)(2,1)S(1)}, u32[]{:S(2)}, u32[]{:S(2)}) %all-to-all-start.4) | async-done | bytes 557088 | tf_op jit(solution)/shard_map/all_to_all | solution.py:335
  124.3 3.6 %token_grad.1 = (f32[4,32,1664]{2,1,0:T(8,128)S(1)}, bf16[4,32,1664]{2,1,0:T(8,128)(2,1)S(1)}) custom-call(s32[2]{0:T(128)S(1)} %pad_add_fusion.place, bf16[4,32,2176]{2,1,0:T(8,128)(2,1)S(1)} %all-to-all-done.4.recv_ref, bf16[32,1664]{1,0:T(8,128)(2,1)S(1)} %copy-done.2, bf16[32,1664]{1,0:T(8,128)(2,1)S(1)} %collective-permute-done.10.s1, ...), custom_call_target="tpu_custom_call" | custom-call | flops 218103808 | bytes 4194304 | tf_op jit(solution)/shard_map/token_grad/pallas_call | solution.py:51
  129.4 2.9 %weight_grad.1 = (bf16[2,4,416,256]{3,2,1,0:T(8,128)(2,1)}, bf16[2,4,416,256]{3,2,1,0:T(8,128)(2,1)}) custom-call(f32[32,1792]{1,0:T(8,128)S(1)} %get-tuple-element.71.x_ref, bf16[2,64,2304]{2,1,0:T(8,128)(2,1)S(1)} %get-tuple-element.58.side_ref, bf16[2,64,1536]{2,1,0:T(8,128)(2,1)S(1)} %get-tuple-element.83.hg_ref), custom_call_target="tpu_custom_call" | custom-call | flops 218103808 | bytes 5242880 | tf_op jit(solution)/shard_map/weight_grad/pallas_call | solution.py:51
  133.1 4.0 %all-to-all-start.5 = ((bf16[4,32,1664]{2,1,0:T(8,128)(2,1)}), bf16[4,32,1664]{2,1,0:T(8,128)(2,1)S(1)}, u32[]{:S(2)}, u32[]{:S(2)}) async-start(bf16[4,32,1664]{2,1,0:T(8,128)(2,1)} %add_convert_fusion), calls=%async_computation.5 | async-start | bytes 851968 | tf_op jit(solution)/shard_map/all_to_all | solution.py:335
  137.3 3.3 %collective-permute-start.17 = (bf16[32,1664]{1,0:T(8,128)(2,1)S(1)}, bf16[32,1664]{1,0:T(8,128)(2,1)S(1)}, u32[]{:S(2)}, u32[]{:S(2)}) collective-permute-start(bf16[32,1664]{1,0:T(8,128)(2,1)S(1)} %add_convert_fusion.3.p0), channel_id=1, source_target_pairs={{0,128},{128,0},{1,129},{129,1},{2,130},{130,2},{3,131},{131,3},{4... | collective-permute-start | bytes 319496 | tf_op jit(solution)/shard_map/ppermute | solution.py:331
  142.1 6.1 %collective-permute-done.17.p1 = bf16[32,1664]{1,0:T(8,128)(2,1)S(1)} collective-permute-done((bf16[32,1664]{1,0:T(8,128)(2,1)S(1)}, bf16[32,1664]{1,0:T(8,128)(2,1)S(1)}, u32[]{:S(2)}, u32[]{:S(2)}) %collective-permute-start.17) | collective-permute-done | bytes 106528 | tf_op jit(solution)/shard_map/ppermute | solution.py:331
  (52 shorter events, 15.6 us)
Async XLA Ops:
  6.8 14.8 %collective-permute-start = (bf16[32,1792]{1,0:T(8,128)(2,1)}, bf16[32,1792]{1,0:T(8,128)(2,1)S(1)}, u32[]{:S(2)}, u32[]{:S(2)}) collective-permute-start(bf16[32,1792]{1,0:T(8,128)(2,1)} %get-tuple-element.47), channel_id=1, source_target_pairs={{0,128},{128,0},{1,129},{129,1},{2,130},{130,2},{3,131},{131,3},{4... | collective-permute-start | bytes 344072 | tf_op jit(solution)/shard_map/ppermute | solution.py:331
  14.6 15.5 %all-to-all-start = ((f32[32,8,128]{2,1,0:T(8,128)}), f32[32,8,128]{2,1,0:T(8,128)S(1)}, u32[]{:S(2)}, u32[]{:S(2)}) async-start(f32[32,8,128]{2,1,0:T(8,128)} %get-tuple-element.46), calls=%async_computation | async-start | bytes 262144 | tf_op jit(solution)/shard_map/all_to_all | solution.py:335
  30.1 0.9 copy-start
  33.7 17.2 %copy-start.3 = (f32[2,4,4,4]{3,2,1,0:T(4,128)S(1)}, f32[2,4,4,4]{3,2,1,0:T(4,128)}, u32[]{:S(2)}) copy-start(f32[2,4,4,4]{3,2,1,0:T(4,128)} %m1.3) | copy-start | bytes 1540
  33.7 17.2 %copy-start.4 = (f32[2,4,4,4]{3,2,1,0:T(4,128)S(1)}, f32[2,4,4,4]{3,2,1,0:T(4,128)}, u32[]{:S(2)}) copy-start(f32[2,4,4,4]{3,2,1,0:T(4,128)} %m2.3) | copy-start | bytes 1540
  33.7 9.8 %collective-permute-start.4 = (bf16[32,1664]{1,0:T(8,128)(2,1)S(1)}, bf16[32,1664]{1,0:T(8,128)(2,1)S(1)}, u32[]{:S(2)}, u32[]{:S(2)}) collective-permute-start(bf16[32,1664]{1,0:T(8,128)(2,1)S(1)} %get-tuple-element.51), channel_id=1, source_target_pairs={{0,128},{128,0},{1,129},{129,1},{2,130},{130,2},{3,131},{131,3},{4... | collective-permute-start | bytes 319496 | tf_op jit(solution)/shard_map/ppermute | solution.py:331
  35.3 8.2 %collective-permute-start.3 = (bf16[32,1792]{1,0:T(8,128)(2,1)S(1)}, bf16[32,1792]{1,0:T(8,128)(2,1)S(1)}, u32[]{:S(2)}, u32[]{:S(2)}) collective-permute-start(bf16[32,1792]{1,0:T(8,128)(2,1)S(1)} %add_convert_fusion.2.p0), channel_id=1, source_target_pairs={{0,96},{32,0},{64,32},{96,64},{1,97},{33,1},{65,33},{97,65},{2,98}... | collective-permute-start | bytes 344072 | tf_op jit(solution)/shard_map/ppermute | solution.py:340
  37.8 5.8 %collective-permute-start.2 = (bf16[32,1792]{1,0:T(8,128)(2,1)S(1)}, bf16[32,1792]{1,0:T(8,128)(2,1)S(1)}, u32[]{:S(2)}, u32[]{:S(2)}) collective-permute-start(bf16[32,1792]{1,0:T(8,128)(2,1)S(1)} %add_convert_fusion.2.p0), channel_id=1, source_target_pairs={{0,64},{32,96},{64,0},{96,32},{1,65},{33,97},{65,1},{97,33},{2,66}... | collective-permute-start | bytes 344072 | tf_op jit(solution)/shard_map/ppermute | solution.py:340
  38.3 8.3 %collective-permute-start.1 = (bf16[32,1792]{1,0:T(8,128)(2,1)S(1)}, bf16[32,1792]{1,0:T(8,128)(2,1)S(1)}, u32[]{:S(2)}, u32[]{:S(2)}) collective-permute-start(bf16[32,1792]{1,0:T(8,128)(2,1)S(1)} %add_convert_fusion.2.p0), channel_id=1, source_target_pairs={{0,32},{32,64},{64,96},{96,0},{1,33},{33,65},{65,97},{97,1},{2,34}... | collective-permute-start | bytes 344072 | tf_op jit(solution)/shard_map/ppermute | solution.py:340
  47.4 11.0 %all-to-all-start.2 = ((bf16[4,32,1664]{2,1,0:T(8,128)(2,1)}), bf16[4,32,1664]{2,1,0:T(8,128)(2,1)S(1)}, u32[]{:S(2)}, u32[]{:S(2)}) async-start(bf16[4,32,1664]{2,1,0:T(8,128)(2,1)} %broadcast_in_dim.5), calls=%async_computation.2 | async-start | bytes 851968 | tf_op jit(solution)/shard_map/all_to_all | solution.py:335
  54.4 10.9 %collective-permute-start.5 = (bf16[32,1664]{1,0:T(8,128)(2,1)S(1)}, bf16[32,1664]{1,0:T(8,128)(2,1)S(1)}, u32[]{:S(2)}, u32[]{:S(2)}) collective-permute-start(bf16[32,1664]{1,0:T(8,128)(2,1)S(1)} %get-tuple-element.56), channel_id=1, source_target_pairs={{0,128},{128,0},{1,129},{129,1},{2,130},{130,2},{3,131},{131,3},{4... | collective-permute-start | bytes 319496 | tf_op jit(solution)/shard_map/ppermute | solution.py:331
  61.8 14.1 %copy-start.1 = (f32[40,1024]{1,0:T(8,128)S(1)}, f32[40,1024]{1,0:T(8,128)}, u32[]{:S(2)}) copy-start(f32[40,1024]{1,0:T(8,128)} %get-tuple-element.50.w_ref) | copy-start | bytes 491524
  61.8 7.8 %collective-permute-start.6 = (bf16[32,1792]{1,0:T(8,128)(2,1)S(1)}, bf16[32,1792]{1,0:T(8,128)(2,1)S(1)}, u32[]{:S(2)}, u32[]{:S(2)}) collective-permute-start(bf16[32,1792]{1,0:T(8,128)(2,1)S(1)} %get-tuple-element.60), channel_id=1, source_target_pairs={{0,128},{128,0},{1,129},{129,1},{2,130},{130,2},{3,131},{131,3},{4... | collective-permute-start | bytes 344072 | tf_op jit(solution)/shard_map/ppermute | solution.py:331
  66.1 9.8 %all-to-all-start.1 = ((bf16[4,32,1664]{2,1,0:T(8,128)(2,1)}), bf16[4,32,1664]{2,1,0:T(8,128)(2,1)S(1)}, u32[]{:S(2)}, u32[]{:S(2)}) async-start(bf16[4,32,1664]{2,1,0:T(8,128)(2,1)} %broadcast_in_dim.4), calls=%async_computation.1 | async-start | bytes 851968 | tf_op jit(solution)/shard_map/all_to_all | solution.py:335
  75.9 10.9 %copy-start.2 = (bf16[32,1664]{1,0:T(8,128)(2,1)S(1)}, bf16[32,1664]{1,0:T(8,128)(2,1)}, u32[]{:S(2)}) copy-start(bf16[32,1664]{1,0:T(8,128)(2,1)} %slot_ref.3) | copy-start | bytes 319492
  79.7 22.5 %all-to-all-start.3 = ((f32[32,8,128]{2,1,0:T(8,128)}), f32[32,8,128]{2,1,0:T(8,128)S(1)}, u32[]{:S(2)}, u32[]{:S(2)}) async-start(f32[32,8,128]{2,1,0:T(8,128)} %get-tuple-element.70), calls=%async_computation.3 | async-start | bytes 262144 | tf_op jit(solution)/shard_map/all_to_all | solution.py:335
  86.8 6.5 %collective-permute-start.12 = (bf16[32,1664]{1,0:T(8,128)(2,1)S(1)}, bf16[32,1664]{1,0:T(8,128)(2,1)S(1)}, u32[]{:S(2)}, u32[]{:S(2)}) collective-permute-start(bf16[32,1664]{1,0:T(8,128)(2,1)S(1)} %copy-done.2), channel_id=1, source_target_pairs={{0,24},{8,0},{16,8},{24,16},{1,25},{9,1},{17,9},{25,17},{2,26},{10... | collective-permute-start | bytes 319496 | tf_op jit(solution)/shard_map/ppermute | solution.py:340
  90.2 12.0 %collective-permute-start.9 = (bf16[32,1792]{1,0:T(8,128)(2,1)S(1)}, bf16[32,1792]{1,0:T(8,128)(2,1)S(1)}, u32[]{:S(2)}, u32[]{:S(2)}) collective-permute-start(bf16[32,1792]{1,0:T(8,128)(2,1)S(1)} %add_convert_fusion.1.p0), channel_id=1, source_target_pairs={{0,96},{32,0},{64,32},{96,64},{1,97},{33,1},{65,33},{97,65},{2,98}... | collective-permute-start | bytes 344072 | tf_op jit(solution)/shard_map/ppermute | solution.py:340
  91.1 11.1 %collective-permute-start.8 = (bf16[32,1792]{1,0:T(8,128)(2,1)S(1)}, bf16[32,1792]{1,0:T(8,128)(2,1)S(1)}, u32[]{:S(2)}, u32[]{:S(2)}) collective-permute-start(bf16[32,1792]{1,0:T(8,128)(2,1)S(1)} %add_convert_fusion.1.p0), channel_id=1, source_target_pairs={{0,64},{32,96},{64,0},{96,32},{1,65},{33,97},{65,1},{97,33},{2,66}... | collective-permute-start | bytes 344072 | tf_op jit(solution)/shard_map/ppermute | solution.py:340
  92.3 9.9 %collective-permute-start.7 = (bf16[32,1792]{1,0:T(8,128)(2,1)S(1)}, bf16[32,1792]{1,0:T(8,128)(2,1)S(1)}, u32[]{:S(2)}, u32[]{:S(2)}) collective-permute-start(bf16[32,1792]{1,0:T(8,128)(2,1)S(1)} %add_convert_fusion.1.p0), channel_id=1, source_target_pairs={{0,32},{32,64},{64,96},{96,0},{1,33},{33,65},{65,97},{97,1},{2,34}... | collective-permute-start | bytes 344072 | tf_op jit(solution)/shard_map/ppermute | solution.py:340
  92.3 9.9 %collective-permute-start.11 = (bf16[32,1664]{1,0:T(8,128)(2,1)S(1)}, bf16[32,1664]{1,0:T(8,128)(2,1)S(1)}, u32[]{:S(2)}, u32[]{:S(2)}) collective-permute-start(bf16[32,1664]{1,0:T(8,128)(2,1)S(1)} %copy-done.2), channel_id=1, source_target_pairs={{0,16},{8,24},{16,0},{24,8},{1,17},{9,25},{17,1},{25,9},{2,18},{10... | collective-permute-start | bytes 319496 | tf_op jit(solution)/shard_map/ppermute | solution.py:340
  93.2 8.9 %collective-permute-start.10 = (bf16[32,1664]{1,0:T(8,128)(2,1)S(1)}, bf16[32,1664]{1,0:T(8,128)(2,1)S(1)}, u32[]{:S(2)}, u32[]{:S(2)}) collective-permute-start(bf16[32,1664]{1,0:T(8,128)(2,1)S(1)} %copy-done.2), channel_id=1, source_target_pairs={{0,8},{8,16},{16,24},{24,0},{1,9},{9,17},{17,25},{25,1},{2,10},{10... | collective-permute-start | bytes 319496 | tf_op jit(solution)/shard_map/ppermute | solution.py:340
  106.1 18.2 %all-to-all-start.4 = ((bf16[4,32,2176]{2,1,0:T(8,128)(2,1)}), bf16[4,32,2176]{2,1,0:T(8,128)(2,1)S(1)}, u32[]{:S(2)}, u32[]{:S(2)}) async-start(bf16[4,32,2176]{2,1,0:T(8,128)(2,1)} %get-tuple-element.73), calls=%async_computation.4 | async-start | bytes 1114112 | tf_op jit(solution)/shard_map/all_to_all | solution.py:335
  111.8 3.9 %collective-permute-start.15 = (bf16[32,1664]{1,0:T(8,128)(2,1)S(1)}, bf16[32,1664]{1,0:T(8,128)(2,1)S(1)}, u32[]{:S(2)}, u32[]{:S(2)}) collective-permute-start(bf16[32,1664]{1,0:T(8,128)(2,1)S(1)} %get-tuple-element.74), channel_id=1, source_target_pairs={{0,96},{32,0},{64,32},{96,64},{1,97},{33,1},{65,33},{97,65},{2,98}... | collective-permute-start | bytes 319496 | tf_op jit(solution)/shard_map/ppermute | solution.py:340
  113.5 7.0 %collective-permute-start.14 = (bf16[32,1664]{1,0:T(8,128)(2,1)S(1)}, bf16[32,1664]{1,0:T(8,128)(2,1)S(1)}, u32[]{:S(2)}, u32[]{:S(2)}) collective-permute-start(bf16[32,1664]{1,0:T(8,128)(2,1)S(1)} %get-tuple-element.74), channel_id=1, source_target_pairs={{0,32},{32,64},{64,96},{96,0},{1,33},{33,65},{65,97},{97,1},{2,34}... | collective-permute-start | bytes 319496 | tf_op jit(solution)/shard_map/ppermute | solution.py:340
  113.5 7.0 %collective-permute-start.13 = (bf16[32,1664]{1,0:T(8,128)(2,1)S(1)}, bf16[32,1664]{1,0:T(8,128)(2,1)S(1)}, u32[]{:S(2)}, u32[]{:S(2)}) collective-permute-start(bf16[32,1664]{1,0:T(8,128)(2,1)S(1)} %get-tuple-element.74), channel_id=1, source_target_pairs={{0,64},{32,96},{64,0},{96,32},{1,65},{33,97},{65,1},{97,33},{2,66}... | collective-permute-start | bytes 319496 | tf_op jit(solution)/shard_map/ppermute | solution.py:340
  127.9 4.4 %collective-permute-start.16 = (bf16[4,32,1664]{2,1,0:T(8,128)(2,1)S(1)}, bf16[4,32,1664]{2,1,0:T(8,128)(2,1)S(1)}, u32[]{:S(2)}, u32[]{:S(2)}) collective-permute-start(bf16[4,32,1664]{2,1,0:T(8,128)(2,1)S(1)} %get-tuple-element.80), channel_id=1, source_target_pairs={{0,1},{1,0},{2,3},{3,2},{4,5},{5,4},{6,7},{7,6},{8,9},{9,8},{10,11... | collective-permute-start | bytes 1277960 | tf_op jit(solution)/shard_map/ppermute | solution.py:331
  133.1 16.1 %all-to-all-start.5 = ((bf16[4,32,1664]{2,1,0:T(8,128)(2,1)}), bf16[4,32,1664]{2,1,0:T(8,128)(2,1)S(1)}, u32[]{:S(2)}, u32[]{:S(2)}) async-start(bf16[4,32,1664]{2,1,0:T(8,128)(2,1)} %add_convert_fusion), calls=%async_computation.5 | async-start | bytes 851968 | tf_op jit(solution)/shard_map/all_to_all | solution.py:335
  137.3 10.9 %collective-permute-start.17 = (bf16[32,1664]{1,0:T(8,128)(2,1)S(1)}, bf16[32,1664]{1,0:T(8,128)(2,1)S(1)}, u32[]{:S(2)}, u32[]{:S(2)}) collective-permute-start(bf16[32,1664]{1,0:T(8,128)(2,1)S(1)} %add_convert_fusion.3.p0), channel_id=1, source_target_pairs={{0,128},{128,0},{1,129},{129,1},{2,130},{130,2},{3,131},{131,3},{4... | collective-permute-start | bytes 319496 | tf_op jit(solution)/shard_map/ppermute | solution.py:331
